TPU v7x, 128 devices: a whole 4x4x4 slice. The times are simulated.
128 devices in a mesh: frag: 4 (over y), orb: 32 (over z, x, core).
Axes of the slice: x: 4, y: 4, z: 4, core: 2. Of those that a mesh axis runs over, the one named last changes fastest.
Arguments:
- orbitals: float32 [8, 128, 48, 2304], P('frag', 'orb'), may hold values from -6 to 6
- potential: float32 [24, 36864], P('frag', 'orb'), may hold values from -3 to 0
- ion_potential: float32 [24, 36864], P('frag', 'orb'), may hold values from -2 to 0
- core_density: float32 [24, 36864], P('frag', 'orb'), may hold values from 0.5 to 2
- frag_blocks: int32 [8, 3], replicated, may hold values from 0 to 23, as said below
- frag_signs: int32 [8], replicated, may hold values from -1 to 1, as said below
Outputs:
- filtered: float32 [8, 128, 48, 2304], P('frag', 'orb')
- new_potential: float32 [24, 36864], P('frag', 'orb')
Inputs may be any that keep to these rules, and one draw needn't show every extreme that they name: `frag_blocks`: fragments g * 2 to (g + 1) * 2 - 1 form group g; block b belongs to owner b // 6. Among the 6 entries of one group no owner is named more than 3 times, and group g names owner (g + s) mod 4 exactly 3 times, for a shift s common to all groups. The first and the last block of every owner are named. `frag_signs`: each sign is +1 or -1.
All inputs are finite; a program needn't handle non-finite values.
Results may differ from a plain program's by a relative error of at most 0.0001.
Values sent between devices are 32-bit elements; how exact they have to be, the bound alone decides.
No kernel may reach another device: no remote copies, remote signals or barrier semaphores. Data moves between devices by JAX's collectives and lax.ppermute only.
A program may use at most 192 MiB of HBM per device.

v0:
```python
import jax
import jax.numpy as jnp
from jax import lax
from jax.sharding import PartitionSpec as P

FB = 3
ORBS = 128
ITERS = 2
CAP = 3


SPACING = 0.5
FILTER_CENTER = 18.0
FILTER_HALF = 16.0
DENSITY_FLOOR = 0.25
EXCHANGE_COEF = 0.9847450218426965
NORM_EPS = 1e-06


def laplacian(values):
    side_cells = values.shape[-2]
    plane_cells = values.shape[-1]
    leading = [(0, 0)] * (values.ndim - 2)
    padded_x = jnp.pad(values, leading + [(2, 2), (0, 0)])
    nearest = padded_x[..., 1 : side_cells + 1, :] + padded_x[..., 3 : side_cells + 3, :]
    distant = padded_x[..., 0:side_cells, :] + padded_x[..., 4 : side_cells + 4, :]
    padded_y = jnp.pad(values, leading + [(0, 0), (2 * side_cells, 2 * side_cells)])
    nearest = (
        nearest
        + padded_y[..., side_cells : side_cells + plane_cells]
        + padded_y[..., 3 * side_cells : 3 * side_cells + plane_cells]
    )
    distant = (
        distant
        + padded_y[..., 0:plane_cells]
        + padded_y[..., 4 * side_cells : 4 * side_cells + plane_cells]
    )
    padded_z = jnp.pad(values, leading + [(0, 0), (2, 2)])
    column = jnp.arange(plane_cells, dtype=jnp.int32) % side_cells
    nearest = nearest + jnp.where(column >= 1, padded_z[..., 1 : 1 + plane_cells], 0.0)
    nearest = nearest + jnp.where(column <= side_cells - 2, padded_z[..., 3 : 3 + plane_cells], 0.0)
    distant = distant + jnp.where(column >= 2, padded_z[..., 0:plane_cells], 0.0)
    distant = distant + jnp.where(column <= side_cells - 3, padded_z[..., 4 : 4 + plane_cells], 0.0)
    return (16.0 * nearest - distant - 90.0 * values) / 12.0


def hamiltonian(values, local_pot):
    return -0.5 / (SPACING * SPACING) * laplacian(values) + local_pot * values


def chebyshev(values, local_pot):
    previous = values
    current = (hamiltonian(values, local_pot) - FILTER_CENTER * values) / FILTER_HALF
    for degree in range(3):
        further = (
            2.0 * (hamiltonian(current, local_pot) - FILTER_CENTER * current) / FILTER_HALF
            - previous
        )
        previous, current = (current, further)
    magnitude = jnp.sqrt(jnp.mean(current * current, axis=(-2, -1), keepdims=True) + NORM_EPS)
    return current / magnitude


def owner_tables(frag_blocks, block_count, groups):
    entries = frag_blocks.reshape(groups, -1)
    owners = entries // block_count
    count = entries.shape[1]
    positions = jnp.arange(count, dtype=jnp.int32)
    earlier = positions[:, None] > positions[None, :]
    same_owner = owners[:, :, None] == owners[:, None, :]
    ranks = jnp.sum(jnp.where(same_owner & earlier[None, :, :], 1, 0), axis=2).astype(jnp.int32)
    return (entries, owners, ranks)


def reduce_density(partial_value):
    return lax.psum_scatter(partial_value, "orb", scatter_dimension=2, tiled=True)


def filter_group(orbital_group, sectioned, side_cells, plane_cells):
    count = orbital_group.shape[0]
    result = chebyshev(orbital_group, sectioned.reshape(count, 1, side_cells, plane_cells))
    partial_value = jnp.sum(result * result, axis=1).reshape(count, FB, -1)
    return (result, reduce_density(partial_value))


def shards(orbitals, potential, ion_potential, core_density, frag_blocks, frag_signs):
    groups = lax.axis_size("frag")
    me_index = lax.axis_index("frag")
    side_cells = orbitals.shape[2]
    plane_cells = orbitals.shape[3]
    frag_count = orbitals.shape[0]
    block_count = potential.shape[0]
    piece_cells = potential.shape[1]
    capacity = CAP
    entries, owners, ranks = owner_tables(frag_blocks, block_count, groups)
    count = entries.shape[1]
    slot_range = jnp.arange(capacity, dtype=jnp.int32)
    send_match = (owners[:, None, :] == me_index) & (ranks[:, None, :] == slot_range[None, :, None])
    send_valid = jnp.any(send_match, axis=2).reshape(-1)
    send_block = jnp.sum(
        jnp.where(send_match, entries[:, None, :] - me_index * block_count, 0), axis=2
    ).reshape(-1)
    send_mask = send_valid.astype(jnp.float32)[:, None]
    my_owners = lax.dynamic_index_in_dim(owners, me_index, 0, keepdims=False)
    my_ranks = lax.dynamic_index_in_dim(ranks, me_index, 0, keepdims=False)
    my_slot = my_owners * capacity + my_ranks
    owner_range = jnp.arange(groups, dtype=jnp.int32)
    back_match = (my_owners[None, None, :] == owner_range[:, None, None]) & (
        my_ranks[None, None, :] == slot_range[None, :, None]
    )
    back_mask = jnp.any(back_match, axis=2).reshape(-1).astype(jnp.float32)[:, None]
    entry_range = jnp.arange(count, dtype=jnp.int32)
    back_entry = jnp.sum(jnp.where(back_match, entry_range[None, None, :], 0), axis=2).reshape(-1)
    my_signs = jnp.repeat(
        lax.dynamic_slice_in_dim(frag_signs, me_index * frag_count, frag_count), FB
    ).astype(jnp.float32)
    block_range = jnp.arange(block_count, dtype=jnp.int32)
    selector = ((send_block[None, :] == block_range[:, None]) & send_valid[None, :]).astype(
        jnp.float32
    )
    current_pot = potential
    orbital_set = orbitals
    for iteration in range(ITERS):
        owned = lax.all_gather(current_pot, "orb", axis=1, tiled=True)
        block_cells = owned.shape[1]
        outgoing = (jnp.take(owned, send_block, axis=0) * send_mask).reshape(
            groups, capacity, block_cells
        )
        incoming = lax.all_to_all(outgoing, "frag", split_axis=0, concat_axis=0, tiled=True)
        sectioned = jnp.take(
            incoming.reshape(groups * capacity, block_cells), my_slot, axis=0
        ).reshape(frag_count, FB, block_cells)
        orbital_set, summed = filter_group(orbital_set, sectioned, side_cells, plane_cells)
        signed = (summed / ORBS).reshape(count, piece_cells) * my_signs[:, None]
        returning = (jnp.take(signed, back_entry, axis=0) * back_mask).reshape(
            groups, capacity, piece_cells
        )
        arrived = lax.all_to_all(returning, "frag", split_axis=0, concat_axis=0, tiled=True)
        collected = jnp.dot(
            selector,
            arrived.reshape(groups * capacity, piece_cells),
            precision=lax.Precision.HIGHEST,
            preferred_element_type=jnp.float32,
        )
        total = core_density + collected
        current_pot = ion_potential - EXCHANGE_COEF * jnp.cbrt(jnp.maximum(total, DENSITY_FLOOR))
    return (orbital_set, current_pot)


def solution(mesh):
    in_specs = (
        P("frag", "orb", None, None),
        P("frag", "orb"),
        P("frag", "orb"),
        P("frag", "orb"),
        P(),
        P(),
    )
    out_specs = (P("frag", "orb", None, None), P("frag", "orb"))
    return jax.shard_map(shards, mesh=mesh, in_specs=in_specs, out_specs=out_specs, check_vma=False)
```

profile of v0, /device:TPU:0, one launch (start us, length us, event | category | flops | bytes accessed | tf_op | source)
XLA Modules:
  0.0 746.9 jit_solution(4298365373455943929)
XLA Ops:
  10.5 26.5 %all_gather.6 = f32[6,36864]{1,0:T(8,128)S(1)} all-gather(f32[6,1152]{1,0:T(8,128)} %param.13), channel_id=1, replica_groups=mesh['frag'=4,'orb'=32] {'orb'}, dimensions={1}, use_global_device_ids=true | all-gather | bytes 912384 | tf_op jit(solution)/shard_map/all_gather | solution.py:124
  41.7 3.9 reshape.233
  45.6 4.5 all-to-all-start
  51.5 28.6 %all-to-all-done = f32[4,3,36864]{2,1,0:T(4,128)} async-done(((f32[4,3,36864]{2,1,0:T(4,128)}), f32[4,3,36864]{2,1,0:T(4,128)}, u32[]{:S(2)}, u32[]{:S(2)}) %all-to-all-start) | async-done | bytes 1769504 | tf_op jit(solution)/shard_map/all_to_all | solution.py:129
  85.9 27.0 %broadcast_multiply_fusion.1 = (f32[2,4,48,2304]{3,2,1,0:T(8,128)}, f32[2,4,48,2304]{3,2,1,0:T(8,128)}) fusion(f32[2,4,48,2304]{3,2,1,0:T(8,128)} %param.12, f32[2,48,2304]{2,1,0:T(8,128)S(1)} %mul.251, pred[2304]{0:T(1024)(128)(4,1)S(1)} %get-tuple-element.24, pred[2304]{0:T(1024)(128)(4,1)S(1)} %get-tuple-element.25, ...), kind=kLoop, calls=%fused_computation.257 | loop fusion | flops 21233664 | bytes 11510784 | tf_op jit(solution)/shard_map/div | solution.py:53
  113.0 26.2 %fusion.25 = f32[2,4,48,2304]{3,2,1,0:T(8,128)S(1)} fusion(f32[2,4,48,2304]{3,2,1,0:T(8,128)} %param.12, f32[2,4,48,2304]{3,2,1,0:T(8,128)} %get-tuple-element.15, f32[2,4,48,2304]{3,2,1,0:T(8,128)} %get-tuple-element.16, f32[2,48,2304]{2,1,0:T(8,128)} %broadcast_multiply_fusion.3, pred[2304]{0:T(1024)(128)(4,1)S(1)} %get-tuple-element.24, ...), kind=kLoop, calls=%fused_computation.95 | loop fusion | flops 22118400 | bytes 15049728 | tf_op jit(solution)/shard_map/sub | solution.py:56
  139.1 10.3 %fusion.41 = f32[2,4,48,2304]{3,2,1,0:T(8,128)} fusion(f32[2,4,48,2304]{3,2,1,0:T(8,128)S(1)} %fusion.25, f32[2,4,48,2304]{3,2,1,0:T(8,128)} %get-tuple-element.16, f32[2,48,2304]{2,1,0:T(8,128)} %copy-done.1, pred[2304]{0:T(1024)(128)(4,1)S(1)} %get-tuple-element.24, pred[2304]{0:T(1024)(128)(4,1)S(1)} %get-tuple-element.25, ...), kind=kLoop, calls=%fused_computation.111 | loop fusion | flops 23003136 | bytes 11510784 | tf_op jit(solution)/shard_map/sub | solution.py:56
  149.4 27.6 %multiply_reduce_fusion.3 = (f32[2,4]{1,0:T(2,128)}, f32[2,4,48,2304]{3,2,1,0:T(8,128)}) fusion(f32[2,4,48,2304]{3,2,1,0:T(8,128)S(1)} %fusion.25, f32[2,4,48,2304]{3,2,1,0:T(8,128)} %fusion.41, f32[2,48,2304]{2,1,0:T(8,128)} %copy-done.1, pred[2304]{0:T(1024)(128)(4,1)S(1)} %get-tuple-element.24, pred[2304]{0:T(1024)(128)(4,1)S(1)} %get-tuple-element.25, ...), kind=kLoop, calls=%fused_computation.227 | loop fusion | flops 23887864 | bytes 11510816 | tf_op jit(solution)/shard_map/reduce_sum | solution.py:60
  177.7 4.3 multiply_reduce_fusion.2
  182.5 32.8 %copy.35 = f32[2,3,36864]{1,0,2:T(2,128)} copy(f32[2,3,36864]{2,1,0:T(4,128)S(1)} %reshape.235) | data formatting | bytes 1769472
  215.3 35.1 %reshape.313 = f32[36864,6]{1,0:T(8,128)} reshape(f32[36864,2,3]{2,1,0:T(2,128)} %bitcast.9) | data formatting | bytes 1769472
  252.1 117.8 %reduce-scatter.7.cloned.1.call-done = f32[1152,6]{1,0:T(8,128)} async-done(((f32[36864,6]{1,0:T(8,128)}), f32[1152,6]{1,0:T(8,128)}) %reduce-scatter.7.cloned.1.call-update) | async-done | bytes 27664
  373.4 9.7 %all_to_all.20 = f32[4,3,1152]{2,1,0:T(4,128)S(1)} all-to-all(f32[4,3,1152]{2,1,0:T(4,128)S(1)} %reshape.238), channel_id=1, replica_groups=mesh['frag'=4,'orb'=32] {'frag'}, dimensions={0} | all-to-all | bytes 110592 | tf_op jit(solution)/shard_map/all_to_all | solution.py:138
  383.4 24.4 %all_gather.7 = f32[6,36864]{1,0:T(8,128)S(1)} all-gather(f32[6,1152]{1,0:T(8,128)S(1)} %fusion.158), channel_id=1, replica_groups=mesh['frag'=4,'orb'=32] {'orb'}, dimensions={1}, use_global_device_ids=true | all-gather | bytes 912384 | tf_op jit(solution)/shard_map/all_gather | solution.py:124
  413.8 33.6 %all_to_all.21 = f32[4,3,36864]{2,1,0:T(4,128)} all-to-all(f32[4,3,36864]{2,1,0:T(4,128)S(1)} %reshape.240), channel_id=1, replica_groups=mesh['frag'=4,'orb'=32] {'frag'}, dimensions={0} | all-to-all | bytes 3538944 | tf_op jit(solution)/shard_map/all_to_all | solution.py:129
  459.4 10.2 %broadcast_multiply_fusion = (f32[2,4,48,2304]{3,2,1,0:T(8,128)}, f32[2,4,48,2304]{3,2,1,0:T(8,128)}) fusion(f32[2,4,48,2304]{3,2,1,0:T(8,128)S(1)} %copy-done, f32[2,48,2304]{2,1,0:T(8,128)} %mul.287, pred[2304]{0:T(1024)(128)(4,1)S(1)} %get-tuple-element.24, pred[2304]{0:T(1024)(128)(4,1)S(1)} %get-tuple-element.25, ...), kind=kLoop, calls=%fused_computation.256 | loop fusion | flops 21233664 | bytes 11510784 | tf_op jit(solution)/shard_map/div | solution.py:53
  469.6 25.9 %fusion.87 = f32[2,4,48,2304]{3,2,1,0:T(8,128)S(1)} fusion(f32[2,4,48,2304]{3,2,1,0:T(8,128)} %get-tuple-element.12, f32[2,4,48,2304]{3,2,1,0:T(8,128)} %get-tuple-element.9, f32[2,4,48,2304]{3,2,1,0:T(8,128)} %get-tuple-element.10, f32[2,48,2304]{2,1,0:T(8,128)} %broadcast_multiply_fusion.2, pred[2304]{0:T(1024)(128)(4,1)S(1)} %get-tuple-element.24, ...), kind=kLoop, calls=%fused_computation.157 | loop fusion | flops 22118400 | bytes 15049728 | tf_op jit(solution)/shard_map/sub | solution.py:56
  495.5 10.3 %fusion.103 = f32[2,4,48,2304]{3,2,1,0:T(8,128)} fusion(f32[2,4,48,2304]{3,2,1,0:T(8,128)S(1)} %fusion.87, f32[2,48,2304]{2,1,0:T(8,128)} %mul.287, f32[2,4,48,2304]{3,2,1,0:T(8,128)} %get-tuple-element.10, pred[2304]{0:T(1024)(128)(4,1)S(1)} %get-tuple-element.24, pred[2304]{0:T(1024)(128)(4,1)S(1)} %get-tuple-element.25, ...), kind=kLoop, calls=%fused_computation.173 | loop fusion | flops 23003136 | bytes 11510784 | tf_op jit(solution)/shard_map/sub | solution.py:56
  505.9 27.5 %multiply_reduce_fusion.1 = (f32[2,4]{1,0:T(2,128)}, f32[2,4,48,2304]{3,2,1,0:T(8,128)}) fusion(f32[2,4,48,2304]{3,2,1,0:T(8,128)S(1)} %fusion.87, f32[2,4,48,2304]{3,2,1,0:T(8,128)} %fusion.103, f32[2,48,2304]{2,1,0:T(8,128)} %mul.287, pred[2304]{0:T(1024)(128)(4,1)S(1)} %get-tuple-element.24, pred[2304]{0:T(1024)(128)(4,1)S(1)} %get-tuple-element.25, ...), kind=kLoop, calls=%fused_computation.211 | loop fusion | flops 23887864 | bytes 11510816 | tf_op jit(solution)/shard_map/reduce_sum | solution.py:60
  534.0 4.3 multiply_reduce_fusion
  538.9 32.8 %copy.37 = f32[2,3,36864]{1,0,2:T(2,128)} copy(f32[2,3,36864]{2,1,0:T(4,128)S(1)} %reshape.242) | data formatting | bytes 1769472
  571.7 35.1 %reshape.315 = f32[36864,6]{1,0:T(8,128)} reshape(f32[36864,2,3]{2,1,0:T(2,128)} %bitcast.10) | data formatting | bytes 1769472
  606.9 118.7 %reduce-scatter.9.cloned.1.call-done = f32[1152,6]{1,0:T(8,128)} async-done(((f32[36864,6]{1,0:T(8,128)}), f32[1152,6]{1,0:T(8,128)}) %reduce-scatter.9.cloned.1.call-update) | async-done | bytes 27664
  729.3 9.7 %all_to_all.22 = f32[4,3,1152]{2,1,0:T(4,128)S(1)} all-to-all(f32[4,3,1152]{2,1,0:T(4,128)S(1)} %reshape.244), channel_id=1, replica_groups=mesh['frag'=4,'orb'=32] {'frag'}, dimensions={0} | all-to-all | bytes 110592 | tf_op jit(solution)/shard_map/all_to_all | solution.py:138
  (136 shorter events, 45.3 us)
Async XLA Ops:
  10.5 28.9 %copy-start.16 = (pred[12]{0:T(512)(128)(4,1)}, pred[12]{0:T(512)(128)(4,1)S(1)}, u32[]{:S(2)}) copy-start(pred[12]{0:T(512)(128)(4,1)S(1)} %compare_and_fusion.2) | copy-start | bytes 40
  37.1 2.4 copy-start.6
  45.6 34.5 %all-to-all-start = ((f32[4,3,36864]{2,1,0:T(4,128)}), f32[4,3,36864]{2,1,0:T(4,128)}, u32[]{:S(2)}, u32[]{:S(2)}) async-start(f32[4,3,36864]{2,1,0:T(4,128)} %reshape.233), calls=%async_computation | async-start | bytes 4718592 | tf_op jit(solution)/shard_map/all_to_all | solution.py:129
  50.1 319.8 %reduce-scatter.7.cloned.1.call-start = ((), (), s32[]{:S(2)}) async-start(), calls=%async_computation.6 | async-start | bytes 19464192
  50.3 1.2 copy-start.21
  84.9 28.1 %copy-start.1 = (f32[2,48,2304]{2,1,0:T(8,128)}, f32[2,48,2304]{2,1,0:T(8,128)S(1)}, u32[]{:S(2)}) copy-start(f32[2,48,2304]{2,1,0:T(8,128)S(1)} %mul.251) | copy-start | bytes 2654212
  250.5 0.9 copy-start.23
  250.5 132.6 %copy-start.2 = (f32[6,1152]{1,0:T(8,128)S(1)}, f32[6,1152]{1,0:T(8,128)}, u32[]{:S(2)}) copy-start(f32[6,1152]{1,0:T(8,128)} %param.14) | copy-start | bytes 82948
  250.5 132.6 %copy-start.4 = (f32[6,1152]{1,0:T(8,128)S(1)}, f32[6,1152]{1,0:T(8,128)}, u32[]{:S(2)}) copy-start(f32[6,1152]{1,0:T(8,128)} %param.15) | copy-start | bytes 82948
  250.5 132.6 %copy-start.9 = (s32[12]{0:T(128)S(1)}, s32[12]{0:T(128)}, u32[]{:S(2)}) copy-start(s32[12]{0:T(128)} %copy-done.8) | copy-start | bytes 148
  250.5 132.6 %copy-start.14 = (pred[12]{0:T(512)(128)(4,1)S(1)}, pred[12]{0:T(512)(128)(4,1)}, u32[]{:S(2)}) copy-start(pred[12]{0:T(512)(128)(4,1)} %copy-done.13) | copy-start | bytes 40
  250.5 475.1 %reduce-scatter.9.cloned.1.call-start = ((), (), s32[]{:S(2)}) async-start(), calls=%async_computation.7 | async-start | bytes 19464192
  251.3 132.0 %copy-start.17 = (f32[6]{0:T(128)}, f32[6]{0:T(128)S(1)}, u32[]{:S(2)}) copy-start(f32[6]{0:T(128)S(1)} %convert_element_type.58) | copy-start | bytes 76
  252.1 131.3 %copy-start.11 = (f32[12]{0:T(128)}, f32[12]{0:T(128)S(1)}, u32[]{:S(2)}) copy-start(f32[12]{0:T(128)S(1)} %reshape.246) | copy-start | bytes 148
  252.1 131.3 %copy-start.7 = (s32[1024]{0:T(1024)}, s32[1024]{0:T(1024)S(1)}, u32[]{:S(2)}) copy-start(s32[1024]{0:T(1024)S(1)} %pad_clamp_fusion) | copy-start | bytes 12292
  252.1 131.3 %copy-start.19 = (pred[12]{0:T(512)(128)(4,1)}, pred[12]{0:T(512)(128)(4,1)S(1)}, u32[]{:S(2)}) copy-start(pred[12]{0:T(512)(128)(4,1)S(1)} %compare_and_fusion) | copy-start | bytes 40
  451.9 7.5 %copy-start = (f32[2,4,48,2304]{3,2,1,0:T(8,128)S(1)}, f32[2,4,48,2304]{3,2,1,0:T(8,128)}, u32[]{:S(2)}) copy-start(f32[2,4,48,2304]{3,2,1,0:T(8,128)} %get-tuple-element.12) | copy-start | bytes 10616836
  606.8 121.6 %copy-start.18 = (f32[6]{0:T(128)S(1)}, f32[6]{0:T(128)}, u32[]{:S(2)}) copy-start(f32[6]{0:T(128)} %copy-done.17) | copy-start | bytes 76
  606.9 122.4 %copy-start.12 = (f32[12]{0:T(128)S(1)}, f32[12]{0:T(128)}, u32[]{:S(2)}) copy-start(f32[12]{0:T(128)} %copy-done.11) | copy-start | bytes 148
  606.9 122.4 %copy-start.20 = (pred[12]{0:T(512)(128)(4,1)S(1)}, pred[12]{0:T(512)(128)(4,1)}, u32[]{:S(2)}) copy-start(pred[12]{0:T(512)(128)(4,1)} %copy-done.19) | copy-start | bytes 40
  606.9 132.2 %copy-start.3 = (f32[6,1152]{1,0:T(8,128)S(1)}, f32[6,1152]{1,0:T(8,128)}, u32[]{:S(2)}) copy-start(f32[6,1152]{1,0:T(8,128)} %param.14) | copy-start | bytes 82948
  606.9 132.2 %copy-start.5 = (f32[6,1152]{1,0:T(8,128)S(1)}, f32[6,1152]{1,0:T(8,128)}, u32[]{:S(2)}) copy-start(f32[6,1152]{1,0:T(8,128)} %param.15) | copy-start | bytes 82948
  606.9 132.2 %copy-start.10 = (s32[12]{0:T(128)S(1)}, s32[12]{0:T(128)}, u32[]{:S(2)}) copy-start(s32[12]{0:T(128)} %copy-done.8) | copy-start | bytes 148
  606.9 132.2 %copy-start.15 = (pred[12]{0:T(512)(128)(4,1)S(1)}, pred[12]{0:T(512)(128)(4,1)}, u32[]{:S(2)}) copy-start(pred[12]{0:T(512)(128)(4,1)} %copy-done.13) | copy-start | bytes 40
  (4 other events, 2.5 us)
Sparse Core Ops, SparseCore 0:
  250.6 119.2 reduce-scatter.6
  607.0 118.5 reduce-scatter.8
where the time goes:
time: 754 us; the launch traced here: 747 us
  waiting for transfers between devices  265 us (35%)
  other arithmetic  191 us (25%)
  local copies, waits for them, and re-layouts  167 us (22%)
  blocking collectives  104 us (14%)
  between operations  14.8 us (2%)
    unnamed x4, waiting for transfers between devices  236 us
    unnamed x58, local copies, waits for them, and re-layouts  143 us
    sub x4, other arithmetic, chebyshev(): 2.0 * (hamiltonian(current, local_pot) - FILTER_CENTER * current)  72.7 us
    reduce_sum x2, other arithmetic, chebyshev(): jnp.mean(current * current, axis=(-2, -1), keepdims=True) + NORM_EPS  55.1 us
    all_gather x2, blocking collectives, shards(): owned = lax.all_gather(current_pot, 'orb', axis=1, tiled=True)  51 us
    div x2, other arithmetic, chebyshev(): (hamiltonian(values, local_pot) - FILTER_CENTER * values) / FILTER_HALF  37.2 us
    all_to_all x1, blocking collectives, shards(): lax.all_to_all(outgoing, 'frag', split_axis=0, concat_axis=0, tiled=True)  33.6 us
    all_to_all x1, waiting for transfers between devices, shards(): lax.all_to_all(outgoing, 'frag', split_axis=0, concat_axis=0, tiled=True)  28.6 us
  transfers between devices with their start and end apart: 3, of which 3 were waited for; matrix products, arithmetic and copies ran while one was open for 0% of the time, Pallas kernels for 0%

commit v1 on v0

v1 whole, which is shorter than its diff:
```python
import functools

import jax
import jax.numpy as jnp
import numpy as np
from jax import lax
from jax.experimental import pallas as pl
from jax.experimental.pallas import tpu as pltpu
from jax.sharding import PartitionSpec as P

G = 48
PLANE = G * G
FB = 3
ORBS = 128
N_FRAG = 4
SLOTS = 16
CHUNK = 16
LOADS = 6
XLOAD = G // LOADS
BIG = 40 << 20
ENT = 6
CELLS = 1152
ROWS = CELLS // 128
PIECE = ENT * ROWS
LOCAL = 8
COLS = 256
WIN = 512
STEPS = PLANE // COLS
PADDED = PLANE + 256
DENSITY_FLOOR = 0.25
EXCHANGE_COEF = 0.9847450218426965
NORM_EPS = 1e-6
F32 = jnp.float32
BF16 = jnp.bfloat16


def stencil_matrices():
    mats = np.zeros((3, WIN, COLS), np.float32)
    for phase in range(3):
        out = 768 + COLS * phase + np.arange(COLS)[None, :]
        src = 768 + COLS * phase - 128 + np.arange(WIN)[:, None]
        diff = np.abs(src - out)
        same = (src // G) == (out // G)
        mats[phase] = (
            np.where(diff == G, -16.0, 0.0)
            + np.where(diff == 2 * G, 1.0, 0.0)
            + np.where((diff == 1) & same, -16.0, 0.0)
            + np.where((diff == 2) & same, 1.0, 0.0)
        )
    return mats


def split(values):
    high = values.astype(BF16)
    low = (values - high.astype(F32)).astype(BF16)
    return high, low


def cols(start, size=128):
    return pl.ds(pl.multiple_of(start, 128), size)


def zero_planes(buf):
    buf[pl.ds(0, 2)] = jnp.zeros((2, LOCAL, PLANE), F32)
    buf[pl.ds(G + 2, 2)] = jnp.zeros((2, LOCAL, PLANE), F32)


def zero_margins(halves):
    for part in range(2):
        halves[:, pl.ds(part * PADDED, 128)] = jnp.zeros((G * LOCAL, 128), BF16)
        halves[:, pl.ds(part * PADDED + PLANE + 128, 128)] = jnp.zeros((G * LOCAL, 128), BF16)


def put_halves(halves, c, values):
    high, low = split(values.reshape(16, PLANE))
    rows = pl.ds(pl.multiple_of(16 * c, 16), 16)
    halves[rows, pl.ds(128, PLANE)] = high
    halves[rows, pl.ds(PADDED + 128, PLANE)] = low


def apply(kind, cur, prev, dst, wf, mats_ref, halves, halves_next, acc_even, acc_odd, sums):
    def product(n, c, acc):
        rows = pl.ds(CHUNK * LOCAL * c, CHUNK * LOCAL)
        mat = mats_ref[lax.rem(n, 3)]
        acc[rows, :] = jnp.dot(halves[rows, cols(COLS * n, WIN)], mat, preferred_element_type=F32) + jnp.dot(
            halves[rows, cols(PADDED + COLS * n, WIN)], mat, preferred_element_type=F32
        )

    def emit(n, c, acc):
        for t in range(COLS // 128):
            lane = cols(COLS * n + 128 * t)
            for d in range(CHUNK * c // 8, CHUNK * (c + 1) // 8):
                near = cur[pl.ds(8 * d, 12), :, lane]
                s1 = near[1:9] + near[3:11]
                s2 = near[0:8] + near[4:12]
                rows = pl.ds(64 * d, 64)
                plane = acc[rows, pl.ds(128 * t, 128)].reshape(8, LOCAL, 128)
                new = plane + s2 - 16.0 * s1
                here = pl.ds(8 * d + (0 if kind == "plain" else 2), 8)
                if kind == "plain":
                    dst[here, :, lane] = (0.5 / 48.0) * new
                    continue
                new = (1.0 / 48.0) * new + wf[pl.ds(8 * d, 8), :, lane] * near[2:10]
                new = new - prev[pl.ds(8 * d + 2, 8), :, lane]
                dst[here, :, lane] = new
                if kind == "last":
                    sums[...] += jnp.sum(new * new, axis=0)
                else:
                    high, low = split(new.reshape(64, 128))
                    halves_next[rows, cols(COLS * n + 128 * t + 128)] = high
                    halves_next[rows, cols(PADDED + COLS * n + 128 * t + 128)] = low

    parts = G // CHUNK
    for c in range(parts):
        product(0, c, acc_even)

    def body(i, carry):
        for c in range(parts):
            product(2 * i + 1, c, acc_odd)
            emit(2 * i, c, acc_even)
        for c in range(parts):
            product(2 * i + 2, c, acc_even)
            emit(2 * i + 1, c, acc_odd)
        return carry

    lax.fori_loop(0, STEPS // 2, body, 0)
    for c in range(parts):
        emit(STEPS - 1, c, acc_even)


def prepare_kernel(first, source, *refs):
    if first:
        mats_ref, field_hbm, plain_hbm, field, plain, hl, acc0, acc1, sem = refs
        loads = [pltpu.make_async_copy(source.at[o], field.at[pl.ds(2, G), o, :], sem.at[o]) for o in range(LOCAL)]
    else:
        scale_ref, mats_ref, field_hbm, plain_hbm, field, plain, hl, acc0, acc1, sem = refs
        loads = [pltpu.make_async_copy(source, field.at[pl.ds(2, G)], sem.at[0])]
    for load in loads:
        load.start()
    zero_planes(field)
    zero_margins(hl)
    for load in loads:
        load.wait()
    scale = None if first else jnp.broadcast_to(scale_ref[:, 0:1], (LOCAL, PLANE))

    def body(c, scale):
        x = pl.ds(2 + 2 * c, 2)
        values = field[x]
        if not first:
            values = values * scale[None]
            field[x] = values
        put_halves(hl, c, values)
        return scale

    lax.fori_loop(0, G // 2, body, scale)
    stores = [
        pltpu.make_async_copy(field.at[pl.ds(2, G)], field_hbm, sem.at[0]),
        pltpu.make_async_copy(plain, plain_hbm, sem.at[1]),
    ]
    stores[0].start()
    apply("plain", field, None, plain, None, mats_ref, hl, None, acc0, acc1, None)
    stores[1].start()
    for store in stores:
        store.wait()


def filter_kernel(field_hbm, plain_hbm, mine_ref, other_ref, mats_ref, raw_hbm, scale_ref, dmine_ref, dother_ref,
                  ya, yb, wf, hl0, hl1, acc0, acc1, sums, sem):
    core = lax.axis_index("orb") % 2
    loads = []
    for p in range(LOADS):
        x = pl.ds(XLOAD * p, XLOAD)
        inner = pl.ds(2 + XLOAD * p, XLOAD)
        loads.append(pltpu.make_async_copy(field_hbm.at[x], ya.at[inner], sem.at[2 * p]))
        loads.append(pltpu.make_async_copy(plain_hbm.at[x], yb.at[inner], sem.at[2 * p + 1]))
    for load in loads:
        load.start()
    upper = lax.broadcasted_iota(jnp.int32, (LOCAL, 128), 0) >= LOCAL // 2

    def build(row, carry):
        for ref, half in ((mine_ref, core), (other_ref, 1 - core)):
            for b in range(FB):
                tiles = []
                for q in range(ROWS):
                    v0 = ref[row, pl.ds(b * ROWS + q, 1), :]
                    v1 = ref[row, pl.ds((FB + b) * ROWS + q, 1), :]
                    v = jnp.where(upper, jnp.broadcast_to(v1, (LOCAL, 128)), jnp.broadcast_to(v0, (LOCAL, 128)))
                    tiles.append(v * 0.125 - 0.375)
                wf[16 * b + row, :, cols(half * CELLS, CELLS)] = jnp.concatenate(tiles, axis=1)
        return carry

    lax.fori_loop(0, SLOTS, build, 0)
    zero_planes(ya)
    zero_planes(yb)
    zero_margins(hl0)
    zero_margins(hl1)
    sums[...] = jnp.zeros((LOCAL, 128), F32)

    def start(c, carry):
        x = pl.ds(2 + 2 * c, 2)
        value = yb[x] + 0.5 * (wf[pl.ds(2 * c, 2)] * ya[x])
        yb[x] = value
        put_halves(hl0, c, value)
        return carry

    for p in range(LOADS):
        loads[2 * p].wait()
        loads[2 * p + 1].wait()
        lax.fori_loop(p * XLOAD // 2, (p + 1) * XLOAD // 2, start, 0)
    apply("middle", yb, ya, ya, wf, mats_ref, hl0, hl1, acc0, acc1, sums)
    apply("middle", ya, yb, yb, wf, mats_ref, hl1, hl0, acc0, acc1, sums)
    apply("last", yb, ya, ya, wf, mats_ref, hl0, None, acc0, acc1, sums)
    store = pltpu.make_async_copy(ya.at[pl.ds(2, G)], raw_hbm, sem.at[0])
    store.start()
    mean = jnp.sum(sums[...], axis=1, keepdims=True) * (1.0 / (G * PLANE))
    inverse = 1.0 / jnp.sqrt(mean + NORM_EPS)
    scale_ref[...] = jnp.broadcast_to(inverse, (LOCAL, 128))

    def finish(row, scale):
        for ref, half in ((dmine_ref, core), (dother_ref, 1 - core)):
            for b in range(FB):
                value = ya[2 + 16 * b + row, :, cols(half * CELLS, CELLS)] * scale
                value = value * value
                value = value + pltpu.roll(value, 1, 0)
                value = value + pltpu.roll(value, 2, 0)
                for q in range(ROWS):
                    ref[row, pl.ds(b * ROWS + q, 1), :] = value[3:4, 128 * q : 128 * q + 128]
                    ref[row, pl.ds((FB + b) * ROWS + q, 1), :] = value[7:8, 128 * q : 128 * q + 128]
            ref[row, pl.ds(PIECE, 2), :] = jnp.zeros((2, 128), F32)
        return scale

    lax.fori_loop(0, SLOTS, finish, jnp.broadcast_to(inverse, (LOCAL, CELLS)))
    store.wait()


def write_kernel(raw_hbm, scale_ref, out_ref, buf, sem):
    loads = []
    for b in range(FB):
        x = pl.ds(16 * b, 16)
        loads.append(pltpu.make_async_copy(raw_hbm.at[x], buf.at[x], sem.at[FB * LOCAL + b]))
        loads[-1].start()
    stores = []
    scale = jnp.broadcast_to(scale_ref[:, 0:1], (LOCAL, PLANE))
    for b in range(FB):
        loads[b].wait()

        def body(c, scale):
            x = pl.ds(16 * b + 2 * c, 2)
            buf[x] = buf[x] * scale[None]
            return scale

        lax.fori_loop(0, 8, body, scale)
        x = pl.ds(16 * b, 16)
        for o in range(LOCAL):
            stores.append(pltpu.make_async_copy(buf.at[x, o, :], out_ref.at[o, x], sem.at[b * LOCAL + o]))
            stores[-1].start()
    for store in stores:
        store.wait()


VMEM_SPEC = pl.BlockSpec(memory_space=pltpu.VMEM)
SMEM_SPEC = pl.BlockSpec(memory_space=pltpu.SMEM)
HBM_SPEC = pl.BlockSpec(memory_space=pltpu.HBM)
PLANES = pltpu.VMEM((G + 4, LOCAL, PLANE), F32)
RAW = jax.ShapeDtypeStruct((G, LOCAL, PLANE), F32)
RAW_HBM = pltpu.HBM((G, LOCAL, PLANE), F32)
SCALE = jax.ShapeDtypeStruct((LOCAL, 128), F32)
SPREAD = jax.ShapeDtypeStruct((SLOTS, PIECE + 2, 128), F32)
HALVES = pltpu.VMEM((G * LOCAL, 2 * PADDED), BF16)
ACC = pltpu.VMEM((G * LOCAL, COLS), F32)
MATS = (3, WIN, COLS)


def in_hbm(value):
    return pltpu.with_memory_space_constraint(value, pltpu.HBM)


def prepare_call(first, source, mats):
    return pl.pallas_call(
        functools.partial(prepare_kernel, first),
        out_shape=(RAW_HBM, RAW_HBM),
        in_specs=[HBM_SPEC] + [VMEM_SPEC] * len(source),
        out_specs=(HBM_SPEC, HBM_SPEC),
        scratch_shapes=[PLANES, pltpu.VMEM(RAW.shape, F32), HALVES, ACC, ACC, pltpu.SemaphoreType.DMA((LOCAL,))],
        name="prepare_first" if first else "prepare_next",
        cost_estimate=pl.CostEstimate(flops=2 * 10**9, bytes_accessed=11 * 10**6, transcendentals=0),
        compiler_params=pltpu.CompilerParams(vmem_limit_bytes=BIG),
    )(in_hbm(source[0]), *source[1:], mats)


def filter_call(field, plain, mine, other, mats):
    return pl.pallas_call(
        filter_kernel,
        out_shape=(RAW_HBM, SCALE, SPREAD, SPREAD),
        in_specs=[HBM_SPEC] * 2 + [VMEM_SPEC] * 3,
        out_specs=(HBM_SPEC,) + (VMEM_SPEC,) * 3,
        scratch_shapes=[
            PLANES,
            PLANES,
            pltpu.VMEM(RAW.shape, F32),
            HALVES,
            HALVES,
            ACC,
            ACC,
            pltpu.VMEM((LOCAL, 128), F32),
            pltpu.SemaphoreType.DMA((2 * LOADS,)),
        ],
        name="filter",
        cost_estimate=pl.CostEstimate(flops=8 * 10**9, bytes_accessed=14 * 10**6, transcendentals=0),
        compiler_params=pltpu.CompilerParams(vmem_limit_bytes=BIG),
    )(in_hbm(field), in_hbm(plain), mine, other, mats)


def write_call(raw, scale):
    return pl.pallas_call(
        write_kernel,
        out_shape=pltpu.HBM((LOCAL, G, PLANE), F32),
        in_specs=[HBM_SPEC, VMEM_SPEC],
        out_specs=HBM_SPEC,
        scratch_shapes=[pltpu.VMEM(RAW.shape, F32), pltpu.SemaphoreType.DMA((FB * LOCAL + FB,))],
        name="write",
        cost_estimate=pl.CostEstimate(flops=10**6, bytes_accessed=11 * 10**6, transcendentals=0),
        compiler_params=pltpu.CompilerParams(vmem_limit_bytes=BIG),
    )(in_hbm(raw), scale)


def entry(blocks_ref, group, e):
    return blocks_ref[e % FB, 2 * group + e // FB]


def select_kernel(count, blocks_ref, *refs):
    group = lax.axis_index("frag")
    ins, outs, rows = refs[:4], refs[4:-1], refs[-1]
    for k in range(count):
        for s in range(N_FRAG):
            for e in range(ENT):
                for q in range(ROWS):
                    rows[k, s * ENT + e, pl.ds(q, 1), :] = ins[s][k, pl.ds(e, 1), pl.ds(128 * q, 128)]
    for k in range(count):
        for e in range(ENT):
            block = entry(blocks_ref, group, e)
            place = lax.rem(group - block // ENT + N_FRAG, N_FRAG) * ENT + lax.rem(block, ENT)
            outs[k][pl.ds(e * ROWS, ROWS), :] = rows[k, place]
            outs[count + k][pl.ds(e * ROWS, ROWS), :] = rows[k, e]


def select_call(blocks, arrays):
    count = arrays[0].shape[0]
    piece = jax.ShapeDtypeStruct((PIECE, 128), F32)
    out_shape = (piece,) * (2 * count)
    return pl.pallas_call(
        functools.partial(select_kernel, count),
        out_shape=out_shape,
        in_specs=[SMEM_SPEC] + [VMEM_SPEC] * 4,
        out_specs=(VMEM_SPEC,) * (2 * count),
        scratch_shapes=[pltpu.VMEM((count, N_FRAG * ENT, ROWS, 128), F32)],
        name=f"select{count}",
        compiler_params=pltpu.CompilerParams(vmem_limit_bytes=8 << 20),
    )(blocks, *arrays)


def place_kernel(blocks_hbm, p0_hbm, p1, p2, p3, out_ref, rows, p0, blocks_ref, sem):
    loads = [pltpu.make_async_copy(blocks_hbm, blocks_ref, sem.at[0]), pltpu.make_async_copy(p0_hbm, p0, sem.at[1])]
    for load in loads:
        load.start()
    group = lax.axis_index("frag")
    for s, ref in ((1, p1), (2, p2), (3, p3), (0, p0)):
        if s == 0:
            for load in loads:
                load.wait()
        for e in range(ENT):
            for q in range(ROWS):
                rows[s * ENT + e, pl.ds(q, 1), :] = ref[pl.ds(e, 1), pl.ds(128 * q, 128)]
    tail = jnp.zeros((2, 128), F32)
    for e in range(ENT):
        block = entry(blocks_ref, group, e)
        place = lax.rem(group - block // ENT + N_FRAG, N_FRAG) * ENT + lax.rem(block, ENT)
        value = rows[place]
        for slot in range(SLOTS):
            out_ref[slot, pl.ds(e * ROWS, ROWS), :] = value
    for slot in range(SLOTS):
        out_ref[slot, pl.ds(PIECE, 2), :] = tail


def place_call(blocks, pots):
    return pl.pallas_call(
        place_kernel,
        out_shape=SPREAD,
        in_specs=[HBM_SPEC] * 2 + [VMEM_SPEC] * 3,
        out_specs=VMEM_SPEC,
        scratch_shapes=[
            pltpu.VMEM((N_FRAG * ENT, ROWS, 128), F32),
            pltpu.VMEM((ENT, CELLS), F32),
            pltpu.SMEM((FB, 2 * N_FRAG), jnp.int32),
            pltpu.SemaphoreType.DMA((2,)),
        ],
        name="place",
        compiler_params=pltpu.CompilerParams(vmem_limit_bytes=8 << 20),
    )(in_hbm(blocks), in_hbm(pots[0]), *pots[1:])


def update_kernel(final, blocks_ref, signs_ref, core_ref, ion_ref, d0, d1, d2, d3, out_ref):
    group = lax.axis_index("frag")
    seen = []
    for s, d in enumerate((d0, d1, d2, d3)):
        source = lax.rem(group - s + N_FRAG, N_FRAG)
        for k in range(ENT):
            sign = jnp.where(signs_ref[2 * source + k // FB] > 0, 1.0 / ORBS, -1.0 / ORBS)
            seen.append((entry(blocks_ref, source, k), sign.astype(F32), d[pl.ds(k * ROWS, ROWS), :]))
    for e in range(ENT):
        mine = group * ENT + e if final else entry(blocks_ref, group, e)
        total = core_ref[pl.ds(e * ROWS, ROWS), :]
        for block, sign, density in seen:
            total = total + jnp.where(block == mine, sign, jnp.float32(0.0)) * density
        total = jnp.maximum(total, DENSITY_FLOOR)
        root = jnp.exp(jnp.log(total) * (1.0 / 3.0))
        root = root - (root * root * root - total) / (3.0 * root * root)
        value = ion_ref[pl.ds(e * ROWS, ROWS), :] - EXCHANGE_COEF * root
        if final:
            for q in range(ROWS):
                out_ref[pl.ds(e, 1), pl.ds(128 * q, 128)] = value[q : q + 1]
        else:
            for slot in range(SLOTS):
                out_ref[slot, pl.ds(e * ROWS, ROWS), :] = value
    if not final:
        for slot in range(SLOTS):
            out_ref[slot, pl.ds(PIECE, 2), :] = jnp.zeros((2, 128), F32)


def update_call(final, blocks, signs, core, ion, densities):
    return pl.pallas_call(
        functools.partial(update_kernel, final),
        out_shape=jax.ShapeDtypeStruct((ENT, CELLS), F32) if final else SPREAD,
        in_specs=[SMEM_SPEC] * 2 + [VMEM_SPEC] * 6,
        out_specs=VMEM_SPEC,
        name="update_last" if final else "update_first",
        compiler_params=pltpu.CompilerParams(vmem_limit_bytes=8 << 20),
    )(blocks, signs, core, ion, *densities)


def frag_all(value):
    return [value] + [
        lax.ppermute(value, "frag", [(g, (g + s) % N_FRAG) for g in range(N_FRAG)]) for s in (1, 2, 3)
    ]


def core_swap(value):
    return lax.ppermute(value, "orb", [(i, i ^ 1) for i in range(2 * SLOTS)])


def plane_exchange(value):
    groups = [[2 * i + c for i in range(SLOTS)] for c in range(2)]
    return lax.all_to_all(value, "orb", 0, 0, axis_index_groups=groups, tiled=True)


def shards(orbitals, potential, ion_potential, core_density, frag_blocks, frag_signs):
    blocks = frag_blocks.T
    mats = jnp.asarray(stencil_matrices(), BF16)

    pots = frag_all(potential)
    spread, source = lax.optimization_barrier((place_call(blocks, pots), orbitals.reshape(LOCAL, G, PLANE)))
    near = plane_exchange(spread)
    field, plain = prepare_call(True, (source,), mats)
    near, field = lax.optimization_barrier((near, field))
    statics = frag_all(jnp.stack([core_density, ion_potential]))
    raw, scale, mine, other = filter_call(field, plain, near, core_swap(near), mats)
    cores, ions, own_core, own_ion = select_call(blocks, statics)

    density, raw = lax.optimization_barrier((mine + core_swap(other), raw))
    density = plane_exchange(density)
    field, plain = prepare_call(False, (raw, scale), mats)
    density, field = lax.optimization_barrier((density, field))
    densities = frag_all(jnp.sum(density, axis=0))
    near = plane_exchange(update_call(False, blocks, frag_signs, cores, ions, densities))
    raw, scale, mine, other = filter_call(field, plain, near, core_swap(near), mats)

    density, raw = lax.optimization_barrier((mine + core_swap(other), raw))
    density = plane_exchange(density)
    filtered = write_call(raw, scale)
    density, filtered = lax.optimization_barrier((density, filtered))
    densities = frag_all(jnp.sum(density, axis=0))
    new_potential = update_call(True, blocks, frag_signs, own_core, own_ion, densities)
    return (filtered.reshape(orbitals.shape), new_potential)


def solution(mesh):
    in_specs = (
        P("frag", "orb", None, None),
        P("frag", "orb"),
        P("frag", "orb"),
        P("frag", "orb"),
        P(),
        P(),
    )
    out_specs = (P("frag", "orb", None, None), P("frag", "orb"))
    return jax.shard_map(shards, mesh=mesh, in_specs=in_specs, out_specs=out_specs, check_vma=False)
```

time: 754 us -> 143 us (0.19)
  waiting for transfers between devices: 265 us -> 22.4 us
  other arithmetic: 191 us -> 1.71 us
  local copies, waits for them, and re-layouts: 167 us -> 1.15 us
  blocking collectives: 104 us -> 16.8 us
  Pallas kernels: 0 us -> 62 us
  starting transfers between devices: 4.58 us -> 37.7 us
  between operations: 14.8 us -> 0.8 us
    unnamed x4 -> x0, waiting for transfers between devices: 236 us -> none
    unnamed x58 -> x12, local copies, waits for them, and re-layouts: 143 us -> 1.15 us
    sub x4 -> x0, other arithmetic: 72.7 us -> none  [chebyshev(): 2.0 * (hamiltonian(current, local_pot) - FILTER_CENTER * current)]
    reduce_sum x7 -> x2, other arithmetic: 64.3 us -> 0.06 us  [shards(): densities = frag_all(jnp.sum(density, axis=0))]
    pallas_call x0 -> x9, Pallas kernels: none -> 62 us  [the longest x2 34.9 us: filter_call(): pl.pallas_call(filter_kernel, out_shape=(RAW_HBM, SCALE, SPREAD, SPREAD),...]
    all_gather x2 -> x0, blocking collectives: 51 us -> none  [shards(): owned = lax.all_gather(current_pot, 'orb', axis=1, tiled=True)]
    div x5 -> x0, other arithmetic: 38 us -> none  [the longest x2 37.2 us: chebyshev(): (hamiltonian(values, local_pot) - FILTER_CENTER * values) / FILTER_HALF]
    all_to_all x3 -> x1, blocking collectives: 52.9 us -> 16.8 us  [plane_exchange(): lax.all_to_all(value, 'orb', 0, 0, axis_index_groups=groups, tiled=True)]
  transfers between devices with their start and end apart: 3 -> 19, of which waited for: 3 -> 12; matrix products, arithmetic and copies ran while one was open for 0% -> 0% of each run, Pallas kernels for 0% -> 16%
where the time goes in v1:
time: 143 us; the launch traced here: 142 us
  Pallas kernels  62 us (43%)
  starting transfers between devices  37.7 us (26%)
  waiting for transfers between devices  22.4 us (16%)
  blocking collectives  16.8 us (12%)
  other arithmetic  1.71 us (1%)
    pallas_call x2, Pallas kernels, filter_call(): pl.pallas_call(filter_kernel, out_shape=(RAW_HBM, SCALE, SPREAD, SPREAD),...  34.9 us
    ppermute x12, starting transfers between devices, frag_all(): lax.ppermute(value, 'frag', [(g, (g + s) % N_FRAG) for g in range(N_FRAG)])  19.1 us
    all_to_all x3, starting transfers between devices, plane_exchange(): lax.all_to_all(value, 'orb', 0, 0, axis_index_groups=groups, tiled=True)  18.1 us
    pallas_call x2, Pallas kernels, prepare_call(): pl.pallas_call(functools.partial(prepare_kernel, first), out_shape=(RAW_H...  17.8 us
    all_to_all x1, blocking collectives, plane_exchange(): lax.all_to_all(value, 'orb', 0, 0, axis_index_groups=groups, tiled=True)  16.8 us
    ppermute x12, waiting for transfers between devices, frag_all(): lax.ppermute(value, 'frag', [(g, (g + s) % N_FRAG) for g in range(N_FRAG)])  7.92 us
    all_to_all x3, waiting for transfers between devices, plane_exchange(): lax.all_to_all(value, 'orb', 0, 0, axis_index_groups=groups, tiled=True)  7.54 us
    ppermute x4, waiting for transfers between devices, core_swap(): return lax.ppermute(value, 'orb', [(i, i ^ 1) for i in range(2 * SLOTS)])  6.97 us
  transfers between devices with their start and end apart: 19, of which 12 were waited for; matrix products, arithmetic and copies ran while one was open for 0% of the time, Pallas kernels for 16%

profile of v1, /device:TPU:0, one launch (start us, length us, event | category | flops | bytes accessed | tf_op | source)
XLA Modules:
  0.0 142.4 jit_solution(12475994434598854664)
XLA Ops:
  0.6 1.8 %collective-permute-start = (f32[6,1152]{1,0:T(8,128)}, f32[6,1152]{1,0:T(8,128)S(1)}, u32[]{:S(2)}, u32[]{:S(2)}) collective-permute-start(f32[6,1152]{1,0:T(8,128)} %p0_hbm.1), channel_id=1, source_target_pairs={{0,32},{32,64},{64,96},{96,0},{1,33},{33,65},{65,97},{97,1},{2,34}... | collective-permute-start | bytes 82952 | tf_op jit(solution)/shard_map/ppermute | solution.py:443
  2.4 2.9 %collective-permute-start.1 = (f32[6,1152]{1,0:T(8,128)}, f32[6,1152]{1,0:T(8,128)S(1)}, u32[]{:S(2)}, u32[]{:S(2)}) collective-permute-start(f32[6,1152]{1,0:T(8,128)} %p0_hbm.1), channel_id=1, source_target_pairs={{0,64},{32,96},{64,0},{96,32},{1,65},{33,97},{65,1},{97,33},{2,66}... | collective-permute-start | bytes 82952 | tf_op jit(solution)/shard_map/ppermute | solution.py:443
  9.5 1.7 %place.1 = f32[16,56,128]{2,1,0:T(8,128)} custom-call(s32[3,8]{1,0:T(4,128)} %bitcast.5, f32[6,1152]{1,0:T(8,128)} %p0_hbm.1, f32[6,1152]{1,0:T(8,128)S(1)} %collective-permute-done.p1, f32[6,1152]{1,0:T(8,128)S(1)} %collective-permute-done.1.p2, f32[6,1152]{1,0:T(8,128)S(1)} %collective-permute-done.2.p3), custom_call_target="tpu_custom_call" | custom-call | tf_op jit(solution)/shard_map/place/pallas_call | solution.py:386
  11.1 7.9 %all-to-all-start = ((f32[16,56,128]{2,1,0:T(8,128)}), f32[16,56,128]{2,1,0:T(8,128)S(1)}, u32[]{:S(2)}, u32[]{:S(2)}) async-start(f32[16,56,128]{2,1,0:T(8,128)} %place.1), calls=%async_computation | async-start | bytes 917504 | tf_op jit(solution)/shard_map/all_to_all | solution.py:453
  20.2 7.9 %prepare_first.1 = (f32[48,8,2304]{2,1,0:T(8,128)}, f32[48,8,2304]{2,1,0:T(8,128)}) custom-call(f32[8,48,2304]{2,1,0:T(8,128)} %bitcast.12, bf16[3,512,256]{2,1,0:T(8,128)(2,1)S(1)} %copy-done.2), custom_call_target="tpu_custom_call" | custom-call | flops 2000000000 | bytes 11000000 | tf_op jit(solution)/shard_map/prepare_first/pallas_call | solution.py:279
  28.8 1.8 %collective-permute-done.3.other_ref = f32[16,56,128]{2,1,0:T(8,128)S(1)} collective-permute-done((f32[16,56,128]{2,1,0:T(8,128)S(1)}, f32[16,56,128]{2,1,0:T(8,128)S(1)}, u32[]{:S(2)}, u32[]{:S(2)}) %collective-permute-start.3) | collective-permute-done | bytes 458784 | tf_op jit(solution)/shard_map/ppermute | solution.py:448
  30.6 17.4 %filter.2 = (f32[48,8,2304]{2,1,0:T(8,128)}, f32[8,128]{1,0:T(8,128)S(1)}, f32[16,56,128]{2,1,0:T(8,128)S(1)}, f32[16,56,128]{2,1,0:T(8,128)S(1)}) custom-call(f32[48,8,2304]{2,1,0:T(8,128)} %get-tuple-element.33.field_hbm, f32[48,8,2304]{2,1,0:T(8,128)} %get-tuple-element.34.plain_hbm, f32[16,56,128]{2,1,0:T(8,128)S(1)} %all-to-all-done.mine_ref, ...), custom_call_target="tpu_custom_call" | custom-call | flops 8000000000 | bytes 14000000 | tf_op jit(solution)/shard_map/filter/pallas_call | solution.py:292
  48.2 1.7 %collective-permute-done.4 = f32[16,56,128]{2,1,0:T(8,128)S(1)} collective-permute-done((f32[16,56,128]{2,1,0:T(8,128)S(1)}, f32[16,56,128]{2,1,0:T(8,128)S(1)}, u32[]{:S(2)}, u32[]{:S(2)}) %collective-permute-start.4) | collective-permute-done | bytes 458784 | tf_op jit(solution)/shard_map/ppermute | solution.py:448
  50.7 6.7 %all-to-all-start.1 = ((f32[16,56,128]{2,1,0:T(8,128)}), f32[16,56,128]{2,1,0:T(8,128)S(1)}, u32[]{:S(2)}, u32[]{:S(2)}) async-start(f32[16,56,128]{2,1,0:T(8,128)} %add.6), calls=%async_computation.1 | async-start | bytes 917504 | tf_op jit(solution)/shard_map/all_to_all | solution.py:453
  57.7 3.8 %collective-permute-start.6 = (f32[2,6,1152]{2,1,0:T(8,128)S(1)}, f32[2,6,1152]{2,1,0:T(8,128)S(1)}, u32[]{:S(2)}, u32[]{:S(2)}) collective-permute-start(f32[2,6,1152]{2,1,0:T(8,128)S(1)} %pad_maximum_fusion.refs_0_), channel_id=1, source_target_pairs={{0,64},{32,96},{64,0},{96,32},{1,65},{33,97},{65,1},{97,33},{2,66}... | collective-permute-start | bytes 165896 | tf_op jit(solution)/shard_map/ppermute | solution.py:443
  61.7 9.9 %prepare_next.1 = (f32[48,8,2304]{2,1,0:T(8,128)}, f32[48,8,2304]{2,1,0:T(8,128)}) custom-call(f32[48,8,2304]{2,1,0:T(8,128)} %get-tuple-element.40.source, f32[8,128]{1,0:T(8,128)S(1)} %get-tuple-element.41.refs_0_, bf16[3,512,256]{2,1,0:T(8,128)(2,1)S(1)} %copy-done.3), custom_call_target="tpu_custom_call" | custom-call | flops 2000000000 | bytes 11000000 | tf_op jit(solution)/shard_map/prepare_next/pallas_call | solution.py:279
  72.1 1.6 %collective-permute-start.8 = (f32[56,128]{1,0:T(8,128)S(1)}, f32[56,128]{1,0:T(8,128)S(1)}, u32[]{:S(2)}, u32[]{:S(2)}) collective-permute-start(f32[56,128]{1,0:T(8,128)S(1)} %reduce_sum.18.d0), channel_id=1, source_target_pairs={{0,32},{32,64},{64,96},{96,0},{1,33},{33,65},{65,97},{97,1},{2,34}... | collective-permute-start | bytes 86024 | tf_op jit(solution)/shard_map/ppermute | solution.py:443
  73.7 2.0 %collective-permute-start.9 = (f32[56,128]{1,0:T(8,128)S(1)}, f32[56,128]{1,0:T(8,128)S(1)}, u32[]{:S(2)}, u32[]{:S(2)}) collective-permute-start(f32[56,128]{1,0:T(8,128)S(1)} %reduce_sum.18.d0), channel_id=1, source_target_pairs={{0,64},{32,96},{64,0},{96,32},{1,65},{33,97},{65,1},{97,33},{2,66}... | collective-permute-start | bytes 86024 | tf_op jit(solution)/shard_map/ppermute | solution.py:443
  77.2 1.9 %collective-permute-done.9.d2 = f32[56,128]{1,0:T(8,128)S(1)} collective-permute-done((f32[56,128]{1,0:T(8,128)S(1)}, f32[56,128]{1,0:T(8,128)S(1)}, u32[]{:S(2)}, u32[]{:S(2)}) %collective-permute-start.9) | collective-permute-done | bytes 28704 | tf_op jit(solution)/shard_map/ppermute | solution.py:443
  79.9 16.8 %all_to_all.20.mine_ref = f32[16,56,128]{2,1,0:T(8,128)S(1)} all-to-all(f32[16,56,128]{2,1,0:T(8,128)S(1)} %update_first.1), channel_id=1, replica_groups={{0,2,4,6,8,10,12,14,16,18,20,22,24,26,28,30},{1,3,5,7,9,11,13,15,17,19,..., dimensions={0} | all-to-all | bytes 917504 | tf_op jit(solution)/shard_map/all_to_all | solution.py:453
  96.7 1.8 %collective-permute-done.11.other_ref = f32[16,56,128]{2,1,0:T(8,128)S(1)} collective-permute-done((f32[16,56,128]{2,1,0:T(8,128)S(1)}, f32[16,56,128]{2,1,0:T(8,128)S(1)}, u32[]{:S(2)}, u32[]{:S(2)}) %collective-permute-start.11) | collective-permute-done | bytes 458784 | tf_op jit(solution)/shard_map/ppermute | solution.py:448
  98.5 17.4 %filter.3 = (f32[48,8,2304]{2,1,0:T(8,128)}, f32[8,128]{1,0:T(8,128)S(1)}, f32[16,56,128]{2,1,0:T(8,128)S(1)}, f32[16,56,128]{2,1,0:T(8,128)S(1)}) custom-call(f32[48,8,2304]{2,1,0:T(8,128)} %get-tuple-element.43.field_hbm, f32[48,8,2304]{2,1,0:T(8,128)} %get-tuple-element.44.plain_hbm, f32[16,56,128]{2,1,0:T(8,128)S(1)} %all_to_all.20.mine_ref, ...), custom_call_target="tpu_custom_call" | custom-call | flops 8000000000 | bytes 14000000 | tf_op jit(solution)/shard_map/filter/pallas_call | solution.py:292
  116.2 1.7 %collective-permute-done.12 = f32[16,56,128]{2,1,0:T(8,128)S(1)} collective-permute-done((f32[16,56,128]{2,1,0:T(8,128)S(1)}, f32[16,56,128]{2,1,0:T(8,128)S(1)}, u32[]{:S(2)}, u32[]{:S(2)}) %collective-permute-start.12) | collective-permute-done | bytes 458784 | tf_op jit(solution)/shard_map/ppermute | solution.py:448
  118.7 3.6 %all-to-all-start.3 = ((f32[16,56,128]{2,1,0:T(8,128)}), f32[16,56,128]{2,1,0:T(8,128)S(1)}, u32[]{:S(2)}, u32[]{:S(2)}) async-start(f32[16,56,128]{2,1,0:T(8,128)} %add.7), calls=%async_computation.3 | async-start | bytes 917504 | tf_op jit(solution)/shard_map/all_to_all | solution.py:453
  122.2 4.5 %write.1 = f32[8,48,2304]{2,1,0:T(8,128)} custom-call(f32[48,8,2304]{2,1,0:T(8,128)} %get-tuple-element.52.raw_hbm, f32[8,128]{1,0:T(8,128)S(1)} %get-tuple-element.53.scale_ref), custom_call_target="tpu_custom_call" | custom-call | flops 1000000 | bytes 11000000 | tf_op jit(solution)/shard_map/write/pallas_call | solution.py:315
  126.7 6.9 %all-to-all-done.3 = f32[16,56,128]{2,1,0:T(8,128)S(1)} async-done(((f32[16,56,128]{2,1,0:T(8,128)}), f32[16,56,128]{2,1,0:T(8,128)S(1)}, u32[]{:S(2)}, u32[]{:S(2)}) %all-to-all-start.3) | async-done | bytes 458784 | tf_op jit(solution)/shard_map/all_to_all | solution.py:453
  133.7 2.0 %collective-permute-start.13 = (f32[56,128]{1,0:T(8,128)S(1)}, f32[56,128]{1,0:T(8,128)S(1)}, u32[]{:S(2)}, u32[]{:S(2)}) collective-permute-start(f32[56,128]{1,0:T(8,128)S(1)} %reduce_sum.19.d0), channel_id=1, source_target_pairs={{0,32},{32,64},{64,96},{96,0},{1,33},{33,65},{65,97},{97,1},{2,34}... | collective-permute-start | bytes 86024 | tf_op jit(solution)/shard_map/ppermute | solution.py:443
  136.8 1.5 %collective-permute-start.15 = (f32[56,128]{1,0:T(8,128)S(1)}, f32[56,128]{1,0:T(8,128)S(1)}, u32[]{:S(2)}, u32[]{:S(2)}) collective-permute-start(f32[56,128]{1,0:T(8,128)S(1)} %reduce_sum.19.d0), channel_id=1, source_target_pairs={{0,96},{32,0},{64,32},{96,64},{1,97},{33,1},{65,33},{97,65},{2,98}... | collective-permute-start | bytes 86024 | tf_op jit(solution)/shard_map/ppermute | solution.py:443
  139.0 2.0 %collective-permute-done.14.d2 = f32[56,128]{1,0:T(8,128)S(1)} collective-permute-done((f32[56,128]{1,0:T(8,128)S(1)}, f32[56,128]{1,0:T(8,128)S(1)}, u32[]{:S(2)}, u32[]{:S(2)}) %collective-permute-start.14) | collective-permute-done | bytes 28704 | tf_op jit(solution)/shard_map/ppermute | solution.py:443
  (41 shorter events, 14.6 us)
Async XLA Ops:
  0.6 6.0 %collective-permute-start = (f32[6,1152]{1,0:T(8,128)}, f32[6,1152]{1,0:T(8,128)S(1)}, u32[]{:S(2)}, u32[]{:S(2)}) collective-permute-start(f32[6,1152]{1,0:T(8,128)} %p0_hbm.1), channel_id=1, source_target_pairs={{0,32},{32,64},{64,96},{96,0},{1,33},{33,65},{65,97},{97,1},{2,34}... | collective-permute-start | bytes 82952 | tf_op jit(solution)/shard_map/ppermute | solution.py:443
  2.4 5.7 %collective-permute-start.1 = (f32[6,1152]{1,0:T(8,128)}, f32[6,1152]{1,0:T(8,128)S(1)}, u32[]{:S(2)}, u32[]{:S(2)}) collective-permute-start(f32[6,1152]{1,0:T(8,128)} %p0_hbm.1), channel_id=1, source_target_pairs={{0,64},{32,96},{64,0},{96,32},{1,65},{33,97},{65,1},{97,33},{2,66}... | collective-permute-start | bytes 82952 | tf_op jit(solution)/shard_map/ppermute | solution.py:443
  5.3 4.2 %collective-permute-start.2 = (f32[6,1152]{1,0:T(8,128)}, f32[6,1152]{1,0:T(8,128)S(1)}, u32[]{:S(2)}, u32[]{:S(2)}) collective-permute-start(f32[6,1152]{1,0:T(8,128)} %p0_hbm.1), channel_id=1, source_target_pairs={{0,96},{32,0},{64,32},{96,64},{1,97},{33,1},{65,33},{97,65},{2,98}... | collective-permute-start | bytes 82952 | tf_op jit(solution)/shard_map/ppermute | solution.py:443
  11.1 17.6 %all-to-all-start = ((f32[16,56,128]{2,1,0:T(8,128)}), f32[16,56,128]{2,1,0:T(8,128)S(1)}, u32[]{:S(2)}, u32[]{:S(2)}) async-start(f32[16,56,128]{2,1,0:T(8,128)} %place.1), calls=%async_computation | async-start | bytes 917504 | tf_op jit(solution)/shard_map/all_to_all | solution.py:453
  20.2 10.4 %copy-start.3 = (bf16[3,512,256]{2,1,0:T(8,128)(2,1)S(1)}, bf16[3,512,256]{2,1,0:T(8,128)(2,1)}, u32[]{:S(2)}) copy-start(bf16[3,512,256]{2,1,0:T(8,128)(2,1)} %constant.4.clone.refs_0_.mats_ref.refs_1_) | copy-start | bytes 2359300
  28.8 1.8 %collective-permute-start.3 = (f32[16,56,128]{2,1,0:T(8,128)S(1)}, f32[16,56,128]{2,1,0:T(8,128)S(1)}, u32[]{:S(2)}, u32[]{:S(2)}) collective-permute-start(f32[16,56,128]{2,1,0:T(8,128)S(1)} %all-to-all-done.mine_ref), channel_id=1, source_target_pairs={{0,1},{1,0},{2,3},{3,2},{4,5},{5,4},{6,7},{7,6},{8,9},{9,8},{10,11... | collective-permute-start | bytes 1376264 | tf_op jit(solution)/shard_map/ppermute | solution.py:448
  30.6 26.8 %copy-start.4 = (f32[6,1152]{1,0:T(8,128)S(1)}, f32[6,1152]{1,0:T(8,128)}, u32[]{:S(2)}) copy-start(f32[6,1152]{1,0:T(8,128)} %param.9) | copy-start | bytes 82948
  30.6 26.9 %copy-start.5 = (f32[6,1152]{1,0:T(8,128)S(1)}, f32[6,1152]{1,0:T(8,128)}, u32[]{:S(2)}) copy-start(f32[6,1152]{1,0:T(8,128)} %param.10) | copy-start | bytes 82948
  48.0 1.9 %collective-permute-start.4 = (f32[16,56,128]{2,1,0:T(8,128)S(1)}, f32[16,56,128]{2,1,0:T(8,128)S(1)}, u32[]{:S(2)}, u32[]{:S(2)}) collective-permute-start(f32[16,56,128]{2,1,0:T(8,128)S(1)} %get-tuple-element.37), channel_id=1, source_target_pairs={{0,1},{1,0},{2,3},{3,2},{4,5},{5,4},{6,7},{7,6},{8,9},{9,8},{10,11... | collective-permute-start | bytes 1376264 | tf_op jit(solution)/shard_map/ppermute | solution.py:448
  50.7 20.8 %all-to-all-start.1 = ((f32[16,56,128]{2,1,0:T(8,128)}), f32[16,56,128]{2,1,0:T(8,128)S(1)}, u32[]{:S(2)}, u32[]{:S(2)}) async-start(f32[16,56,128]{2,1,0:T(8,128)} %add.6), calls=%async_computation.1 | async-start | bytes 917504 | tf_op jit(solution)/shard_map/all_to_all | solution.py:453
  57.5 16.3 %collective-permute-start.5 = (f32[2,6,1152]{2,1,0:T(8,128)S(1)}, f32[2,6,1152]{2,1,0:T(8,128)S(1)}, u32[]{:S(2)}, u32[]{:S(2)}) collective-permute-start(f32[2,6,1152]{2,1,0:T(8,128)S(1)} %pad_maximum_fusion.refs_0_), channel_id=1, source_target_pairs={{0,32},{32,64},{64,96},{96,0},{1,33},{33,65},{65,97},{97,1},{2,34}... | collective-permute-start | bytes 165896 | tf_op jit(solution)/shard_map/ppermute | solution.py:443
  57.7 18.1 %collective-permute-start.6 = (f32[2,6,1152]{2,1,0:T(8,128)S(1)}, f32[2,6,1152]{2,1,0:T(8,128)S(1)}, u32[]{:S(2)}, u32[]{:S(2)}) collective-permute-start(f32[2,6,1152]{2,1,0:T(8,128)S(1)} %pad_maximum_fusion.refs_0_), channel_id=1, source_target_pairs={{0,64},{32,96},{64,0},{96,32},{1,65},{33,97},{65,1},{97,33},{2,66}... | collective-permute-start | bytes 165896 | tf_op jit(solution)/shard_map/ppermute | solution.py:443
  61.5 14.2 %collective-permute-start.7 = (f32[2,6,1152]{2,1,0:T(8,128)S(1)}, f32[2,6,1152]{2,1,0:T(8,128)S(1)}, u32[]{:S(2)}, u32[]{:S(2)}) collective-permute-start(f32[2,6,1152]{2,1,0:T(8,128)S(1)} %pad_maximum_fusion.refs_0_), channel_id=1, source_target_pairs={{0,96},{32,0},{64,32},{96,64},{1,97},{33,1},{65,33},{97,65},{2,98}... | collective-permute-start | bytes 165896 | tf_op jit(solution)/shard_map/ppermute | solution.py:443
  61.7 14.1 %copy-start = (s32[8,3]{0,1:T(4,128)S(1)}, s32[8,3]{0,1:T(4,128)}, u32[]{:S(2)}) copy-start(s32[8,3]{0,1:T(4,128)} %param.11) | copy-start | bytes 292
  61.7 17.4 %copy-start.1 = (s32[8]{0:T(128)S(1)}, s32[8]{0:T(128)}, u32[]{:S(2)}) copy-start(s32[8]{0:T(128)} %signs_ref.3) | copy-start | bytes 100
  71.6 5.0 %collective-permute-start.10 = (f32[56,128]{1,0:T(8,128)S(1)}, f32[56,128]{1,0:T(8,128)S(1)}, u32[]{:S(2)}, u32[]{:S(2)}) collective-permute-start(f32[56,128]{1,0:T(8,128)S(1)} %reduce_sum.18.d0), channel_id=1, source_target_pairs={{0,96},{32,0},{64,32},{96,64},{1,97},{33,1},{65,33},{97,65},{2,98}... | collective-permute-start | bytes 86024 | tf_op jit(solution)/shard_map/ppermute | solution.py:443
  72.1 5.1 %collective-permute-start.8 = (f32[56,128]{1,0:T(8,128)S(1)}, f32[56,128]{1,0:T(8,128)S(1)}, u32[]{:S(2)}, u32[]{:S(2)}) collective-permute-start(f32[56,128]{1,0:T(8,128)S(1)} %reduce_sum.18.d0), channel_id=1, source_target_pairs={{0,32},{32,64},{64,96},{96,0},{1,33},{33,65},{65,97},{97,1},{2,34}... | collective-permute-start | bytes 86024 | tf_op jit(solution)/shard_map/ppermute | solution.py:443
  73.7 5.4 %collective-permute-start.9 = (f32[56,128]{1,0:T(8,128)S(1)}, f32[56,128]{1,0:T(8,128)S(1)}, u32[]{:S(2)}, u32[]{:S(2)}) collective-permute-start(f32[56,128]{1,0:T(8,128)S(1)} %reduce_sum.18.d0), channel_id=1, source_target_pairs={{0,64},{32,96},{64,0},{96,32},{1,65},{33,97},{65,1},{97,33},{2,66}... | collective-permute-start | bytes 86024 | tf_op jit(solution)/shard_map/ppermute | solution.py:443
  96.7 1.8 %collective-permute-start.11 = (f32[16,56,128]{2,1,0:T(8,128)S(1)}, f32[16,56,128]{2,1,0:T(8,128)S(1)}, u32[]{:S(2)}, u32[]{:S(2)}) collective-permute-start(f32[16,56,128]{2,1,0:T(8,128)S(1)} %all_to_all.20.mine_ref), channel_id=1, source_target_pairs={{0,1},{1,0},{2,3},{3,2},{4,5},{5,4},{6,7},{7,6},{8,9},{9,8},{10,11... | collective-permute-start | bytes 1376264 | tf_op jit(solution)/shard_map/ppermute | solution.py:448
  115.9 1.9 %collective-permute-start.12 = (f32[16,56,128]{2,1,0:T(8,128)S(1)}, f32[16,56,128]{2,1,0:T(8,128)S(1)}, u32[]{:S(2)}, u32[]{:S(2)}) collective-permute-start(f32[16,56,128]{2,1,0:T(8,128)S(1)} %get-tuple-element.49), channel_id=1, source_target_pairs={{0,1},{1,0},{2,3},{3,2},{4,5},{5,4},{6,7},{7,6},{8,9},{9,8},{10,11... | collective-permute-start | bytes 1376264 | tf_op jit(solution)/shard_map/ppermute | solution.py:448
  118.7 15.0 %all-to-all-start.3 = ((f32[16,56,128]{2,1,0:T(8,128)}), f32[16,56,128]{2,1,0:T(8,128)S(1)}, u32[]{:S(2)}, u32[]{:S(2)}) async-start(f32[16,56,128]{2,1,0:T(8,128)} %add.7), calls=%async_computation.3 | async-start | bytes 917504 | tf_op jit(solution)/shard_map/all_to_all | solution.py:453
  133.7 5.4 %collective-permute-start.13 = (f32[56,128]{1,0:T(8,128)S(1)}, f32[56,128]{1,0:T(8,128)S(1)}, u32[]{:S(2)}, u32[]{:S(2)}) collective-permute-start(f32[56,128]{1,0:T(8,128)S(1)} %reduce_sum.19.d0), channel_id=1, source_target_pairs={{0,32},{32,64},{64,96},{96,0},{1,33},{33,65},{65,97},{97,1},{2,34}... | collective-permute-start | bytes 86024 | tf_op jit(solution)/shard_map/ppermute | solution.py:443
  135.6 5.4 %collective-permute-start.14 = (f32[56,128]{1,0:T(8,128)S(1)}, f32[56,128]{1,0:T(8,128)S(1)}, u32[]{:S(2)}, u32[]{:S(2)}) collective-permute-start(f32[56,128]{1,0:T(8,128)S(1)} %reduce_sum.19.d0), channel_id=1, source_target_pairs={{0,64},{32,96},{64,0},{96,32},{1,65},{33,97},{65,1},{97,33},{2,66}... | collective-permute-start | bytes 86024 | tf_op jit(solution)/shard_map/ppermute | solution.py:443
  136.8 4.2 %collective-permute-start.15 = (f32[56,128]{1,0:T(8,128)S(1)}, f32[56,128]{1,0:T(8,128)S(1)}, u32[]{:S(2)}, u32[]{:S(2)}) collective-permute-start(f32[56,128]{1,0:T(8,128)S(1)} %reduce_sum.19.d0), channel_id=1, source_target_pairs={{0,96},{32,0},{64,32},{96,64},{1,97},{33,1},{65,33},{97,65},{2,98}... | collective-permute-start | bytes 86024 | tf_op jit(solution)/shard_map/ppermute | solution.py:443
  (1 other events, 1.1 us)

commit v2 on v1

--- a/solution.py
+++ b/solution.py
@@ -14,7 +14,9 @@
 ORBS = 128
 N_FRAG = 4
 SLOTS = 16
-CHUNK = 16
+BAND = 64
+BANDS = 6
+UNROLL = 4
 LOADS = 6
 XLOAD = G // LOADS
 BIG = 40 << 20
@@ -26,7 +28,7 @@
 COLS = 256
 WIN = 512
 STEPS = PLANE // COLS
-PADDED = PLANE + 256
+TILES = PLANE // 128 + 2
 DENSITY_FLOOR = 0.25
 EXCHANGE_COEF = 0.9847450218426965
 NORM_EPS = 1e-6
@@ -67,80 +69,118 @@
 
 def zero_margins(halves):
     for part in range(2):
-        halves[:, pl.ds(part * PADDED, 128)] = jnp.zeros((G * LOCAL, 128), BF16)
-        halves[:, pl.ds(part * PADDED + PLANE + 128, 128)] = jnp.zeros((G * LOCAL, 128), BF16)
+        halves[part * TILES] = jnp.zeros((G * LOCAL, 128), BF16)
+        halves[part * TILES + TILES - 1] = jnp.zeros((G * LOCAL, 128), BF16)
 
 
 def put_halves(halves, c, values):
-    high, low = split(values.reshape(16, PLANE))
     rows = pl.ds(pl.multiple_of(16 * c, 16), 16)
-    halves[rows, pl.ds(128, PLANE)] = high
-    halves[rows, pl.ds(PADDED + 128, PLANE)] = low
-
-
-def apply(kind, cur, prev, dst, wf, mats_ref, halves, halves_next, acc_even, acc_odd, sums):
-    def product(n, c, acc):
-        rows = pl.ds(CHUNK * LOCAL * c, CHUNK * LOCAL)
-        mat = mats_ref[lax.rem(n, 3)]
-        acc[rows, :] = jnp.dot(halves[rows, cols(COLS * n, WIN)], mat, preferred_element_type=F32) + jnp.dot(
-            halves[rows, cols(PADDED + COLS * n, WIN)], mat, preferred_element_type=F32
-        )
-
-    def emit(n, c, acc):
-        for t in range(COLS // 128):
-            lane = cols(COLS * n + 128 * t)
-            for d in range(CHUNK * c // 8, CHUNK * (c + 1) // 8):
-                near = cur[pl.ds(8 * d, 12), :, lane]
+    for j in range(TILES - 2):
+        high, low = split(values[:, :, 128 * j : 128 * j + 128].reshape(16, 128))
+        halves[1 + j, rows, :] = high
+        halves[TILES + 1 + j, rows, :] = low
+
+
+def run_chain(apps, mats_ref):
+    def scoped(*accs):
+        def acc(parity, unit, i):
+            return accs[(2 * parity + unit) * BANDS + i]
+
+        def push(n, parity, unit):
+            mat = jnp.concatenate([mats_ref[lax.rem(n, 3), t, pl.ds(COLS * unit, COLS), :] for t in range(2)], axis=1)
+            pltpu.matmul_push_rhs(mat, staging_register=parity, mxu_index=unit)
+
+        def feed(app, n, parity, i):
+            halves = app[5]
+            rows = pl.ds(BAND * i, BAND)
+            for unit in range(2):
+                high, low = (
+                    jnp.concatenate([halves[part * TILES + 2 * (n + unit) + t, rows, :] for t in range(2)], axis=1)
+                    for part in range(2)
+                )
+                pltpu.matmul_acc_lhs(acc(parity, unit, i), high, load_staged_rhs=parity if i == 0 else None)
+                pltpu.matmul_acc_lhs(acc(parity, unit, i), low)
+                if i == BANDS - 2 + unit:
+                    push(n + 1, 1 - parity, unit)
+
+        def emit(app, n, parity, i):
+            kind, cur, prev, dst, wf, _, halves_next, sums, done = app
+            rows = pl.ds(BAND * i, BAND)
+            values = pltpu.matmul_pop(acc(parity, 0, i)) + pltpu.matmul_pop(acc(parity, 1, i))
+            for t in range(COLS // 128):
+                lane = cols(COLS * n + 128 * t)
+                near = cur[pl.ds(8 * i, 12), :, lane]
                 s1 = near[1:9] + near[3:11]
                 s2 = near[0:8] + near[4:12]
-                rows = pl.ds(64 * d, 64)
-                plane = acc[rows, pl.ds(128 * t, 128)].reshape(8, LOCAL, 128)
+                plane = values[:, 128 * t : 128 * t + 128].reshape(8, LOCAL, 128)
                 new = plane + s2 - 16.0 * s1
-                here = pl.ds(8 * d + (0 if kind == "plain" else 2), 8)
+                here = pl.ds(8 * i + (0 if kind == "plain" else 2), 8)
                 if kind == "plain":
                     dst[here, :, lane] = (0.5 / 48.0) * new
                     continue
-                new = (1.0 / 48.0) * new + wf[pl.ds(8 * d, 8), :, lane] * near[2:10]
-                new = new - prev[pl.ds(8 * d + 2, 8), :, lane]
+                new = (1.0 / 48.0) * new + wf[pl.ds(8 * i, 8), :, lane] * near[2:10]
+                new = new - prev[pl.ds(8 * i + 2, 8), :, lane]
                 dst[here, :, lane] = new
                 if kind == "last":
                     sums[...] += jnp.sum(new * new, axis=0)
                 else:
-                    high, low = split(new.reshape(64, 128))
-                    halves_next[rows, cols(COLS * n + 128 * t + 128)] = high
-                    halves_next[rows, cols(PADDED + COLS * n + 128 * t + 128)] = low
-
-    parts = G // CHUNK
-    for c in range(parts):
-        product(0, c, acc_even)
-
-    def body(i, carry):
-        for c in range(parts):
-            product(2 * i + 1, c, acc_odd)
-            emit(2 * i, c, acc_even)
-        for c in range(parts):
-            product(2 * i + 2, c, acc_even)
-            emit(2 * i + 1, c, acc_odd)
-        return carry
-
-    lax.fori_loop(0, STEPS // 2, body, 0)
-    for c in range(parts):
-        emit(STEPS - 1, c, acc_even)
+                    high, low = split(new.reshape(BAND, 128))
+                    halves_next[2 * n + t + 1, rows, :] = high
+                    halves_next[TILES + 2 * n + t + 1, rows, :] = low
+            if done is not None and i == BANDS - 1:
+                done(n)
+
+        for unit in range(2):
+            push(0, 0, unit)
+        for i in range(BANDS):
+            feed(apps[0], 0, 0, i)
+        for number, app in enumerate(apps):
+
+            def body(j, carry):
+                for u in range(UNROLL):
+                    for i in range(BANDS):
+                        feed(app, UNROLL * j + u + 1, (number + u + 1) % 2, i)
+                        emit(app, UNROLL * j + u, (number + u) % 2, i)
+                return carry
+
+            lax.fori_loop(0, STEPS // UNROLL, body, 0)
+            for i in range(BANDS):
+                if number + 1 < len(apps):
+                    feed(apps[number + 1], 0, (number + 1) % 2, i)
+                emit(app, STEPS - 1, number % 2, i)
+        rest = len(apps) % 2
+        for unit in range(2):
+            pltpu.matmul_acc_lhs(acc(rest, unit, 0), jnp.zeros((BAND, COLS), BF16), load_staged_rhs=rest)
+            pltpu.matmul_pop(acc(rest, unit, 0))
+
+    pl.run_scoped(
+        scoped,
+        *[pltpu.ACC(unit)((BAND, COLS), F32) for _ in range(2) for unit in range(2) for _ in range(BANDS)],
+    )
 
 
 def prepare_kernel(first, source, *refs):
     if first:
-        mats_ref, field_hbm, plain_hbm, field, plain, hl, acc0, acc1, sem = refs
-        loads = [pltpu.make_async_copy(source.at[o], field.at[pl.ds(2, G), o, :], sem.at[o]) for o in range(LOCAL)]
+        mats_ref, field_hbm, plain_hbm, field, plain, hl, sem = refs
     else:
-        scale_ref, mats_ref, field_hbm, plain_hbm, field, plain, hl, acc0, acc1, sem = refs
-        loads = [pltpu.make_async_copy(source, field.at[pl.ds(2, G)], sem.at[0])]
-    for load in loads:
-        load.start()
+        scale_ref, mats_ref, field_hbm, plain_hbm, field, plain, hl, sem = refs
+    loads = []
+    for p in range(FB):
+        inner = pl.ds(2 + 16 * p, 16)
+        x = pl.ds(16 * p, 16)
+        if first:
+            loads.append(
+                [
+                    pltpu.make_async_copy(source.at[o, x], field.at[inner, o, :], sem.at[LOCAL * p + o])
+                    for o in range(LOCAL)
+                ]
+            )
+        else:
+            loads.append([pltpu.make_async_copy(source.at[x], field.at[inner], sem.at[LOCAL * p])])
+        for load in loads[-1]:
+            load.start()
     zero_planes(field)
     zero_margins(hl)
-    for load in loads:
-        load.wait()
     scale = None if first else jnp.broadcast_to(scale_ref[:, 0:1], (LOCAL, PLANE))
 
     def body(c, scale):
@@ -152,20 +192,31 @@
         put_halves(hl, c, values)
         return scale
 
-    lax.fori_loop(0, G // 2, body, scale)
-    stores = [
-        pltpu.make_async_copy(field.at[pl.ds(2, G)], field_hbm, sem.at[0]),
-        pltpu.make_async_copy(plain, plain_hbm, sem.at[1]),
-    ]
-    stores[0].start()
-    apply("plain", field, None, plain, None, mats_ref, hl, None, acc0, acc1, None)
-    stores[1].start()
+    stores = []
+    for p in range(FB):
+        for load in loads[p]:
+            load.wait()
+        lax.fori_loop(8 * p, 8 * p + 8, body, scale)
+        stores.append(
+            pltpu.make_async_copy(
+                field.at[pl.ds(2 + 16 * p, 16)], field_hbm.at[pl.ds(16 * p, 16)], sem.at[FB * LOCAL + p]
+            )
+        )
+        stores[-1].start()
+
+    def column(n):
+        lane = cols(COLS * n, COLS)
+        return pltpu.make_async_copy(plain.at[:, :, lane], plain_hbm.at[:, :, lane], sem.at[FB * (LOCAL + 1) + n])
+
+    run_chain([("plain", field, None, plain, None, hl, None, None, lambda n: column(n).start())], mats_ref)
     for store in stores:
         store.wait()
+    for n in range(STEPS):
+        column(n).wait()
 
 
 def filter_kernel(field_hbm, plain_hbm, mine_ref, other_ref, mats_ref, raw_hbm, scale_ref, dmine_ref, dother_ref,
-                  ya, yb, wf, hl0, hl1, acc0, acc1, sums, sem):
+                  ya, yb, wf, hl0, hl1, sums, sem):
     core = lax.axis_index("orb") % 2
     loads = []
     for p in range(LOADS):
@@ -189,7 +240,7 @@
                 wf[16 * b + row, :, cols(half * CELLS, CELLS)] = jnp.concatenate(tiles, axis=1)
         return carry
 
-    lax.fori_loop(0, SLOTS, build, 0)
+    lax.fori_loop(0, SLOTS, build, 0, unroll=2)
     zero_planes(ya)
     zero_planes(yb)
     zero_margins(hl0)
@@ -207,9 +258,14 @@
         loads[2 * p].wait()
         loads[2 * p + 1].wait()
         lax.fori_loop(p * XLOAD // 2, (p + 1) * XLOAD // 2, start, 0)
-    apply("middle", yb, ya, ya, wf, mats_ref, hl0, hl1, acc0, acc1, sums)
-    apply("middle", ya, yb, yb, wf, mats_ref, hl1, hl0, acc0, acc1, sums)
-    apply("last", yb, ya, ya, wf, mats_ref, hl0, None, acc0, acc1, sums)
+    run_chain(
+        [
+            ("middle", yb, ya, ya, wf, hl0, hl1, sums, None),
+            ("middle", ya, yb, yb, wf, hl1, hl0, sums, None),
+            ("last", yb, ya, ya, wf, hl0, None, sums, None),
+        ],
+        mats_ref,
+    )
     store = pltpu.make_async_copy(ya.at[pl.ds(2, G)], raw_hbm, sem.at[0])
     store.start()
     mean = jnp.sum(sums[...], axis=1, keepdims=True) * (1.0 / (G * PLANE))
@@ -229,7 +285,7 @@
             ref[row, pl.ds(PIECE, 2), :] = jnp.zeros((2, 128), F32)
         return scale
 
-    lax.fori_loop(0, SLOTS, finish, jnp.broadcast_to(inverse, (LOCAL, CELLS)))
+    lax.fori_loop(0, SLOTS, finish, jnp.broadcast_to(inverse, (LOCAL, CELLS)), unroll=2)
     store.wait()
 
 
@@ -266,9 +322,7 @@
 RAW_HBM = pltpu.HBM((G, LOCAL, PLANE), F32)
 SCALE = jax.ShapeDtypeStruct((LOCAL, 128), F32)
 SPREAD = jax.ShapeDtypeStruct((SLOTS, PIECE + 2, 128), F32)
-HALVES = pltpu.VMEM((G * LOCAL, 2 * PADDED), BF16)
-ACC = pltpu.VMEM((G * LOCAL, COLS), F32)
-MATS = (3, WIN, COLS)
+HALVES = pltpu.VMEM((2 * TILES, G * LOCAL, 128), BF16)
 
 
 def in_hbm(value):
@@ -281,7 +335,8 @@
         out_shape=(RAW_HBM, RAW_HBM),
         in_specs=[HBM_SPEC] + [VMEM_SPEC] * len(source),
         out_specs=(HBM_SPEC, HBM_SPEC),
-        scratch_shapes=[PLANES, pltpu.VMEM(RAW.shape, F32), HALVES, ACC, ACC, pltpu.SemaphoreType.DMA((LOCAL,))],
+        scratch_shapes=[PLANES, pltpu.VMEM(RAW.shape, F32), HALVES]
+        + [pltpu.SemaphoreType.DMA((FB * (LOCAL + 1) + STEPS,))],
         name="prepare_first" if first else "prepare_next",
         cost_estimate=pl.CostEstimate(flops=2 * 10**9, bytes_accessed=11 * 10**6, transcendentals=0),
         compiler_params=pltpu.CompilerParams(vmem_limit_bytes=BIG),
@@ -300,8 +355,6 @@
             pltpu.VMEM(RAW.shape, F32),
             HALVES,
             HALVES,
-            ACC,
-            ACC,
             pltpu.VMEM((LOCAL, 128), F32),
             pltpu.SemaphoreType.DMA((2 * LOADS,)),
         ],
@@ -455,7 +508,8 @@
 
 def shards(orbitals, potential, ion_potential, core_density, frag_blocks, frag_signs):
     blocks = frag_blocks.T
-    mats = jnp.asarray(stencil_matrices(), BF16)
+    mats = stencil_matrices().reshape(3, WIN, 2, 128).transpose(0, 2, 1, 3)
+    mats = jnp.asarray(mats, BF16)
 
     pots = frag_all(potential)
     spread, source = lax.optimization_barrier((place_call(blocks, pots), orbitals.reshape(LOCAL, G, PLANE)))
@@ -466,12 +520,13 @@
     raw, scale, mine, other = filter_call(field, plain, near, core_swap(near), mats)
     cores, ions, own_core, own_ion = select_call(blocks, statics)
 
-    density, raw = lax.optimization_barrier((mine + core_swap(other), raw))
-    density = plane_exchange(density)
+    density = plane_exchange(mine + core_swap(other))
+    densities = frag_all(jnp.sum(density, axis=0))
+    spread = update_call(False, blocks, frag_signs, cores, ions, densities)
+    spread, raw = lax.optimization_barrier((spread, raw))
+    near = plane_exchange(spread)
     field, plain = prepare_call(False, (raw, scale), mats)
-    density, field = lax.optimization_barrier((density, field))
-    densities = frag_all(jnp.sum(density, axis=0))
-    near = plane_exchange(update_call(False, blocks, frag_signs, cores, ions, densities))
+    near, field = lax.optimization_barrier((near, field))
     raw, scale, mine, other = filter_call(field, plain, near, core_swap(near), mats)
 
     density, raw = lax.optimization_barrier((mine + core_swap(other), raw))

time: 143 us -> 126 us (0.88)
  blocking collectives: 16.8 us -> 0 us
  Pallas kernels: 62 us -> 45.7 us
  waiting for transfers between devices: 22.4 us -> 35.9 us
  starting transfers between devices: 37.7 us -> 39.8 us
    all_to_all x1 -> x0, blocking collectives: 16.8 us -> none  [plane_exchange(): lax.all_to_all(value, 'orb', 0, 0, axis_index_groups=groups, tiled=True)]
    all_to_all x3 -> x4, waiting for transfers between devices: 7.54 us -> 19.2 us  [plane_exchange(): lax.all_to_all(value, 'orb', 0, 0, axis_index_groups=groups, tiled=True)]
    pallas_call x2, Pallas kernels: 34.9 us -> 23.4 us  [filter_call(): pl.pallas_call(filter_kernel, out_shape=(RAW_HBM, SCALE, SPREAD, SPREAD),...]
    pallas_call x2, Pallas kernels: 17.8 us -> 12.3 us  [prepare_call(): pl.pallas_call(functools.partial(prepare_kernel, first), out_shape=(RAW_H...]
    all_to_all x3 -> x4, starting transfers between devices: 18.1 us -> 20.2 us  [plane_exchange(): lax.all_to_all(value, 'orb', 0, 0, axis_index_groups=groups, tiled=True)]
    ppermute x12, waiting for transfers between devices: 7.92 us -> 9.67 us  [frag_all(): lax.ppermute(value, 'frag', [(g, (g + s) % N_FRAG) for g in range(N_FRAG)])]
  transfers between devices with their start and end apart: 19 -> 20, of which waited for: 12 -> 15; matrix products, arithmetic and copies ran while one was open for 0% -> 0% of each run, Pallas kernels for 16% -> 14%
where the time goes in v2:
time: 126 us; the launch traced here: 125 us
  Pallas kernels  45.7 us (36%)
  starting transfers between devices  39.8 us (32%)
  waiting for transfers between devices  35.9 us (28%)
  other arithmetic  1.71 us (1%)
    pallas_call x2, Pallas kernels, filter_call(): pl.pallas_call(filter_kernel, out_shape=(RAW_HBM, SCALE, SPREAD, SPREAD),...  23.4 us
    all_to_all x4, starting transfers between devices, plane_exchange(): lax.all_to_all(value, 'orb', 0, 0, axis_index_groups=groups, tiled=True)  20.2 us
    all_to_all x4, waiting for transfers between devices, plane_exchange(): lax.all_to_all(value, 'orb', 0, 0, axis_index_groups=groups, tiled=True)  19.2 us
    ppermute x12, starting transfers between devices, frag_all(): lax.ppermute(value, 'frag', [(g, (g + s) % N_FRAG) for g in range(N_FRAG)])  19.2 us
    pallas_call x2, Pallas kernels, prepare_call(): pl.pallas_call(functools.partial(prepare_kernel, first), out_shape=(RAW_H...  12.3 us
    ppermute x12, waiting for transfers between devices, frag_all(): lax.ppermute(value, 'frag', [(g, (g + s) % N_FRAG) for g in range(N_FRAG)])  9.67 us
    ppermute x4, waiting for transfers between devices, core_swap(): return lax.ppermute(value, 'orb', [(i, i ^ 1) for i in range(2 * SLOTS)])  6.98 us
    pallas_call x1, Pallas kernels, write_call(): pl.pallas_call(write_kernel, out_shape=pltpu.HBM((LOCAL, G, PLANE), F32),...  4.5 us
  transfers between devices with their start and end apart: 20, of which 15 were waited for; matrix products, arithmetic and copies ran while one was open for 0% of the time, Pallas kernels for 14%

profile of v2, /device:TPU:0, one launch (start us, length us, event | category | flops | bytes accessed | tf_op | source)
XLA Modules:
  0.0 125.0 jit_solution(11449010068916137465)
XLA Ops:
  0.6 1.8 %collective-permute-start.3 = (f32[6,1152]{1,0:T(8,128)}, f32[6,1152]{1,0:T(8,128)S(1)}, u32[]{:S(2)}, u32[]{:S(2)}) collective-permute-start(f32[6,1152]{1,0:T(8,128)} %p0_hbm.1), channel_id=1, source_target_pairs={{0,32},{32,64},{64,96},{96,0},{1,33},{33,65},{65,97},{97,1},{2,34}... | collective-permute-start | bytes 82952 | tf_op jit(solution)/shard_map/ppermute | solution.py:496
  2.4 2.9 %collective-permute-start.4 = (f32[6,1152]{1,0:T(8,128)}, f32[6,1152]{1,0:T(8,128)S(1)}, u32[]{:S(2)}, u32[]{:S(2)}) collective-permute-start(f32[6,1152]{1,0:T(8,128)} %p0_hbm.1), channel_id=1, source_target_pairs={{0,64},{32,96},{64,0},{96,32},{1,65},{33,97},{65,1},{97,33},{2,66}... | collective-permute-start | bytes 82952 | tf_op jit(solution)/shard_map/ppermute | solution.py:496
  11.1 7.9 %all-to-all-start = ((f32[16,56,128]{2,1,0:T(8,128)}), f32[16,56,128]{2,1,0:T(8,128)S(1)}, u32[]{:S(2)}, u32[]{:S(2)}) async-start(f32[16,56,128]{2,1,0:T(8,128)} %place.1), calls=%async_computation | async-start | bytes 917504 | tf_op jit(solution)/shard_map/all_to_all | solution.py:506
  20.1 5.5 %prepare_first.1 = (f32[48,8,2304]{2,1,0:T(8,128)}, f32[48,8,2304]{2,1,0:T(8,128)}) custom-call(f32[8,48,2304]{2,1,0:T(8,128)} %bitcast.12, bf16[3,2,512,128]{3,2,1,0:T(8,128)(2,1)S(1)} %copy-done.2), custom_call_target="tpu_custom_call" | custom-call | flops 2000000000 | bytes 11000000 | tf_op jit(solution)/shard_map/prepare_first/pallas_call | solution.py:333
  25.6 3.1 %all-to-all-done.mine_ref = f32[16,56,128]{2,1,0:T(8,128)S(1)} async-done(((f32[16,56,128]{2,1,0:T(8,128)}), f32[16,56,128]{2,1,0:T(8,128)S(1)}, u32[]{:S(2)}, u32[]{:S(2)}) %all-to-all-start) | async-done | bytes 458784 | tf_op jit(solution)/shard_map/all_to_all | solution.py:506
  28.8 1.8 %collective-permute-done.6.other_ref = f32[16,56,128]{2,1,0:T(8,128)S(1)} collective-permute-done((f32[16,56,128]{2,1,0:T(8,128)S(1)}, f32[16,56,128]{2,1,0:T(8,128)S(1)}, u32[]{:S(2)}, u32[]{:S(2)}) %collective-permute-start.6) | collective-permute-done | bytes 458784 | tf_op jit(solution)/shard_map/ppermute | solution.py:501
  30.6 11.7 %filter.2 = (f32[48,8,2304]{2,1,0:T(8,128)}, f32[8,128]{1,0:T(8,128)S(1)}, f32[16,56,128]{2,1,0:T(8,128)S(1)}, f32[16,56,128]{2,1,0:T(8,128)S(1)}) custom-call(f32[48,8,2304]{2,1,0:T(8,128)} %get-tuple-element.35.field_hbm, f32[48,8,2304]{2,1,0:T(8,128)} %get-tuple-element.36.plain_hbm, f32[16,56,128]{2,1,0:T(8,128)S(1)} %all-to-all-done.mine_ref, ...), custom_call_target="tpu_custom_call" | custom-call | flops 8000000000 | bytes 14000000 | tf_op jit(solution)/shard_map/filter/pallas_call | solution.py:347
  42.5 1.7 %collective-permute-done.7 = f32[16,56,128]{2,1,0:T(8,128)S(1)} collective-permute-done((f32[16,56,128]{2,1,0:T(8,128)S(1)}, f32[16,56,128]{2,1,0:T(8,128)S(1)}, u32[]{:S(2)}, u32[]{:S(2)}) %collective-permute-start.7) | collective-permute-done | bytes 458784 | tf_op jit(solution)/shard_map/ppermute | solution.py:501
  45.0 4.2 %all-to-all-start.1 = ((f32[16,56,128]{2,1,0:T(8,128)}), f32[16,56,128]{2,1,0:T(8,128)S(1)}, u32[]{:S(2)}, u32[]{:S(2)}) async-start(f32[16,56,128]{2,1,0:T(8,128)} %add.6), calls=%async_computation.1 | async-start | bytes 917504 | tf_op jit(solution)/shard_map/all_to_all | solution.py:506
  49.5 3.8 %collective-permute-start.1 = (f32[2,6,1152]{2,1,0:T(8,128)S(1)}, f32[2,6,1152]{2,1,0:T(8,128)S(1)}, u32[]{:S(2)}, u32[]{:S(2)}) collective-permute-start(f32[2,6,1152]{2,1,0:T(8,128)S(1)} %pad_maximum_fusion.refs_0_), channel_id=1, source_target_pairs={{0,64},{32,96},{64,0},{96,32},{1,65},{33,97},{65,1},{97,33},{2,66}... | collective-permute-start | bytes 165896 | tf_op jit(solution)/shard_map/ppermute | solution.py:496
  53.4 6.8 %all-to-all-done.1 = f32[16,56,128]{2,1,0:T(8,128)S(1)} async-done(((f32[16,56,128]{2,1,0:T(8,128)}), f32[16,56,128]{2,1,0:T(8,128)S(1)}, u32[]{:S(2)}, u32[]{:S(2)}) %all-to-all-start.1) | async-done | bytes 458784 | tf_op jit(solution)/shard_map/all_to_all | solution.py:506
  60.3 2.6 %collective-permute-start.10 = (f32[56,128]{1,0:T(8,128)S(1)}, f32[56,128]{1,0:T(8,128)S(1)}, u32[]{:S(2)}, u32[]{:S(2)}) collective-permute-start(f32[56,128]{1,0:T(8,128)S(1)} %reduce_sum.18.d0), channel_id=1, source_target_pairs={{0,96},{32,0},{64,32},{96,64},{1,97},{33,1},{65,33},{97,65},{2,98}... | collective-permute-start | bytes 86024 | tf_op jit(solution)/shard_map/ppermute | solution.py:496
  65.4 2.7 %collective-permute-done.8.d1 = f32[56,128]{1,0:T(8,128)S(1)} collective-permute-done((f32[56,128]{1,0:T(8,128)S(1)}, f32[56,128]{1,0:T(8,128)S(1)}, u32[]{:S(2)}, u32[]{:S(2)}) %collective-permute-start.8) | collective-permute-done | bytes 28704 | tf_op jit(solution)/shard_map/ppermute | solution.py:496
  69.9 3.7 %all-to-all-start.2 = ((f32[16,56,128]{2,1,0:T(8,128)}), f32[16,56,128]{2,1,0:T(8,128)S(1)}, u32[]{:S(2)}, u32[]{:S(2)}) async-start(f32[16,56,128]{2,1,0:T(8,128)} %update_first.1), calls=%async_computation.2 | async-start | bytes 917504 | tf_op jit(solution)/shard_map/all_to_all | solution.py:506
  73.7 6.9 %prepare_next.1 = (f32[48,8,2304]{2,1,0:T(8,128)}, f32[48,8,2304]{2,1,0:T(8,128)}) custom-call(f32[48,8,2304]{2,1,0:T(8,128)} %get-tuple-element.42.source, f32[8,128]{1,0:T(8,128)S(1)} %get-tuple-element.43.refs_0_, bf16[3,2,512,128]{3,2,1,0:T(8,128)(2,1)S(1)} %copy-done.3), custom_call_target="tpu_custom_call" | custom-call | flops 2000000000 | bytes 11000000 | tf_op jit(solution)/shard_map/prepare_next/pallas_call | solution.py:333
  80.6 2.7 %all-to-all-done.2.mine_ref = f32[16,56,128]{2,1,0:T(8,128)S(1)} async-done(((f32[16,56,128]{2,1,0:T(8,128)}), f32[16,56,128]{2,1,0:T(8,128)S(1)}, u32[]{:S(2)}, u32[]{:S(2)}) %all-to-all-start.2) | async-done | bytes 458784 | tf_op jit(solution)/shard_map/all_to_all | solution.py:506
  83.2 1.8 %collective-permute-done.11.other_ref = f32[16,56,128]{2,1,0:T(8,128)S(1)} collective-permute-done((f32[16,56,128]{2,1,0:T(8,128)S(1)}, f32[16,56,128]{2,1,0:T(8,128)S(1)}, u32[]{:S(2)}, u32[]{:S(2)}) %collective-permute-start.11) | collective-permute-done | bytes 458784 | tf_op jit(solution)/shard_map/ppermute | solution.py:501
  85.0 11.7 %filter.3 = (f32[48,8,2304]{2,1,0:T(8,128)}, f32[8,128]{1,0:T(8,128)S(1)}, f32[16,56,128]{2,1,0:T(8,128)S(1)}, f32[16,56,128]{2,1,0:T(8,128)S(1)}) custom-call(f32[48,8,2304]{2,1,0:T(8,128)} %get-tuple-element.45.field_hbm, f32[48,8,2304]{2,1,0:T(8,128)} %get-tuple-element.46.plain_hbm, f32[16,56,128]{2,1,0:T(8,128)S(1)} %all-to-all-done.2.mine_ref, ...), custom_call_target="tpu_custom_call" | custom-call | flops 8000000000 | bytes 14000000 | tf_op jit(solution)/shard_map/filter/pallas_call | solution.py:347
  99.4 4.4 %all-to-all-start.3 = ((f32[16,56,128]{2,1,0:T(8,128)}), f32[16,56,128]{2,1,0:T(8,128)S(1)}, u32[]{:S(2)}, u32[]{:S(2)}) async-start(f32[16,56,128]{2,1,0:T(8,128)} %add.7), calls=%async_computation.3 | async-start | bytes 917504 | tf_op jit(solution)/shard_map/all_to_all | solution.py:506
  103.8 4.5 %write.1 = f32[8,48,2304]{2,1,0:T(8,128)} custom-call(f32[48,8,2304]{2,1,0:T(8,128)} %get-tuple-element.52.raw_hbm, f32[8,128]{1,0:T(8,128)S(1)} %get-tuple-element.53.scale_ref), custom_call_target="tpu_custom_call" | custom-call | flops 1000000 | bytes 11000000 | tf_op jit(solution)/shard_map/write/pallas_call | solution.py:368
  108.3 6.6 %all-to-all-done.3 = f32[16,56,128]{2,1,0:T(8,128)S(1)} async-done(((f32[16,56,128]{2,1,0:T(8,128)}), f32[16,56,128]{2,1,0:T(8,128)S(1)}, u32[]{:S(2)}, u32[]{:S(2)}) %all-to-all-start.3) | async-done | bytes 458784 | tf_op jit(solution)/shard_map/all_to_all | solution.py:506
  115.6 4.1 %collective-permute-start.14 = (f32[56,128]{1,0:T(8,128)S(1)}, f32[56,128]{1,0:T(8,128)S(1)}, u32[]{:S(2)}, u32[]{:S(2)}) collective-permute-start(f32[56,128]{1,0:T(8,128)S(1)} %reduce_sum.19.d0), channel_id=1, source_target_pairs={{0,64},{32,96},{64,0},{96,32},{1,65},{33,97},{65,1},{97,33},{2,66}... | collective-permute-start | bytes 86024 | tf_op jit(solution)/shard_map/ppermute | solution.py:496
  120.1 1.8 %collective-permute-done.14.d2 = f32[56,128]{1,0:T(8,128)S(1)} collective-permute-done((f32[56,128]{1,0:T(8,128)S(1)}, f32[56,128]{1,0:T(8,128)S(1)}, u32[]{:S(2)}, u32[]{:S(2)}) %collective-permute-start.14) | collective-permute-done | bytes 28704 | tf_op jit(solution)/shard_map/ppermute | solution.py:496
  121.9 1.7 %collective-permute-done.15.d3 = f32[56,128]{1,0:T(8,128)S(1)} collective-permute-done((f32[56,128]{1,0:T(8,128)S(1)}, f32[56,128]{1,0:T(8,128)S(1)}, u32[]{:S(2)}, u32[]{:S(2)}) %collective-permute-start.15) | collective-permute-done | bytes 28704 | tf_op jit(solution)/shard_map/ppermute | solution.py:496
  (42 shorter events, 17.9 us)
Async XLA Ops:
  0.6 6.0 %collective-permute-start.3 = (f32[6,1152]{1,0:T(8,128)}, f32[6,1152]{1,0:T(8,128)S(1)}, u32[]{:S(2)}, u32[]{:S(2)}) collective-permute-start(f32[6,1152]{1,0:T(8,128)} %p0_hbm.1), channel_id=1, source_target_pairs={{0,32},{32,64},{64,96},{96,0},{1,33},{33,65},{65,97},{97,1},{2,34}... | collective-permute-start | bytes 82952 | tf_op jit(solution)/shard_map/ppermute | solution.py:496
  2.4 5.7 %collective-permute-start.4 = (f32[6,1152]{1,0:T(8,128)}, f32[6,1152]{1,0:T(8,128)S(1)}, u32[]{:S(2)}, u32[]{:S(2)}) collective-permute-start(f32[6,1152]{1,0:T(8,128)} %p0_hbm.1), channel_id=1, source_target_pairs={{0,64},{32,96},{64,0},{96,32},{1,65},{33,97},{65,1},{97,33},{2,66}... | collective-permute-start | bytes 82952 | tf_op jit(solution)/shard_map/ppermute | solution.py:496
  5.3 4.2 %collective-permute-start.5 = (f32[6,1152]{1,0:T(8,128)}, f32[6,1152]{1,0:T(8,128)S(1)}, u32[]{:S(2)}, u32[]{:S(2)}) collective-permute-start(f32[6,1152]{1,0:T(8,128)} %p0_hbm.1), channel_id=1, source_target_pairs={{0,96},{32,0},{64,32},{96,64},{1,97},{33,1},{65,33},{97,65},{2,98}... | collective-permute-start | bytes 82952 | tf_op jit(solution)/shard_map/ppermute | solution.py:496
  11.1 17.6 %all-to-all-start = ((f32[16,56,128]{2,1,0:T(8,128)}), f32[16,56,128]{2,1,0:T(8,128)S(1)}, u32[]{:S(2)}, u32[]{:S(2)}) async-start(f32[16,56,128]{2,1,0:T(8,128)} %place.1), calls=%async_computation | async-start | bytes 917504 | tf_op jit(solution)/shard_map/all_to_all | solution.py:506
  28.7 1.8 %collective-permute-start.6 = (f32[16,56,128]{2,1,0:T(8,128)S(1)}, f32[16,56,128]{2,1,0:T(8,128)S(1)}, u32[]{:S(2)}, u32[]{:S(2)}) collective-permute-start(f32[16,56,128]{2,1,0:T(8,128)S(1)} %all-to-all-done.mine_ref), channel_id=1, source_target_pairs={{0,1},{1,0},{2,3},{3,2},{4,5},{5,4},{6,7},{7,6},{8,9},{9,8},{10,11... | collective-permute-start | bytes 1376264 | tf_op jit(solution)/shard_map/ppermute | solution.py:501
  30.6 18.6 %copy-start.4 = (f32[6,1152]{1,0:T(8,128)S(1)}, f32[6,1152]{1,0:T(8,128)}, u32[]{:S(2)}) copy-start(f32[6,1152]{1,0:T(8,128)} %param.9) | copy-start | bytes 82948
  30.6 18.6 %copy-start.5 = (f32[6,1152]{1,0:T(8,128)S(1)}, f32[6,1152]{1,0:T(8,128)}, u32[]{:S(2)}) copy-start(f32[6,1152]{1,0:T(8,128)} %param.10) | copy-start | bytes 82948
  30.6 33.9 %copy-start = (s32[8,3]{0,1:T(4,128)S(1)}, s32[8,3]{0,1:T(4,128)}, u32[]{:S(2)}) copy-start(s32[8,3]{0,1:T(4,128)} %param.11) | copy-start | bytes 292
  30.6 37.8 %copy-start.1 = (s32[8]{0:T(128)S(1)}, s32[8]{0:T(128)}, u32[]{:S(2)}) copy-start(s32[8]{0:T(128)} %signs_ref.3) | copy-start | bytes 100
  42.3 1.9 %collective-permute-start.7 = (f32[16,56,128]{2,1,0:T(8,128)S(1)}, f32[16,56,128]{2,1,0:T(8,128)S(1)}, u32[]{:S(2)}, u32[]{:S(2)}) collective-permute-start(f32[16,56,128]{2,1,0:T(8,128)S(1)} %get-tuple-element.39), channel_id=1, source_target_pairs={{0,1},{1,0},{2,3},{3,2},{4,5},{5,4},{6,7},{7,6},{8,9},{9,8},{10,11... | collective-permute-start | bytes 1376264 | tf_op jit(solution)/shard_map/ppermute | solution.py:501
  45.0 15.3 %all-to-all-start.1 = ((f32[16,56,128]{2,1,0:T(8,128)}), f32[16,56,128]{2,1,0:T(8,128)S(1)}, u32[]{:S(2)}, u32[]{:S(2)}) async-start(f32[16,56,128]{2,1,0:T(8,128)} %add.6), calls=%async_computation.1 | async-start | bytes 917504 | tf_op jit(solution)/shard_map/all_to_all | solution.py:506
  49.2 13.7 %collective-permute-start = (f32[2,6,1152]{2,1,0:T(8,128)S(1)}, f32[2,6,1152]{2,1,0:T(8,128)S(1)}, u32[]{:S(2)}, u32[]{:S(2)}) collective-permute-start(f32[2,6,1152]{2,1,0:T(8,128)S(1)} %pad_maximum_fusion.refs_0_), channel_id=1, source_target_pairs={{0,32},{32,64},{64,96},{96,0},{1,33},{33,65},{65,97},{97,1},{2,34}... | collective-permute-start | bytes 165896 | tf_op jit(solution)/shard_map/ppermute | solution.py:496
  49.5 15.0 %collective-permute-start.1 = (f32[2,6,1152]{2,1,0:T(8,128)S(1)}, f32[2,6,1152]{2,1,0:T(8,128)S(1)}, u32[]{:S(2)}, u32[]{:S(2)}) collective-permute-start(f32[2,6,1152]{2,1,0:T(8,128)S(1)} %pad_maximum_fusion.refs_0_), channel_id=1, source_target_pairs={{0,64},{32,96},{64,0},{96,32},{1,65},{33,97},{65,1},{97,33},{2,66}... | collective-permute-start | bytes 165896 | tf_op jit(solution)/shard_map/ppermute | solution.py:496
  53.3 11.2 %collective-permute-start.2 = (f32[2,6,1152]{2,1,0:T(8,128)S(1)}, f32[2,6,1152]{2,1,0:T(8,128)S(1)}, u32[]{:S(2)}, u32[]{:S(2)}) collective-permute-start(f32[2,6,1152]{2,1,0:T(8,128)S(1)} %pad_maximum_fusion.refs_0_), channel_id=1, source_target_pairs={{0,96},{32,0},{64,32},{96,64},{1,97},{33,1},{65,33},{97,65},{2,98}... | collective-permute-start | bytes 165896 | tf_op jit(solution)/shard_map/ppermute | solution.py:496
  60.3 5.0 %collective-permute-start.10 = (f32[56,128]{1,0:T(8,128)S(1)}, f32[56,128]{1,0:T(8,128)S(1)}, u32[]{:S(2)}, u32[]{:S(2)}) collective-permute-start(f32[56,128]{1,0:T(8,128)S(1)} %reduce_sum.18.d0), channel_id=1, source_target_pairs={{0,96},{32,0},{64,32},{96,64},{1,97},{33,1},{65,33},{97,65},{2,98}... | collective-permute-start | bytes 86024 | tf_op jit(solution)/shard_map/ppermute | solution.py:496
  63.0 5.1 %collective-permute-start.8 = (f32[56,128]{1,0:T(8,128)S(1)}, f32[56,128]{1,0:T(8,128)S(1)}, u32[]{:S(2)}, u32[]{:S(2)}) collective-permute-start(f32[56,128]{1,0:T(8,128)S(1)} %reduce_sum.18.d0), channel_id=1, source_target_pairs={{0,32},{32,64},{64,96},{96,0},{1,33},{33,65},{65,97},{97,1},{2,34}... | collective-permute-start | bytes 86024 | tf_op jit(solution)/shard_map/ppermute | solution.py:496
  63.0 5.4 %collective-permute-start.9 = (f32[56,128]{1,0:T(8,128)S(1)}, f32[56,128]{1,0:T(8,128)S(1)}, u32[]{:S(2)}, u32[]{:S(2)}) collective-permute-start(f32[56,128]{1,0:T(8,128)S(1)} %reduce_sum.18.d0), channel_id=1, source_target_pairs={{0,64},{32,96},{64,0},{96,32},{1,65},{33,97},{65,1},{97,33},{2,66}... | collective-permute-start | bytes 86024 | tf_op jit(solution)/shard_map/ppermute | solution.py:496
  69.9 13.3 %all-to-all-start.2 = ((f32[16,56,128]{2,1,0:T(8,128)}), f32[16,56,128]{2,1,0:T(8,128)S(1)}, u32[]{:S(2)}, u32[]{:S(2)}) async-start(f32[16,56,128]{2,1,0:T(8,128)} %update_first.1), calls=%async_computation.2 | async-start | bytes 917504 | tf_op jit(solution)/shard_map/all_to_all | solution.py:506
  83.2 1.8 %collective-permute-start.11 = (f32[16,56,128]{2,1,0:T(8,128)S(1)}, f32[16,56,128]{2,1,0:T(8,128)S(1)}, u32[]{:S(2)}, u32[]{:S(2)}) collective-permute-start(f32[16,56,128]{2,1,0:T(8,128)S(1)} %all-to-all-done.2.mine_ref), channel_id=1, source_target_pairs={{0,1},{1,0},{2,3},{3,2},{4,5},{5,4},{6,7},{7,6},{8,9},{9,8},{10,11... | collective-permute-start | bytes 1376264 | tf_op jit(solution)/shard_map/ppermute | solution.py:501
  96.7 1.9 %collective-permute-start.12 = (f32[16,56,128]{2,1,0:T(8,128)S(1)}, f32[16,56,128]{2,1,0:T(8,128)S(1)}, u32[]{:S(2)}, u32[]{:S(2)}) collective-permute-start(f32[16,56,128]{2,1,0:T(8,128)S(1)} %get-tuple-element.49), channel_id=1, source_target_pairs={{0,1},{1,0},{2,3},{3,2},{4,5},{5,4},{6,7},{7,6},{8,9},{9,8},{10,11... | collective-permute-start | bytes 1376264 | tf_op jit(solution)/shard_map/ppermute | solution.py:501
  99.4 15.5 %all-to-all-start.3 = ((f32[16,56,128]{2,1,0:T(8,128)}), f32[16,56,128]{2,1,0:T(8,128)S(1)}, u32[]{:S(2)}, u32[]{:S(2)}) async-start(f32[16,56,128]{2,1,0:T(8,128)} %add.7), calls=%async_computation.3 | async-start | bytes 917504 | tf_op jit(solution)/shard_map/all_to_all | solution.py:506
  115.0 5.2 %collective-permute-start.13 = (f32[56,128]{1,0:T(8,128)S(1)}, f32[56,128]{1,0:T(8,128)S(1)}, u32[]{:S(2)}, u32[]{:S(2)}) collective-permute-start(f32[56,128]{1,0:T(8,128)S(1)} %reduce_sum.19.d0), channel_id=1, source_target_pairs={{0,32},{32,64},{64,96},{96,0},{1,33},{33,65},{65,97},{97,1},{2,34}... | collective-permute-start | bytes 86024 | tf_op jit(solution)/shard_map/ppermute | solution.py:496
  115.6 6.3 %collective-permute-start.14 = (f32[56,128]{1,0:T(8,128)S(1)}, f32[56,128]{1,0:T(8,128)S(1)}, u32[]{:S(2)}, u32[]{:S(2)}) collective-permute-start(f32[56,128]{1,0:T(8,128)S(1)} %reduce_sum.19.d0), channel_id=1, source_target_pairs={{0,64},{32,96},{64,0},{96,32},{1,65},{33,97},{65,1},{97,33},{2,66}... | collective-permute-start | bytes 86024 | tf_op jit(solution)/shard_map/ppermute | solution.py:496
  119.7 3.9 %collective-permute-start.15 = (f32[56,128]{1,0:T(8,128)S(1)}, f32[56,128]{1,0:T(8,128)S(1)}, u32[]{:S(2)}, u32[]{:S(2)}) collective-permute-start(f32[56,128]{1,0:T(8,128)S(1)} %reduce_sum.19.d0), channel_id=1, source_target_pairs={{0,96},{32,0},{64,32},{96,64},{1,97},{33,1},{65,33},{97,65},{2,98}... | collective-permute-start | bytes 86024 | tf_op jit(solution)/shard_map/ppermute | solution.py:496
  (2 other events, 11.6 us)

commit v3 on v2

--- a/solution.py
+++ b/solution.py
@@ -215,8 +215,8 @@
         column(n).wait()
 
 
-def filter_kernel(field_hbm, plain_hbm, mine_ref, other_ref, mats_ref, raw_hbm, scale_ref, dmine_ref, dother_ref,
-                  ya, yb, wf, hl0, hl1, sums, sem):
+def filter_kernel(final, field_hbm, plain_hbm, mine_ref, other_ref, mats_ref, out_hbm, scale_ref, dmine_ref,
+                  dother_ref, ya, yb, wf, hl0, hl1, sums, sem):
     core = lax.axis_index("orb") % 2
     loads = []
     for p in range(LOADS):
@@ -266,50 +266,41 @@
         ],
         mats_ref,
     )
-    store = pltpu.make_async_copy(ya.at[pl.ds(2, G)], raw_hbm, sem.at[0])
-    store.start()
+    stores = []
+    if not final:
+        stores.append(pltpu.make_async_copy(ya.at[pl.ds(2, G)], out_hbm, sem.at[0]))
+        stores[-1].start()
     mean = jnp.sum(sums[...], axis=1, keepdims=True) * (1.0 / (G * PLANE))
     inverse = 1.0 / jnp.sqrt(mean + NORM_EPS)
     scale_ref[...] = jnp.broadcast_to(inverse, (LOCAL, 128))
 
-    def finish(row, scale):
+    def finish(b, row, scale):
         for ref, half in ((dmine_ref, core), (dother_ref, 1 - core)):
-            for b in range(FB):
-                value = ya[2 + 16 * b + row, :, cols(half * CELLS, CELLS)] * scale
-                value = value * value
-                value = value + pltpu.roll(value, 1, 0)
-                value = value + pltpu.roll(value, 2, 0)
-                for q in range(ROWS):
-                    ref[row, pl.ds(b * ROWS + q, 1), :] = value[3:4, 128 * q : 128 * q + 128]
-                    ref[row, pl.ds((FB + b) * ROWS + q, 1), :] = value[7:8, 128 * q : 128 * q + 128]
-            ref[row, pl.ds(PIECE, 2), :] = jnp.zeros((2, 128), F32)
+            lane = cols(half * CELLS, CELLS)
+            value = ya[2 + 16 * b + row, :, lane] * scale
+            if final:
+                yb[2 + 16 * b + row, :, lane] = value
+            value = value * value
+            value = value + pltpu.roll(value, 1, 0)
+            value = value + pltpu.roll(value, 2, 0)
+            for q in range(ROWS):
+                ref[SLOTS - 1 - row, pl.ds(b * ROWS + q, 1), :] = value[3:4, 128 * q : 128 * q + 128]
+                ref[SLOTS - 1 - row, pl.ds((FB + b) * ROWS + q, 1), :] = value[7:8, 128 * q : 128 * q + 128]
+            if b == 0:
+                ref[SLOTS - 1 - row, pl.ds(PIECE, 2), :] = jnp.zeros((2, 128), F32)
         return scale
 
-    lax.fori_loop(0, SLOTS, finish, jnp.broadcast_to(inverse, (LOCAL, CELLS)), unroll=2)
-    store.wait()
-
-
-def write_kernel(raw_hbm, scale_ref, out_ref, buf, sem):
-    loads = []
+    scale = jnp.broadcast_to(inverse, (LOCAL, CELLS))
     for b in range(FB):
-        x = pl.ds(16 * b, 16)
-        loads.append(pltpu.make_async_copy(raw_hbm.at[x], buf.at[x], sem.at[FB * LOCAL + b]))
-        loads[-1].start()
-    stores = []
-    scale = jnp.broadcast_to(scale_ref[:, 0:1], (LOCAL, PLANE))
-    for b in range(FB):
-        loads[b].wait()
-
-        def body(c, scale):
-            x = pl.ds(16 * b + 2 * c, 2)
-            buf[x] = buf[x] * scale[None]
-            return scale
-
-        lax.fori_loop(0, 8, body, scale)
-        x = pl.ds(16 * b, 16)
-        for o in range(LOCAL):
-            stores.append(pltpu.make_async_copy(buf.at[x, o, :], out_ref.at[o, x], sem.at[b * LOCAL + o]))
-            stores[-1].start()
+        scale = lax.fori_loop(0, SLOTS, functools.partial(finish, b), scale, unroll=4)
+        if final:
+            for o in range(LOCAL):
+                stores.append(
+                    pltpu.make_async_copy(
+                        yb.at[pl.ds(2 + 16 * b, 16), o, :], out_hbm.at[o, pl.ds(16 * b, 16)], sem.at[b * LOCAL + o]
+                    )
+                )
+                stores[-1].start()
     for store in stores:
         store.wait()
 
@@ -343,10 +334,10 @@
     )(in_hbm(source[0]), *source[1:], mats)
 
 
-def filter_call(field, plain, mine, other, mats):
+def filter_call(final, field, plain, mine, other, mats):
     return pl.pallas_call(
-        filter_kernel,
-        out_shape=(RAW_HBM, SCALE, SPREAD, SPREAD),
+        functools.partial(filter_kernel, final),
+        out_shape=(pltpu.HBM((LOCAL, G, PLANE), F32) if final else RAW_HBM, SCALE, SPREAD, SPREAD),
         in_specs=[HBM_SPEC] * 2 + [VMEM_SPEC] * 3,
         out_specs=(HBM_SPEC,) + (VMEM_SPEC,) * 3,
         scratch_shapes=[
@@ -356,25 +347,12 @@
             HALVES,
             HALVES,
             pltpu.VMEM((LOCAL, 128), F32),
-            pltpu.SemaphoreType.DMA((2 * LOADS,)),
+            pltpu.SemaphoreType.DMA((FB * LOCAL,)),
         ],
-        name="filter",
+        name="filter_last" if final else "filter_first",
         cost_estimate=pl.CostEstimate(flops=8 * 10**9, bytes_accessed=14 * 10**6, transcendentals=0),
         compiler_params=pltpu.CompilerParams(vmem_limit_bytes=BIG),
     )(in_hbm(field), in_hbm(plain), mine, other, mats)
-
-
-def write_call(raw, scale):
-    return pl.pallas_call(
-        write_kernel,
-        out_shape=pltpu.HBM((LOCAL, G, PLANE), F32),
-        in_specs=[HBM_SPEC, VMEM_SPEC],
-        out_specs=HBM_SPEC,
-        scratch_shapes=[pltpu.VMEM(RAW.shape, F32), pltpu.SemaphoreType.DMA((FB * LOCAL + FB,))],
-        name="write",
-        cost_estimate=pl.CostEstimate(flops=10**6, bytes_accessed=11 * 10**6, transcendentals=0),
-        compiler_params=pltpu.CompilerParams(vmem_limit_bytes=BIG),
-    )(in_hbm(raw), scale)
 
 
 def entry(blocks_ref, group, e):
@@ -501,8 +479,9 @@
     return lax.ppermute(value, "orb", [(i, i ^ 1) for i in range(2 * SLOTS)])
 
 
-def plane_exchange(value):
-    groups = [[2 * i + c for i in range(SLOTS)] for c in range(2)]
+def plane_exchange(value, backward=False):
+    order = range(SLOTS - 1, -1, -1) if backward else range(SLOTS)
+    groups = [[2 * i + c for i in order] for c in range(2)]
     return lax.all_to_all(value, "orb", 0, 0, axis_index_groups=groups, tiled=True)
 
 
@@ -517,22 +496,18 @@
     field, plain = prepare_call(True, (source,), mats)
     near, field = lax.optimization_barrier((near, field))
     statics = frag_all(jnp.stack([core_density, ion_potential]))
-    raw, scale, mine, other = filter_call(field, plain, near, core_swap(near), mats)
+    raw, scale, mine, other = filter_call(False, field, plain, near, core_swap(near), mats)
     cores, ions, own_core, own_ion = select_call(blocks, statics)
 
-    density = plane_exchange(mine + core_swap(other))
+    density = plane_exchange(mine + core_swap(other), backward=True)
     densities = frag_all(jnp.sum(density, axis=0))
     spread = update_call(False, blocks, frag_signs, cores, ions, densities)
     spread, raw = lax.optimization_barrier((spread, raw))
     near = plane_exchange(spread)
     field, plain = prepare_call(False, (raw, scale), mats)
     near, field = lax.optimization_barrier((near, field))
-    raw, scale, mine, other = filter_call(field, plain, near, core_swap(near), mats)
-
-    density, raw = lax.optimization_barrier((mine + core_swap(other), raw))
-    density = plane_exchange(density)
-    filtered = write_call(raw, scale)
-    density, filtered = lax.optimization_barrier((density, filtered))
+    filtered, _, mine, other = filter_call(True, field, plain, near, core_swap(near), mats)
+    density = plane_exchange(mine + core_swap(other), backward=True)
     densities = frag_all(jnp.sum(density, axis=0))
     new_potential = update_call(True, blocks, frag_signs, own_core, own_ion, densities)
     return (filtered.reshape(orbitals.shape), new_potential)

time: 126 us -> 124 us (0.984)
  blocking collectives: 0 us -> 13.4 us
  waiting for transfers between devices: 35.9 us -> 25.5 us
  Pallas kernels: 45.7 us -> 42 us
    all_to_all x0 -> x1, blocking collectives: none -> 13.4 us  [plane_exchange(): lax.all_to_all(value, 'orb', 0, 0, axis_index_groups=groups, tiled=True)]
    all_to_all x4 -> x3, waiting for transfers between devices: 19.2 us -> 8.83 us  [plane_exchange(): lax.all_to_all(value, 'orb', 0, 0, axis_index_groups=groups, tiled=True)]
    pallas_call x3 -> x2, Pallas kernels: 27.9 us -> 24.3 us  [filter_call(): pl.pallas_call(functools.partial(filter_kernel, final), out_shape=(pltpu....]
    all_to_all x4 -> x3, starting transfers between devices: 20.2 us -> 20.1 us  [plane_exchange(): lax.all_to_all(value, 'orb', 0, 0, axis_index_groups=groups, tiled=True)]
  transfers between devices with their start and end apart: 20 -> 19, of which waited for: 15 -> 14; matrix products, arithmetic and copies ran while one was open for 0% -> 0% of each run, Pallas kernels for 14% -> 11%
where the time goes in v3:
time: 124 us
  Pallas kernels  42 us (34%)
  starting transfers between devices  39.7 us (32%)
  waiting for transfers between devices  25.5 us (21%)
  blocking collectives  13.4 us (11%)
    pallas_call x2, Pallas kernels, filter_call(): pl.pallas_call(functools.partial(filter_kernel, final), out_shape=(pltpu....  24.3 us
    all_to_all x3, starting transfers between devices, plane_exchange(): lax.all_to_all(value, 'orb', 0, 0, axis_index_groups=groups, tiled=True)  20.1 us
    ppermute x12, starting transfers between devices, frag_all(): lax.ppermute(value, 'frag', [(g, (g + s) % N_FRAG) for g in range(N_FRAG)])  19.2 us
    all_to_all x1, blocking collectives, plane_exchange(): lax.all_to_all(value, 'orb', 0, 0, axis_index_groups=groups, tiled=True)  13.4 us
    pallas_call x2, Pallas kernels, prepare_call(): pl.pallas_call(functools.partial(prepare_kernel, first), out_shape=(RAW_H...  12.3 us
    ppermute x12, waiting for transfers between devices, frag_all(): lax.ppermute(value, 'frag', [(g, (g + s) % N_FRAG) for g in range(N_FRAG)])  9.67 us
    all_to_all x3, waiting for transfers between devices, plane_exchange(): lax.all_to_all(value, 'orb', 0, 0, axis_index_groups=groups, tiled=True)  8.83 us
    ppermute x4, waiting for transfers between devices, core_swap(): return lax.ppermute(value, 'orb', [(i, i ^ 1) for i in range(2 * SLOTS)])  6.98 us
  transfers between devices with their start and end apart: 19, of which 14 were waited for; matrix products, arithmetic and copies ran while one was open for 0% of the time, Pallas kernels for 11%

profile of v3, /device:TPU:0, one launch (start us, length us, event | category | flops | bytes accessed | tf_op | source)
XLA Modules:
  0.0 123.5 jit_solution(5097215878278171214)
XLA Ops:
  0.6 1.8 %collective-permute-start.3 = (f32[6,1152]{1,0:T(8,128)}, f32[6,1152]{1,0:T(8,128)S(1)}, u32[]{:S(2)}, u32[]{:S(2)}) collective-permute-start(f32[6,1152]{1,0:T(8,128)} %p0_hbm.1), channel_id=1, source_target_pairs={{0,32},{32,64},{64,96},{96,0},{1,33},{33,65},{65,97},{97,1},{2,34}... | collective-permute-start | bytes 82952 | tf_op jit(solution)/shard_map/ppermute | solution.py:474
  2.4 2.9 %collective-permute-start.4 = (f32[6,1152]{1,0:T(8,128)}, f32[6,1152]{1,0:T(8,128)S(1)}, u32[]{:S(2)}, u32[]{:S(2)}) collective-permute-start(f32[6,1152]{1,0:T(8,128)} %p0_hbm.1), channel_id=1, source_target_pairs={{0,64},{32,96},{64,0},{96,32},{1,65},{33,97},{65,1},{97,33},{2,66}... | collective-permute-start | bytes 82952 | tf_op jit(solution)/shard_map/ppermute | solution.py:474
  9.5 1.7 %place.1 = f32[16,56,128]{2,1,0:T(8,128)} custom-call(s32[3,8]{1,0:T(4,128)} %bitcast.5, f32[6,1152]{1,0:T(8,128)} %p0_hbm.1, f32[6,1152]{1,0:T(8,128)S(1)} %collective-permute-done.3.p1, f32[6,1152]{1,0:T(8,128)S(1)} %collective-permute-done.4.p2, f32[6,1152]{1,0:T(8,128)S(1)} %collective-permute-done.5.p3), custom_call_target="tpu_custom_call" | custom-call | tf_op jit(solution)/shard_map/place/pallas_call | solution.py:417
  11.1 7.9 %all-to-all-start = ((f32[16,56,128]{2,1,0:T(8,128)}), f32[16,56,128]{2,1,0:T(8,128)S(1)}, u32[]{:S(2)}, u32[]{:S(2)}) async-start(f32[16,56,128]{2,1,0:T(8,128)} %place.1), calls=%async_computation | async-start | bytes 917504 | tf_op jit(solution)/shard_map/all_to_all | solution.py:485
  20.2 5.4 %prepare_first.1 = (f32[48,8,2304]{2,1,0:T(8,128)}, f32[48,8,2304]{2,1,0:T(8,128)}) custom-call(f32[8,48,2304]{2,1,0:T(8,128)} %bitcast.11, bf16[3,2,512,128]{3,2,1,0:T(8,128)(2,1)S(1)} %copy-done.2), custom_call_target="tpu_custom_call" | custom-call | flops 2000000000 | bytes 11000000 | tf_op jit(solution)/shard_map/prepare_first/pallas_call | solution.py:324
  25.6 3.2 %all-to-all-done.mine_ref = f32[16,56,128]{2,1,0:T(8,128)S(1)} async-done(((f32[16,56,128]{2,1,0:T(8,128)}), f32[16,56,128]{2,1,0:T(8,128)S(1)}, u32[]{:S(2)}, u32[]{:S(2)}) %all-to-all-start) | async-done | bytes 458784 | tf_op jit(solution)/shard_map/all_to_all | solution.py:485
  28.8 1.8 %collective-permute-done.6.other_ref = f32[16,56,128]{2,1,0:T(8,128)S(1)} collective-permute-done((f32[16,56,128]{2,1,0:T(8,128)S(1)}, f32[16,56,128]{2,1,0:T(8,128)S(1)}, u32[]{:S(2)}, u32[]{:S(2)}) %collective-permute-start.6) | collective-permute-done | bytes 458784 | tf_op jit(solution)/shard_map/ppermute | solution.py:479
  30.6 11.7 %filter_first.1 = (f32[48,8,2304]{2,1,0:T(8,128)}, f32[8,128]{1,0:T(8,128)S(1)}, f32[16,56,128]{2,1,0:T(8,128)S(1)}, f32[16,56,128]{2,1,0:T(8,128)S(1)}) custom-call(f32[48,8,2304]{2,1,0:T(8,128)} %get-tuple-element.30.field_hbm, f32[48,8,2304]{2,1,0:T(8,128)} %get-tuple-element.31.plain_hbm, f32[16,56,128]{2,1,0:T(8,128)S(1)} %all-to-all-done.mine_ref, ...), custom_call_target="tpu_custom_call" | custom-call | flops 8000000000 | bytes 14000000 | tf_op jit(solution)/shard_map/filter_first/pallas_call | solution.py:338
  42.5 1.7 %collective-permute-done.7 = f32[16,56,128]{2,1,0:T(8,128)S(1)} collective-permute-done((f32[16,56,128]{2,1,0:T(8,128)S(1)}, f32[16,56,128]{2,1,0:T(8,128)S(1)}, u32[]{:S(2)}, u32[]{:S(2)}) %collective-permute-start.7) | collective-permute-done | bytes 458784 | tf_op jit(solution)/shard_map/ppermute | solution.py:479
  45.0 6.6 %all-to-all-start.1 = ((f32[16,56,128]{2,1,0:T(8,128)}), f32[16,56,128]{2,1,0:T(8,128)S(1)}, u32[]{:S(2)}, u32[]{:S(2)}) async-start(f32[16,56,128]{2,1,0:T(8,128)} %add.6), calls=%async_computation.1 | async-start | bytes 917504 | tf_op jit(solution)/shard_map/all_to_all | solution.py:485
  51.9 3.8 %collective-permute-start.1 = (f32[2,6,1152]{2,1,0:T(8,128)S(1)}, f32[2,6,1152]{2,1,0:T(8,128)S(1)}, u32[]{:S(2)}, u32[]{:S(2)}) collective-permute-start(f32[2,6,1152]{2,1,0:T(8,128)S(1)} %pad_maximum_fusion.refs_0_), channel_id=1, source_target_pairs={{0,64},{32,96},{64,0},{96,32},{1,65},{33,97},{65,1},{97,33},{2,66}... | collective-permute-start | bytes 165896 | tf_op jit(solution)/shard_map/ppermute | solution.py:474
  55.9 2.8 %all-to-all-done.1 = f32[16,56,128]{2,1,0:T(8,128)S(1)} async-done(((f32[16,56,128]{2,1,0:T(8,128)}), f32[16,56,128]{2,1,0:T(8,128)S(1)}, u32[]{:S(2)}, u32[]{:S(2)}) %all-to-all-start.1) | async-done | bytes 458784 | tf_op jit(solution)/shard_map/all_to_all | solution.py:485
  58.7 2.6 %collective-permute-start.10 = (f32[56,128]{1,0:T(8,128)S(1)}, f32[56,128]{1,0:T(8,128)S(1)}, u32[]{:S(2)}, u32[]{:S(2)}) collective-permute-start(f32[56,128]{1,0:T(8,128)S(1)} %reduce_sum.18.d0), channel_id=1, source_target_pairs={{0,96},{32,0},{64,32},{96,64},{1,97},{33,1},{65,33},{97,65},{2,98}... | collective-permute-start | bytes 86024 | tf_op jit(solution)/shard_map/ppermute | solution.py:474
  63.7 2.7 %collective-permute-done.8.d1 = f32[56,128]{1,0:T(8,128)S(1)} collective-permute-done((f32[56,128]{1,0:T(8,128)S(1)}, f32[56,128]{1,0:T(8,128)S(1)}, u32[]{:S(2)}, u32[]{:S(2)}) %collective-permute-start.8) | collective-permute-done | bytes 28704 | tf_op jit(solution)/shard_map/ppermute | solution.py:474
  68.3 5.6 %all-to-all-start.2 = ((f32[16,56,128]{2,1,0:T(8,128)}), f32[16,56,128]{2,1,0:T(8,128)S(1)}, u32[]{:S(2)}, u32[]{:S(2)}) async-start(f32[16,56,128]{2,1,0:T(8,128)} %update_first.1), calls=%async_computation.2 | async-start | bytes 917504 | tf_op jit(solution)/shard_map/all_to_all | solution.py:485
  73.9 6.8 %prepare_next.1 = (f32[48,8,2304]{2,1,0:T(8,128)}, f32[48,8,2304]{2,1,0:T(8,128)}) custom-call(f32[48,8,2304]{2,1,0:T(8,128)} %get-tuple-element.37.source, f32[8,128]{1,0:T(8,128)S(1)} %get-tuple-element.38.refs_0_, bf16[3,2,512,128]{3,2,1,0:T(8,128)(2,1)S(1)} %copy-done.3), custom_call_target="tpu_custom_call" | custom-call | flops 2000000000 | bytes 11000000 | tf_op jit(solution)/shard_map/prepare_next/pallas_call | solution.py:324
  80.7 2.9 %all-to-all-done.2.mine_ref = f32[16,56,128]{2,1,0:T(8,128)S(1)} async-done(((f32[16,56,128]{2,1,0:T(8,128)}), f32[16,56,128]{2,1,0:T(8,128)S(1)}, u32[]{:S(2)}, u32[]{:S(2)}) %all-to-all-start.2) | async-done | bytes 458784 | tf_op jit(solution)/shard_map/all_to_all | solution.py:485
  83.6 1.8 %collective-permute-done.11.other_ref = f32[16,56,128]{2,1,0:T(8,128)S(1)} collective-permute-done((f32[16,56,128]{2,1,0:T(8,128)S(1)}, f32[16,56,128]{2,1,0:T(8,128)S(1)}, u32[]{:S(2)}, u32[]{:S(2)}) %collective-permute-start.11) | collective-permute-done | bytes 458784 | tf_op jit(solution)/shard_map/ppermute | solution.py:479
  85.4 12.6 %filter_last.1 = (f32[8,48,2304]{2,1,0:T(8,128)}, f32[8,128]{1,0:T(8,128)}, f32[16,56,128]{2,1,0:T(8,128)S(1)}, f32[16,56,128]{2,1,0:T(8,128)S(1)}) custom-call(f32[48,8,2304]{2,1,0:T(8,128)} %get-tuple-element.40.field_hbm, f32[48,8,2304]{2,1,0:T(8,128)} %get-tuple-element.41.plain_hbm, f32[16,56,128]{2,1,0:T(8,128)S(1)} %all-to-all-done.2.mine_ref, ...), custom_call_target="tpu_custom_call" | custom-call | flops 8000000000 | bytes 14000000 | tf_op jit(solution)/shard_map/filter_last/pallas_call | solution.py:338
  98.2 1.7 %collective-permute-done.12 = f32[16,56,128]{2,1,0:T(8,128)S(1)} collective-permute-done((f32[16,56,128]{2,1,0:T(8,128)S(1)}, f32[16,56,128]{2,1,0:T(8,128)S(1)}, u32[]{:S(2)}, u32[]{:S(2)}) %collective-permute-start.12) | collective-permute-done | bytes 458784 | tf_op jit(solution)/shard_map/ppermute | solution.py:479
  100.0 13.4 %all_to_all.20 = f32[16,56,128]{2,1,0:T(8,128)S(1)} all-to-all(f32[16,56,128]{2,1,0:T(8,128)S(1)} %add.7), channel_id=1, replica_groups={{30,28,26,24,22,20,18,16,14,12,10,8,6,4,2,0},{31,29,27,25,23,21,19,17,1..., dimensions={0} | all-to-all | bytes 917504 | tf_op jit(solution)/shard_map/all_to_all | solution.py:485
  114.1 4.1 %collective-permute-start.14 = (f32[56,128]{1,0:T(8,128)S(1)}, f32[56,128]{1,0:T(8,128)S(1)}, u32[]{:S(2)}, u32[]{:S(2)}) collective-permute-start(f32[56,128]{1,0:T(8,128)S(1)} %reduce_sum.19.d0), channel_id=1, source_target_pairs={{0,64},{32,96},{64,0},{96,32},{1,65},{33,97},{65,1},{97,33},{2,66}... | collective-permute-start | bytes 86024 | tf_op jit(solution)/shard_map/ppermute | solution.py:474
  118.7 1.7 %collective-permute-done.14.d2 = f32[56,128]{1,0:T(8,128)S(1)} collective-permute-done((f32[56,128]{1,0:T(8,128)S(1)}, f32[56,128]{1,0:T(8,128)S(1)}, u32[]{:S(2)}, u32[]{:S(2)}) %collective-permute-start.14) | collective-permute-done | bytes 28704 | tf_op jit(solution)/shard_map/ppermute | solution.py:474
  120.4 1.7 %collective-permute-done.15.d3 = f32[56,128]{1,0:T(8,128)S(1)} collective-permute-done((f32[56,128]{1,0:T(8,128)S(1)}, f32[56,128]{1,0:T(8,128)S(1)}, u32[]{:S(2)}, u32[]{:S(2)}) %collective-permute-start.15) | collective-permute-done | bytes 28704 | tf_op jit(solution)/shard_map/ppermute | solution.py:474
  (40 shorter events, 13.9 us)
Async XLA Ops:
  0.6 6.0 %collective-permute-start.3 = (f32[6,1152]{1,0:T(8,128)}, f32[6,1152]{1,0:T(8,128)S(1)}, u32[]{:S(2)}, u32[]{:S(2)}) collective-permute-start(f32[6,1152]{1,0:T(8,128)} %p0_hbm.1), channel_id=1, source_target_pairs={{0,32},{32,64},{64,96},{96,0},{1,33},{33,65},{65,97},{97,1},{2,34}... | collective-permute-start | bytes 82952 | tf_op jit(solution)/shard_map/ppermute | solution.py:474
  2.4 5.7 %collective-permute-start.4 = (f32[6,1152]{1,0:T(8,128)}, f32[6,1152]{1,0:T(8,128)S(1)}, u32[]{:S(2)}, u32[]{:S(2)}) collective-permute-start(f32[6,1152]{1,0:T(8,128)} %p0_hbm.1), channel_id=1, source_target_pairs={{0,64},{32,96},{64,0},{96,32},{1,65},{33,97},{65,1},{97,33},{2,66}... | collective-permute-start | bytes 82952 | tf_op jit(solution)/shard_map/ppermute | solution.py:474
  5.3 4.2 %collective-permute-start.5 = (f32[6,1152]{1,0:T(8,128)}, f32[6,1152]{1,0:T(8,128)S(1)}, u32[]{:S(2)}, u32[]{:S(2)}) collective-permute-start(f32[6,1152]{1,0:T(8,128)} %p0_hbm.1), channel_id=1, source_target_pairs={{0,96},{32,0},{64,32},{96,64},{1,97},{33,1},{65,33},{97,65},{2,98}... | collective-permute-start | bytes 82952 | tf_op jit(solution)/shard_map/ppermute | solution.py:474
  11.1 17.6 %all-to-all-start = ((f32[16,56,128]{2,1,0:T(8,128)}), f32[16,56,128]{2,1,0:T(8,128)S(1)}, u32[]{:S(2)}, u32[]{:S(2)}) async-start(f32[16,56,128]{2,1,0:T(8,128)} %place.1), calls=%async_computation | async-start | bytes 917504 | tf_op jit(solution)/shard_map/all_to_all | solution.py:485
  20.2 10.4 %copy-start.3 = (bf16[3,2,512,128]{3,2,1,0:T(8,128)(2,1)S(1)}, bf16[3,2,512,128]{3,2,1,0:T(8,128)(2,1)}, u32[]{:S(2)}) copy-start(bf16[3,2,512,128]{3,2,1,0:T(8,128)(2,1)} %constant.4.clone.refs_0_.mats_ref.refs_1_) | copy-start | bytes 2359300
  28.8 1.8 %collective-permute-start.6 = (f32[16,56,128]{2,1,0:T(8,128)S(1)}, f32[16,56,128]{2,1,0:T(8,128)S(1)}, u32[]{:S(2)}, u32[]{:S(2)}) collective-permute-start(f32[16,56,128]{2,1,0:T(8,128)S(1)} %all-to-all-done.mine_ref), channel_id=1, source_target_pairs={{0,1},{1,0},{2,3},{3,2},{4,5},{5,4},{6,7},{7,6},{8,9},{9,8},{10,11... | collective-permute-start | bytes 1376264 | tf_op jit(solution)/shard_map/ppermute | solution.py:479
  30.6 21.0 %copy-start.4 = (f32[6,1152]{1,0:T(8,128)S(1)}, f32[6,1152]{1,0:T(8,128)}, u32[]{:S(2)}) copy-start(f32[6,1152]{1,0:T(8,128)} %param.9) | copy-start | bytes 82948
  30.6 21.0 %copy-start.5 = (f32[6,1152]{1,0:T(8,128)S(1)}, f32[6,1152]{1,0:T(8,128)}, u32[]{:S(2)}) copy-start(f32[6,1152]{1,0:T(8,128)} %param.10) | copy-start | bytes 82948
  30.6 32.3 %copy-start = (s32[8,3]{0,1:T(4,128)S(1)}, s32[8,3]{0,1:T(4,128)}, u32[]{:S(2)}) copy-start(s32[8,3]{0,1:T(4,128)} %param.11) | copy-start | bytes 292
  30.6 36.1 %copy-start.1 = (s32[8]{0:T(128)S(1)}, s32[8]{0:T(128)}, u32[]{:S(2)}) copy-start(s32[8]{0:T(128)} %signs_ref.3) | copy-start | bytes 100
  42.3 1.9 %collective-permute-start.7 = (f32[16,56,128]{2,1,0:T(8,128)S(1)}, f32[16,56,128]{2,1,0:T(8,128)S(1)}, u32[]{:S(2)}, u32[]{:S(2)}) collective-permute-start(f32[16,56,128]{2,1,0:T(8,128)S(1)} %get-tuple-element.34), channel_id=1, source_target_pairs={{0,1},{1,0},{2,3},{3,2},{4,5},{5,4},{6,7},{7,6},{8,9},{9,8},{10,11... | collective-permute-start | bytes 1376264 | tf_op jit(solution)/shard_map/ppermute | solution.py:479
  45.0 13.6 %all-to-all-start.1 = ((f32[16,56,128]{2,1,0:T(8,128)}), f32[16,56,128]{2,1,0:T(8,128)S(1)}, u32[]{:S(2)}, u32[]{:S(2)}) async-start(f32[16,56,128]{2,1,0:T(8,128)} %add.6), calls=%async_computation.1 | async-start | bytes 917504 | tf_op jit(solution)/shard_map/all_to_all | solution.py:485
  51.7 9.6 %collective-permute-start = (f32[2,6,1152]{2,1,0:T(8,128)S(1)}, f32[2,6,1152]{2,1,0:T(8,128)S(1)}, u32[]{:S(2)}, u32[]{:S(2)}) collective-permute-start(f32[2,6,1152]{2,1,0:T(8,128)S(1)} %pad_maximum_fusion.refs_0_), channel_id=1, source_target_pairs={{0,32},{32,64},{64,96},{96,0},{1,33},{33,65},{65,97},{97,1},{2,34}... | collective-permute-start | bytes 165896 | tf_op jit(solution)/shard_map/ppermute | solution.py:474
  51.9 10.9 %collective-permute-start.1 = (f32[2,6,1152]{2,1,0:T(8,128)S(1)}, f32[2,6,1152]{2,1,0:T(8,128)S(1)}, u32[]{:S(2)}, u32[]{:S(2)}) collective-permute-start(f32[2,6,1152]{2,1,0:T(8,128)S(1)} %pad_maximum_fusion.refs_0_), channel_id=1, source_target_pairs={{0,64},{32,96},{64,0},{96,32},{1,65},{33,97},{65,1},{97,33},{2,66}... | collective-permute-start | bytes 165896 | tf_op jit(solution)/shard_map/ppermute | solution.py:474
  55.7 7.1 %collective-permute-start.2 = (f32[2,6,1152]{2,1,0:T(8,128)S(1)}, f32[2,6,1152]{2,1,0:T(8,128)S(1)}, u32[]{:S(2)}, u32[]{:S(2)}) collective-permute-start(f32[2,6,1152]{2,1,0:T(8,128)S(1)} %pad_maximum_fusion.refs_0_), channel_id=1, source_target_pairs={{0,96},{32,0},{64,32},{96,64},{1,97},{33,1},{65,33},{97,65},{2,98}... | collective-permute-start | bytes 165896 | tf_op jit(solution)/shard_map/ppermute | solution.py:474
  58.7 5.0 %collective-permute-start.10 = (f32[56,128]{1,0:T(8,128)S(1)}, f32[56,128]{1,0:T(8,128)S(1)}, u32[]{:S(2)}, u32[]{:S(2)}) collective-permute-start(f32[56,128]{1,0:T(8,128)S(1)} %reduce_sum.18.d0), channel_id=1, source_target_pairs={{0,96},{32,0},{64,32},{96,64},{1,97},{33,1},{65,33},{97,65},{2,98}... | collective-permute-start | bytes 86024 | tf_op jit(solution)/shard_map/ppermute | solution.py:474
  61.3 5.1 %collective-permute-start.8 = (f32[56,128]{1,0:T(8,128)S(1)}, f32[56,128]{1,0:T(8,128)S(1)}, u32[]{:S(2)}, u32[]{:S(2)}) collective-permute-start(f32[56,128]{1,0:T(8,128)S(1)} %reduce_sum.18.d0), channel_id=1, source_target_pairs={{0,32},{32,64},{64,96},{96,0},{1,33},{33,65},{65,97},{97,1},{2,34}... | collective-permute-start | bytes 86024 | tf_op jit(solution)/shard_map/ppermute | solution.py:474
  61.3 5.4 %collective-permute-start.9 = (f32[56,128]{1,0:T(8,128)S(1)}, f32[56,128]{1,0:T(8,128)S(1)}, u32[]{:S(2)}, u32[]{:S(2)}) collective-permute-start(f32[56,128]{1,0:T(8,128)S(1)} %reduce_sum.18.d0), channel_id=1, source_target_pairs={{0,64},{32,96},{64,0},{96,32},{1,65},{33,97},{65,1},{97,33},{2,66}... | collective-permute-start | bytes 86024 | tf_op jit(solution)/shard_map/ppermute | solution.py:474
  68.3 15.3 %all-to-all-start.2 = ((f32[16,56,128]{2,1,0:T(8,128)}), f32[16,56,128]{2,1,0:T(8,128)S(1)}, u32[]{:S(2)}, u32[]{:S(2)}) async-start(f32[16,56,128]{2,1,0:T(8,128)} %update_first.1), calls=%async_computation.2 | async-start | bytes 917504 | tf_op jit(solution)/shard_map/all_to_all | solution.py:485
  83.6 1.8 %collective-permute-start.11 = (f32[16,56,128]{2,1,0:T(8,128)S(1)}, f32[16,56,128]{2,1,0:T(8,128)S(1)}, u32[]{:S(2)}, u32[]{:S(2)}) collective-permute-start(f32[16,56,128]{2,1,0:T(8,128)S(1)} %all-to-all-done.2.mine_ref), channel_id=1, source_target_pairs={{0,1},{1,0},{2,3},{3,2},{4,5},{5,4},{6,7},{7,6},{8,9},{9,8},{10,11... | collective-permute-start | bytes 1376264 | tf_op jit(solution)/shard_map/ppermute | solution.py:479
  98.0 1.9 %collective-permute-start.12 = (f32[16,56,128]{2,1,0:T(8,128)S(1)}, f32[16,56,128]{2,1,0:T(8,128)S(1)}, u32[]{:S(2)}, u32[]{:S(2)}) collective-permute-start(f32[16,56,128]{2,1,0:T(8,128)S(1)} %get-tuple-element.47), channel_id=1, source_target_pairs={{0,1},{1,0},{2,3},{3,2},{4,5},{5,4},{6,7},{7,6},{8,9},{9,8},{10,11... | collective-permute-start | bytes 1376264 | tf_op jit(solution)/shard_map/ppermute | solution.py:479
  113.5 5.2 %collective-permute-start.13 = (f32[56,128]{1,0:T(8,128)S(1)}, f32[56,128]{1,0:T(8,128)S(1)}, u32[]{:S(2)}, u32[]{:S(2)}) collective-permute-start(f32[56,128]{1,0:T(8,128)S(1)} %reduce_sum.19.d0), channel_id=1, source_target_pairs={{0,32},{32,64},{64,96},{96,0},{1,33},{33,65},{65,97},{97,1},{2,34}... | collective-permute-start | bytes 86024 | tf_op jit(solution)/shard_map/ppermute | solution.py:474
  114.1 6.3 %collective-permute-start.14 = (f32[56,128]{1,0:T(8,128)S(1)}, f32[56,128]{1,0:T(8,128)S(1)}, u32[]{:S(2)}, u32[]{:S(2)}) collective-permute-start(f32[56,128]{1,0:T(8,128)S(1)} %reduce_sum.19.d0), channel_id=1, source_target_pairs={{0,64},{32,96},{64,0},{96,32},{1,65},{33,97},{65,1},{97,33},{2,66}... | collective-permute-start | bytes 86024 | tf_op jit(solution)/shard_map/ppermute | solution.py:474
  118.2 3.9 %collective-permute-start.15 = (f32[56,128]{1,0:T(8,128)S(1)}, f32[56,128]{1,0:T(8,128)S(1)}, u32[]{:S(2)}, u32[]{:S(2)}) collective-permute-start(f32[56,128]{1,0:T(8,128)S(1)} %reduce_sum.19.d0), channel_id=1, source_target_pairs={{0,96},{32,0},{64,32},{96,64},{1,97},{33,1},{65,33},{97,65},{2,98}... | collective-permute-start | bytes 86024 | tf_op jit(solution)/shard_map/ppermute | solution.py:474
  (1 other events, 1.1 us)

commit v4 on v3

--- a/solution.py
+++ b/solution.py
@@ -229,12 +229,13 @@
     upper = lax.broadcasted_iota(jnp.int32, (LOCAL, 128), 0) >= LOCAL // 2
 
     def build(row, carry):
+        slot = SLOTS - 1 - row if final else row
         for ref, half in ((mine_ref, core), (other_ref, 1 - core)):
             for b in range(FB):
                 tiles = []
                 for q in range(ROWS):
-                    v0 = ref[row, pl.ds(b * ROWS + q, 1), :]
-                    v1 = ref[row, pl.ds((FB + b) * ROWS + q, 1), :]
+                    v0 = ref[slot, pl.ds(b * ROWS + q, 1), :]
+                    v1 = ref[slot, pl.ds((FB + b) * ROWS + q, 1), :]
                     v = jnp.where(upper, jnp.broadcast_to(v1, (LOCAL, 128)), jnp.broadcast_to(v0, (LOCAL, 128)))
                     tiles.append(v * 0.125 - 0.375)
                 wf[16 * b + row, :, cols(half * CELLS, CELLS)] = jnp.concatenate(tiles, axis=1)
@@ -275,6 +276,7 @@
     scale_ref[...] = jnp.broadcast_to(inverse, (LOCAL, 128))
 
     def finish(b, row, scale):
+        slot = row if final else SLOTS - 1 - row
         for ref, half in ((dmine_ref, core), (dother_ref, 1 - core)):
             lane = cols(half * CELLS, CELLS)
             value = ya[2 + 16 * b + row, :, lane] * scale
@@ -284,10 +286,10 @@
             value = value + pltpu.roll(value, 1, 0)
             value = value + pltpu.roll(value, 2, 0)
             for q in range(ROWS):
-                ref[SLOTS - 1 - row, pl.ds(b * ROWS + q, 1), :] = value[3:4, 128 * q : 128 * q + 128]
-                ref[SLOTS - 1 - row, pl.ds((FB + b) * ROWS + q, 1), :] = value[7:8, 128 * q : 128 * q + 128]
+                ref[slot, pl.ds(b * ROWS + q, 1), :] = value[3:4, 128 * q : 128 * q + 128]
+                ref[slot, pl.ds((FB + b) * ROWS + q, 1), :] = value[7:8, 128 * q : 128 * q + 128]
             if b == 0:
-                ref[SLOTS - 1 - row, pl.ds(PIECE, 2), :] = jnp.zeros((2, 128), F32)
+                ref[slot, pl.ds(PIECE, 2), :] = jnp.zeros((2, 128), F32)
         return scale
 
     scale = jnp.broadcast_to(inverse, (LOCAL, CELLS))
@@ -503,11 +505,11 @@
     densities = frag_all(jnp.sum(density, axis=0))
     spread = update_call(False, blocks, frag_signs, cores, ions, densities)
     spread, raw = lax.optimization_barrier((spread, raw))
-    near = plane_exchange(spread)
+    near = plane_exchange(spread, backward=True)
     field, plain = prepare_call(False, (raw, scale), mats)
     near, field = lax.optimization_barrier((near, field))
     filtered, _, mine, other = filter_call(True, field, plain, near, core_swap(near), mats)
-    density = plane_exchange(mine + core_swap(other), backward=True)
+    density = plane_exchange(mine + core_swap(other))
     densities = frag_all(jnp.sum(density, axis=0))
     new_potential = update_call(True, blocks, frag_signs, own_core, own_ion, densities)
     return (filtered.reshape(orbitals.shape), new_potential)

time: 124 us -> 125 us (level)
  waiting for transfers between devices: 25.5 us -> 22.6 us
  starting transfers between devices: 39.7 us -> 41.8 us
  blocking collectives: 13.4 us -> 15.2 us
    all_to_all x3, waiting for transfers between devices: 8.83 us -> 5.92 us  [plane_exchange(): lax.all_to_all(value, 'orb', 0, 0, axis_index_groups=groups, tiled=True)]
    all_to_all x3, starting transfers between devices: 20.1 us -> 22.2 us  [plane_exchange(): lax.all_to_all(value, 'orb', 0, 0, axis_index_groups=groups, tiled=True)]
    all_to_all x1, blocking collectives: 13.4 us -> 15.2 us  [plane_exchange(): lax.all_to_all(value, 'orb', 0, 0, axis_index_groups=groups, tiled=True)]
  transfers between devices with their start and end apart: 19 -> 19, of which waited for: 14 -> 13; matrix products, arithmetic and copies ran while one was open for 0% -> 0% of each run, Pallas kernels for 11% -> 11%
where the time goes in v4:
time: 125 us
  Pallas kernels  42.1 us (34%)
  starting transfers between devices  41.8 us (33%)
  waiting for transfers between devices  22.6 us (18%)
  blocking collectives  15.2 us (12%)
    pallas_call x2, Pallas kernels, filter_call(): pl.pallas_call(functools.partial(filter_kernel, final), out_shape=(pltpu....  24.3 us
    all_to_all x3, starting transfers between devices, plane_exchange(): lax.all_to_all(value, 'orb', 0, 0, axis_index_groups=groups, tiled=True)  22.2 us
    ppermute x12, starting transfers between devices, frag_all(): lax.ppermute(value, 'frag', [(g, (g + s) % N_FRAG) for g in range(N_FRAG)])  19.2 us
    all_to_all x1, blocking collectives, plane_exchange(): lax.all_to_all(value, 'orb', 0, 0, axis_index_groups=groups, tiled=True)  15.2 us
    pallas_call x2, Pallas kernels, prepare_call(): pl.pallas_call(functools.partial(prepare_kernel, first), out_shape=(RAW_H...  12.2 us
    ppermute x12, waiting for transfers between devices, frag_all(): lax.ppermute(value, 'frag', [(g, (g + s) % N_FRAG) for g in range(N_FRAG)])  9.67 us
    ppermute x4, waiting for transfers between devices, core_swap(): return lax.ppermute(value, 'orb', [(i, i ^ 1) for i in range(2 * SLOTS)])  6.97 us
    all_to_all x3, waiting for transfers between devices, plane_exchange(): lax.all_to_all(value, 'orb', 0, 0, axis_index_groups=groups, tiled=True)  5.92 us
  transfers between devices with their start and end apart: 19, of which 13 were waited for; matrix products, arithmetic and copies ran while one was open for 0% of the time, Pallas kernels for 11%

profile of v4, /device:TPU:0, one launch (start us, length us, event | category | flops | bytes accessed | tf_op | source)
XLA Modules:
  0.0 124.5 jit_solution(6993757403560648508)
XLA Ops:
  0.6 1.8 %collective-permute-start.3 = (f32[6,1152]{1,0:T(8,128)}, f32[6,1152]{1,0:T(8,128)S(1)}, u32[]{:S(2)}, u32[]{:S(2)}) collective-permute-start(f32[6,1152]{1,0:T(8,128)} %p0_hbm.1), channel_id=1, source_target_pairs={{0,32},{32,64},{64,96},{96,0},{1,33},{33,65},{65,97},{97,1},{2,34}... | collective-permute-start | bytes 82952 | tf_op jit(solution)/shard_map/ppermute | solution.py:476
  2.4 2.9 %collective-permute-start.4 = (f32[6,1152]{1,0:T(8,128)}, f32[6,1152]{1,0:T(8,128)S(1)}, u32[]{:S(2)}, u32[]{:S(2)}) collective-permute-start(f32[6,1152]{1,0:T(8,128)} %p0_hbm.1), channel_id=1, source_target_pairs={{0,64},{32,96},{64,0},{96,32},{1,65},{33,97},{65,1},{97,33},{2,66}... | collective-permute-start | bytes 82952 | tf_op jit(solution)/shard_map/ppermute | solution.py:476
  9.5 1.7 %place.1 = f32[16,56,128]{2,1,0:T(8,128)} custom-call(s32[3,8]{1,0:T(4,128)} %bitcast.5, f32[6,1152]{1,0:T(8,128)} %p0_hbm.1, f32[6,1152]{1,0:T(8,128)S(1)} %collective-permute-done.3.p1, f32[6,1152]{1,0:T(8,128)S(1)} %collective-permute-done.4.p2, f32[6,1152]{1,0:T(8,128)S(1)} %collective-permute-done.5.p3), custom_call_target="tpu_custom_call" | custom-call | tf_op jit(solution)/shard_map/place/pallas_call | solution.py:419
  11.1 7.9 %all-to-all-start = ((f32[16,56,128]{2,1,0:T(8,128)}), f32[16,56,128]{2,1,0:T(8,128)S(1)}, u32[]{:S(2)}, u32[]{:S(2)}) async-start(f32[16,56,128]{2,1,0:T(8,128)} %place.1), calls=%async_computation | async-start | bytes 917504 | tf_op jit(solution)/shard_map/all_to_all | solution.py:487
  20.2 5.4 %prepare_first.1 = (f32[48,8,2304]{2,1,0:T(8,128)}, f32[48,8,2304]{2,1,0:T(8,128)}) custom-call(f32[8,48,2304]{2,1,0:T(8,128)} %bitcast.11, bf16[3,2,512,128]{3,2,1,0:T(8,128)(2,1)S(1)} %copy-done.2), custom_call_target="tpu_custom_call" | custom-call | flops 2000000000 | bytes 11000000 | tf_op jit(solution)/shard_map/prepare_first/pallas_call | solution.py:326
  25.6 3.2 %all-to-all-done.mine_ref = f32[16,56,128]{2,1,0:T(8,128)S(1)} async-done(((f32[16,56,128]{2,1,0:T(8,128)}), f32[16,56,128]{2,1,0:T(8,128)S(1)}, u32[]{:S(2)}, u32[]{:S(2)}) %all-to-all-start) | async-done | bytes 458784 | tf_op jit(solution)/shard_map/all_to_all | solution.py:487
  28.8 1.8 %collective-permute-done.6.other_ref = f32[16,56,128]{2,1,0:T(8,128)S(1)} collective-permute-done((f32[16,56,128]{2,1,0:T(8,128)S(1)}, f32[16,56,128]{2,1,0:T(8,128)S(1)}, u32[]{:S(2)}, u32[]{:S(2)}) %collective-permute-start.6) | collective-permute-done | bytes 458784 | tf_op jit(solution)/shard_map/ppermute | solution.py:481
  30.6 11.7 %filter_first.1 = (f32[48,8,2304]{2,1,0:T(8,128)}, f32[8,128]{1,0:T(8,128)S(1)}, f32[16,56,128]{2,1,0:T(8,128)S(1)}, f32[16,56,128]{2,1,0:T(8,128)S(1)}) custom-call(f32[48,8,2304]{2,1,0:T(8,128)} %get-tuple-element.30.field_hbm, f32[48,8,2304]{2,1,0:T(8,128)} %get-tuple-element.31.plain_hbm, f32[16,56,128]{2,1,0:T(8,128)S(1)} %all-to-all-done.mine_ref, ...), custom_call_target="tpu_custom_call" | custom-call | flops 8000000000 | bytes 14000000 | tf_op jit(solution)/shard_map/filter_first/pallas_call | solution.py:340
  42.5 1.7 %collective-permute-done.7 = f32[16,56,128]{2,1,0:T(8,128)S(1)} collective-permute-done((f32[16,56,128]{2,1,0:T(8,128)S(1)}, f32[16,56,128]{2,1,0:T(8,128)S(1)}, u32[]{:S(2)}, u32[]{:S(2)}) %collective-permute-start.7) | collective-permute-done | bytes 458784 | tf_op jit(solution)/shard_map/ppermute | solution.py:481
  45.0 6.6 %all-to-all-start.1 = ((f32[16,56,128]{2,1,0:T(8,128)}), f32[16,56,128]{2,1,0:T(8,128)S(1)}, u32[]{:S(2)}, u32[]{:S(2)}) async-start(f32[16,56,128]{2,1,0:T(8,128)} %add.6), calls=%async_computation.1 | async-start | bytes 917504 | tf_op jit(solution)/shard_map/all_to_all | solution.py:487
  51.9 3.8 %collective-permute-start.1 = (f32[2,6,1152]{2,1,0:T(8,128)S(1)}, f32[2,6,1152]{2,1,0:T(8,128)S(1)}, u32[]{:S(2)}, u32[]{:S(2)}) collective-permute-start(f32[2,6,1152]{2,1,0:T(8,128)S(1)} %pad_maximum_fusion.refs_0_), channel_id=1, source_target_pairs={{0,64},{32,96},{64,0},{96,32},{1,65},{33,97},{65,1},{97,33},{2,66}... | collective-permute-start | bytes 165896 | tf_op jit(solution)/shard_map/ppermute | solution.py:476
  55.9 2.8 %all-to-all-done.1 = f32[16,56,128]{2,1,0:T(8,128)S(1)} async-done(((f32[16,56,128]{2,1,0:T(8,128)}), f32[16,56,128]{2,1,0:T(8,128)S(1)}, u32[]{:S(2)}, u32[]{:S(2)}) %all-to-all-start.1) | async-done | bytes 458784 | tf_op jit(solution)/shard_map/all_to_all | solution.py:487
  58.7 2.6 %collective-permute-start.10 = (f32[56,128]{1,0:T(8,128)S(1)}, f32[56,128]{1,0:T(8,128)S(1)}, u32[]{:S(2)}, u32[]{:S(2)}) collective-permute-start(f32[56,128]{1,0:T(8,128)S(1)} %reduce_sum.18.d0), channel_id=1, source_target_pairs={{0,96},{32,0},{64,32},{96,64},{1,97},{33,1},{65,33},{97,65},{2,98}... | collective-permute-start | bytes 86024 | tf_op jit(solution)/shard_map/ppermute | solution.py:476
  63.7 2.7 %collective-permute-done.8.d1 = f32[56,128]{1,0:T(8,128)S(1)} collective-permute-done((f32[56,128]{1,0:T(8,128)S(1)}, f32[56,128]{1,0:T(8,128)S(1)}, u32[]{:S(2)}, u32[]{:S(2)}) %collective-permute-start.8) | collective-permute-done | bytes 28704 | tf_op jit(solution)/shard_map/ppermute | solution.py:476
  66.7 1.6 %update_first.1 = f32[16,56,128]{2,1,0:T(8,128)} custom-call(s32[3,8]{1,0:T(4,128)S(1)} %bitcast.7, s32[8]{0:T(128)S(1)} %copy-done.1, f32[54,128]{1,0:T(8,128)S(1)} %get-tuple-element.25.core_ref, f32[54,128]{1,0:T(8,128)S(1)} %get-tuple-element.26.ion_ref, f32[56,128]{1,0:T(8,128)S(1)} %reduce_sum.18.d0, f32[56,128]{1,0:T(8,128)S(1)} %collective-permute-done.8.d1, ...), custom_call_target="tpu_custom_call" | custom-call | tf_op jit(solution)/shard_map/update_first/pallas_call | solution.py:464
  68.3 7.6 %all-to-all-start.2 = ((f32[16,56,128]{2,1,0:T(8,128)}), f32[16,56,128]{2,1,0:T(8,128)S(1)}, u32[]{:S(2)}, u32[]{:S(2)}) async-start(f32[16,56,128]{2,1,0:T(8,128)} %update_first.1), calls=%async_computation.2 | async-start | bytes 917504 | tf_op jit(solution)/shard_map/all_to_all | solution.py:487
  75.9 6.8 %prepare_next.1 = (f32[48,8,2304]{2,1,0:T(8,128)}, f32[48,8,2304]{2,1,0:T(8,128)}) custom-call(f32[48,8,2304]{2,1,0:T(8,128)} %get-tuple-element.37.source, f32[8,128]{1,0:T(8,128)S(1)} %get-tuple-element.38.refs_0_, bf16[3,2,512,128]{3,2,1,0:T(8,128)(2,1)S(1)} %copy-done.3), custom_call_target="tpu_custom_call" | custom-call | flops 2000000000 | bytes 11000000 | tf_op jit(solution)/shard_map/prepare_next/pallas_call | solution.py:326
  82.8 1.8 %collective-permute-done.11.other_ref = f32[16,56,128]{2,1,0:T(8,128)S(1)} collective-permute-done((f32[16,56,128]{2,1,0:T(8,128)S(1)}, f32[16,56,128]{2,1,0:T(8,128)S(1)}, u32[]{:S(2)}, u32[]{:S(2)}) %collective-permute-start.11) | collective-permute-done | bytes 458784 | tf_op jit(solution)/shard_map/ppermute | solution.py:481
  84.6 12.6 %filter_last.1 = (f32[8,48,2304]{2,1,0:T(8,128)}, f32[8,128]{1,0:T(8,128)}, f32[16,56,128]{2,1,0:T(8,128)S(1)}, f32[16,56,128]{2,1,0:T(8,128)S(1)}) custom-call(f32[48,8,2304]{2,1,0:T(8,128)} %get-tuple-element.40.field_hbm, f32[48,8,2304]{2,1,0:T(8,128)} %get-tuple-element.41.plain_hbm, f32[16,56,128]{2,1,0:T(8,128)S(1)} %all-to-all-done.2.mine_ref, ...), custom_call_target="tpu_custom_call" | custom-call | flops 8000000000 | bytes 14000000 | tf_op jit(solution)/shard_map/filter_last/pallas_call | solution.py:340
  97.5 1.7 %collective-permute-done.12 = f32[16,56,128]{2,1,0:T(8,128)S(1)} collective-permute-done((f32[16,56,128]{2,1,0:T(8,128)S(1)}, f32[16,56,128]{2,1,0:T(8,128)S(1)}, u32[]{:S(2)}, u32[]{:S(2)}) %collective-permute-start.12) | collective-permute-done | bytes 458784 | tf_op jit(solution)/shard_map/ppermute | solution.py:481
  99.2 15.2 %all_to_all.20 = f32[16,56,128]{2,1,0:T(8,128)S(1)} all-to-all(f32[16,56,128]{2,1,0:T(8,128)S(1)} %add.7), channel_id=1, replica_groups={{0,2,4,6,8,10,12,14,16,18,20,22,24,26,28,30},{1,3,5,7,9,11,13,15,17,19,..., dimensions={0} | all-to-all | bytes 917504 | tf_op jit(solution)/shard_map/all_to_all | solution.py:487
  115.1 4.1 %collective-permute-start.14 = (f32[56,128]{1,0:T(8,128)S(1)}, f32[56,128]{1,0:T(8,128)S(1)}, u32[]{:S(2)}, u32[]{:S(2)}) collective-permute-start(f32[56,128]{1,0:T(8,128)S(1)} %reduce_sum.19.d0), channel_id=1, source_target_pairs={{0,64},{32,96},{64,0},{96,32},{1,65},{33,97},{65,1},{97,33},{2,66}... | collective-permute-start | bytes 86024 | tf_op jit(solution)/shard_map/ppermute | solution.py:476
  119.6 1.8 %collective-permute-done.14.d2 = f32[56,128]{1,0:T(8,128)S(1)} collective-permute-done((f32[56,128]{1,0:T(8,128)S(1)}, f32[56,128]{1,0:T(8,128)S(1)}, u32[]{:S(2)}, u32[]{:S(2)}) %collective-permute-start.14) | collective-permute-done | bytes 28704 | tf_op jit(solution)/shard_map/ppermute | solution.py:476
  121.4 1.7 %collective-permute-done.15.d3 = f32[56,128]{1,0:T(8,128)S(1)} collective-permute-done((f32[56,128]{1,0:T(8,128)S(1)}, f32[56,128]{1,0:T(8,128)S(1)}, u32[]{:S(2)}, u32[]{:S(2)}) %collective-permute-start.15) | collective-permute-done | bytes 28704 | tf_op jit(solution)/shard_map/ppermute | solution.py:476
  (40 shorter events, 12.3 us)
Async XLA Ops:
  0.6 6.0 %collective-permute-start.3 = (f32[6,1152]{1,0:T(8,128)}, f32[6,1152]{1,0:T(8,128)S(1)}, u32[]{:S(2)}, u32[]{:S(2)}) collective-permute-start(f32[6,1152]{1,0:T(8,128)} %p0_hbm.1), channel_id=1, source_target_pairs={{0,32},{32,64},{64,96},{96,0},{1,33},{33,65},{65,97},{97,1},{2,34}... | collective-permute-start | bytes 82952 | tf_op jit(solution)/shard_map/ppermute | solution.py:476
  2.4 5.7 %collective-permute-start.4 = (f32[6,1152]{1,0:T(8,128)}, f32[6,1152]{1,0:T(8,128)S(1)}, u32[]{:S(2)}, u32[]{:S(2)}) collective-permute-start(f32[6,1152]{1,0:T(8,128)} %p0_hbm.1), channel_id=1, source_target_pairs={{0,64},{32,96},{64,0},{96,32},{1,65},{33,97},{65,1},{97,33},{2,66}... | collective-permute-start | bytes 82952 | tf_op jit(solution)/shard_map/ppermute | solution.py:476
  5.3 4.2 %collective-permute-start.5 = (f32[6,1152]{1,0:T(8,128)}, f32[6,1152]{1,0:T(8,128)S(1)}, u32[]{:S(2)}, u32[]{:S(2)}) collective-permute-start(f32[6,1152]{1,0:T(8,128)} %p0_hbm.1), channel_id=1, source_target_pairs={{0,96},{32,0},{64,32},{96,64},{1,97},{33,1},{65,33},{97,65},{2,98}... | collective-permute-start | bytes 82952 | tf_op jit(solution)/shard_map/ppermute | solution.py:476
  11.1 17.6 %all-to-all-start = ((f32[16,56,128]{2,1,0:T(8,128)}), f32[16,56,128]{2,1,0:T(8,128)S(1)}, u32[]{:S(2)}, u32[]{:S(2)}) async-start(f32[16,56,128]{2,1,0:T(8,128)} %place.1), calls=%async_computation | async-start | bytes 917504 | tf_op jit(solution)/shard_map/all_to_all | solution.py:487
  20.2 10.4 %copy-start.3 = (bf16[3,2,512,128]{3,2,1,0:T(8,128)(2,1)S(1)}, bf16[3,2,512,128]{3,2,1,0:T(8,128)(2,1)}, u32[]{:S(2)}) copy-start(bf16[3,2,512,128]{3,2,1,0:T(8,128)(2,1)} %constant.4.clone.refs_0_.mats_ref.refs_1_) | copy-start | bytes 2359300
  28.8 1.8 %collective-permute-start.6 = (f32[16,56,128]{2,1,0:T(8,128)S(1)}, f32[16,56,128]{2,1,0:T(8,128)S(1)}, u32[]{:S(2)}, u32[]{:S(2)}) collective-permute-start(f32[16,56,128]{2,1,0:T(8,128)S(1)} %all-to-all-done.mine_ref), channel_id=1, source_target_pairs={{0,1},{1,0},{2,3},{3,2},{4,5},{5,4},{6,7},{7,6},{8,9},{9,8},{10,11... | collective-permute-start | bytes 1376264 | tf_op jit(solution)/shard_map/ppermute | solution.py:481
  30.6 21.0 %copy-start.4 = (f32[6,1152]{1,0:T(8,128)S(1)}, f32[6,1152]{1,0:T(8,128)}, u32[]{:S(2)}) copy-start(f32[6,1152]{1,0:T(8,128)} %param.9) | copy-start | bytes 82948
  30.6 21.0 %copy-start.5 = (f32[6,1152]{1,0:T(8,128)S(1)}, f32[6,1152]{1,0:T(8,128)}, u32[]{:S(2)}) copy-start(f32[6,1152]{1,0:T(8,128)} %param.10) | copy-start | bytes 82948
  30.6 32.3 %copy-start = (s32[8,3]{0,1:T(4,128)S(1)}, s32[8,3]{0,1:T(4,128)}, u32[]{:S(2)}) copy-start(s32[8,3]{0,1:T(4,128)} %param.11) | copy-start | bytes 292
  30.6 36.1 %copy-start.1 = (s32[8]{0:T(128)S(1)}, s32[8]{0:T(128)}, u32[]{:S(2)}) copy-start(s32[8]{0:T(128)} %signs_ref.3) | copy-start | bytes 100
  42.3 1.9 %collective-permute-start.7 = (f32[16,56,128]{2,1,0:T(8,128)S(1)}, f32[16,56,128]{2,1,0:T(8,128)S(1)}, u32[]{:S(2)}, u32[]{:S(2)}) collective-permute-start(f32[16,56,128]{2,1,0:T(8,128)S(1)} %get-tuple-element.34), channel_id=1, source_target_pairs={{0,1},{1,0},{2,3},{3,2},{4,5},{5,4},{6,7},{7,6},{8,9},{9,8},{10,11... | collective-permute-start | bytes 1376264 | tf_op jit(solution)/shard_map/ppermute | solution.py:481
  45.0 13.6 %all-to-all-start.1 = ((f32[16,56,128]{2,1,0:T(8,128)}), f32[16,56,128]{2,1,0:T(8,128)S(1)}, u32[]{:S(2)}, u32[]{:S(2)}) async-start(f32[16,56,128]{2,1,0:T(8,128)} %add.6), calls=%async_computation.1 | async-start | bytes 917504 | tf_op jit(solution)/shard_map/all_to_all | solution.py:487
  51.7 9.6 %collective-permute-start = (f32[2,6,1152]{2,1,0:T(8,128)S(1)}, f32[2,6,1152]{2,1,0:T(8,128)S(1)}, u32[]{:S(2)}, u32[]{:S(2)}) collective-permute-start(f32[2,6,1152]{2,1,0:T(8,128)S(1)} %pad_maximum_fusion.refs_0_), channel_id=1, source_target_pairs={{0,32},{32,64},{64,96},{96,0},{1,33},{33,65},{65,97},{97,1},{2,34}... | collective-permute-start | bytes 165896 | tf_op jit(solution)/shard_map/ppermute | solution.py:476
  51.9 10.9 %collective-permute-start.1 = (f32[2,6,1152]{2,1,0:T(8,128)S(1)}, f32[2,6,1152]{2,1,0:T(8,128)S(1)}, u32[]{:S(2)}, u32[]{:S(2)}) collective-permute-start(f32[2,6,1152]{2,1,0:T(8,128)S(1)} %pad_maximum_fusion.refs_0_), channel_id=1, source_target_pairs={{0,64},{32,96},{64,0},{96,32},{1,65},{33,97},{65,1},{97,33},{2,66}... | collective-permute-start | bytes 165896 | tf_op jit(solution)/shard_map/ppermute | solution.py:476
  55.7 7.1 %collective-permute-start.2 = (f32[2,6,1152]{2,1,0:T(8,128)S(1)}, f32[2,6,1152]{2,1,0:T(8,128)S(1)}, u32[]{:S(2)}, u32[]{:S(2)}) collective-permute-start(f32[2,6,1152]{2,1,0:T(8,128)S(1)} %pad_maximum_fusion.refs_0_), channel_id=1, source_target_pairs={{0,96},{32,0},{64,32},{96,64},{1,97},{33,1},{65,33},{97,65},{2,98}... | collective-permute-start | bytes 165896 | tf_op jit(solution)/shard_map/ppermute | solution.py:476
  58.7 5.0 %collective-permute-start.10 = (f32[56,128]{1,0:T(8,128)S(1)}, f32[56,128]{1,0:T(8,128)S(1)}, u32[]{:S(2)}, u32[]{:S(2)}) collective-permute-start(f32[56,128]{1,0:T(8,128)S(1)} %reduce_sum.18.d0), channel_id=1, source_target_pairs={{0,96},{32,0},{64,32},{96,64},{1,97},{33,1},{65,33},{97,65},{2,98}... | collective-permute-start | bytes 86024 | tf_op jit(solution)/shard_map/ppermute | solution.py:476
  61.3 5.1 %collective-permute-start.8 = (f32[56,128]{1,0:T(8,128)S(1)}, f32[56,128]{1,0:T(8,128)S(1)}, u32[]{:S(2)}, u32[]{:S(2)}) collective-permute-start(f32[56,128]{1,0:T(8,128)S(1)} %reduce_sum.18.d0), channel_id=1, source_target_pairs={{0,32},{32,64},{64,96},{96,0},{1,33},{33,65},{65,97},{97,1},{2,34}... | collective-permute-start | bytes 86024 | tf_op jit(solution)/shard_map/ppermute | solution.py:476
  61.3 5.4 %collective-permute-start.9 = (f32[56,128]{1,0:T(8,128)S(1)}, f32[56,128]{1,0:T(8,128)S(1)}, u32[]{:S(2)}, u32[]{:S(2)}) collective-permute-start(f32[56,128]{1,0:T(8,128)S(1)} %reduce_sum.18.d0), channel_id=1, source_target_pairs={{0,64},{32,96},{64,0},{96,32},{1,65},{33,97},{65,1},{97,33},{2,66}... | collective-permute-start | bytes 86024 | tf_op jit(solution)/shard_map/ppermute | solution.py:476
  68.3 14.4 %all-to-all-start.2 = ((f32[16,56,128]{2,1,0:T(8,128)}), f32[16,56,128]{2,1,0:T(8,128)S(1)}, u32[]{:S(2)}, u32[]{:S(2)}) async-start(f32[16,56,128]{2,1,0:T(8,128)} %update_first.1), calls=%async_computation.2 | async-start | bytes 917504 | tf_op jit(solution)/shard_map/all_to_all | solution.py:487
  82.7 1.9 %collective-permute-start.11 = (f32[16,56,128]{2,1,0:T(8,128)S(1)}, f32[16,56,128]{2,1,0:T(8,128)S(1)}, u32[]{:S(2)}, u32[]{:S(2)}) collective-permute-start(f32[16,56,128]{2,1,0:T(8,128)S(1)} %all-to-all-done.2.mine_ref), channel_id=1, source_target_pairs={{0,1},{1,0},{2,3},{3,2},{4,5},{5,4},{6,7},{7,6},{8,9},{9,8},{10,11... | collective-permute-start | bytes 1376264 | tf_op jit(solution)/shard_map/ppermute | solution.py:481
  97.3 1.9 %collective-permute-start.12 = (f32[16,56,128]{2,1,0:T(8,128)S(1)}, f32[16,56,128]{2,1,0:T(8,128)S(1)}, u32[]{:S(2)}, u32[]{:S(2)}) collective-permute-start(f32[16,56,128]{2,1,0:T(8,128)S(1)} %get-tuple-element.47), channel_id=1, source_target_pairs={{0,1},{1,0},{2,3},{3,2},{4,5},{5,4},{6,7},{7,6},{8,9},{9,8},{10,11... | collective-permute-start | bytes 1376264 | tf_op jit(solution)/shard_map/ppermute | solution.py:481
  114.5 5.2 %collective-permute-start.13 = (f32[56,128]{1,0:T(8,128)S(1)}, f32[56,128]{1,0:T(8,128)S(1)}, u32[]{:S(2)}, u32[]{:S(2)}) collective-permute-start(f32[56,128]{1,0:T(8,128)S(1)} %reduce_sum.19.d0), channel_id=1, source_target_pairs={{0,32},{32,64},{64,96},{96,0},{1,33},{33,65},{65,97},{97,1},{2,34}... | collective-permute-start | bytes 86024 | tf_op jit(solution)/shard_map/ppermute | solution.py:476
  115.1 6.3 %collective-permute-start.14 = (f32[56,128]{1,0:T(8,128)S(1)}, f32[56,128]{1,0:T(8,128)S(1)}, u32[]{:S(2)}, u32[]{:S(2)}) collective-permute-start(f32[56,128]{1,0:T(8,128)S(1)} %reduce_sum.19.d0), channel_id=1, source_target_pairs={{0,64},{32,96},{64,0},{96,32},{1,65},{33,97},{65,1},{97,33},{2,66}... | collective-permute-start | bytes 86024 | tf_op jit(solution)/shard_map/ppermute | solution.py:476
  119.2 3.9 %collective-permute-start.15 = (f32[56,128]{1,0:T(8,128)S(1)}, f32[56,128]{1,0:T(8,128)S(1)}, u32[]{:S(2)}, u32[]{:S(2)}) collective-permute-start(f32[56,128]{1,0:T(8,128)S(1)} %reduce_sum.19.d0), channel_id=1, source_target_pairs={{0,96},{32,0},{64,32},{96,64},{1,97},{33,1},{65,33},{97,65},{2,98}... | collective-permute-start | bytes 86024 | tf_op jit(solution)/shard_map/ppermute | solution.py:476
  (1 other events, 1.1 us)

commit v5 on v4

--- a/solution.py
+++ b/solution.py
@@ -229,7 +229,7 @@
     upper = lax.broadcasted_iota(jnp.int32, (LOCAL, 128), 0) >= LOCAL // 2
 
     def build(row, carry):
-        slot = SLOTS - 1 - row if final else row
+        slot = SLOTS - 1 - row
         for ref, half in ((mine_ref, core), (other_ref, 1 - core)):
             for b in range(FB):
                 tiles = []
@@ -276,7 +276,7 @@
     scale_ref[...] = jnp.broadcast_to(inverse, (LOCAL, 128))
 
     def finish(b, row, scale):
-        slot = row if final else SLOTS - 1 - row
+        slot = SLOTS - 1 - row
         for ref, half in ((dmine_ref, core), (dother_ref, 1 - core)):
             lane = cols(half * CELLS, CELLS)
             value = ya[2 + 16 * b + row, :, lane] * scale
@@ -481,9 +481,8 @@
     return lax.ppermute(value, "orb", [(i, i ^ 1) for i in range(2 * SLOTS)])
 
 
-def plane_exchange(value, backward=False):
-    order = range(SLOTS - 1, -1, -1) if backward else range(SLOTS)
-    groups = [[2 * i + c for i in order] for c in range(2)]
+def plane_exchange(value):
+    groups = [[2 * i + c for i in range(SLOTS - 1, -1, -1)] for c in range(2)]
     return lax.all_to_all(value, "orb", 0, 0, axis_index_groups=groups, tiled=True)
 
 
@@ -501,11 +500,11 @@
     raw, scale, mine, other = filter_call(False, field, plain, near, core_swap(near), mats)
     cores, ions, own_core, own_ion = select_call(blocks, statics)
 
-    density = plane_exchange(mine + core_swap(other), backward=True)
+    density = plane_exchange(mine + core_swap(other))
     densities = frag_all(jnp.sum(density, axis=0))
     spread = update_call(False, blocks, frag_signs, cores, ions, densities)
     spread, raw = lax.optimization_barrier((spread, raw))
-    near = plane_exchange(spread, backward=True)
+    near = plane_exchange(spread)
     field, plain = prepare_call(False, (raw, scale), mats)
     near, field = lax.optimization_barrier((near, field))
     filtered, _, mine, other = filter_call(True, field, plain, near, core_swap(near), mats)

time: 125 us -> 123 us (0.984)
  waiting for transfers between devices: 22.6 us -> 19.4 us
  starting transfers between devices: 41.8 us -> 44.3 us
    all_to_all x3, waiting for transfers between devices: 5.92 us -> 2.77 us  [plane_exchange(): lax.all_to_all(value, 'orb', 0, 0, axis_index_groups=groups, tiled=True)]
    all_to_all x3, starting transfers between devices: 22.2 us -> 24.5 us  [plane_exchange(): lax.all_to_all(value, 'orb', 0, 0, axis_index_groups=groups, tiled=True)]
  transfers between devices with their start and end apart: 19 -> 19, of which waited for: 13 -> 12; matrix products, arithmetic and copies ran while one was open for 0% -> 0% of each run, Pallas kernels for 11% -> 11%
where the time goes in v5:
time: 123 us
  starting transfers between devices  44.3 us (36%)
  Pallas kernels  42 us (34%)
  waiting for transfers between devices  19.4 us (16%)
  blocking collectives  14 us (11%)
    all_to_all x3, starting transfers between devices, plane_exchange(): lax.all_to_all(value, 'orb', 0, 0, axis_index_groups=groups, tiled=True)  24.5 us
    pallas_call x2, Pallas kernels, filter_call(): pl.pallas_call(functools.partial(filter_kernel, final), out_shape=(pltpu....  24.3 us
    ppermute x12, starting transfers between devices, frag_all(): lax.ppermute(value, 'frag', [(g, (g + s) % N_FRAG) for g in range(N_FRAG)])  19.1 us
    all_to_all x1, blocking collectives, plane_exchange(): lax.all_to_all(value, 'orb', 0, 0, axis_index_groups=groups, tiled=True)  14 us
    pallas_call x2, Pallas kernels, prepare_call(): pl.pallas_call(functools.partial(prepare_kernel, first), out_shape=(RAW_H...  12.3 us
    ppermute x12, waiting for transfers between devices, frag_all(): lax.ppermute(value, 'frag', [(g, (g + s) % N_FRAG) for g in range(N_FRAG)])  9.67 us
    ppermute x4, waiting for transfers between devices, core_swap(): return lax.ppermute(value, 'orb', [(i, i ^ 1) for i in range(2 * SLOTS)])  6.97 us
    pallas_call x2, Pallas kernels, update_call(): pl.pallas_call(functools.partial(update_kernel, final), out_shape=jax.Sha...  3.04 us
  transfers between devices with their start and end apart: 19, of which 12 were waited for; matrix products, arithmetic and copies ran while one was open for 0% of the time, Pallas kernels for 11%

profile of v5, /device:TPU:0, one launch (start us, length us, event | category | flops | bytes accessed | tf_op | source)
XLA Modules:
  0.0 122.6 jit_solution(16287789953423716105)
XLA Ops:
  0.6 1.8 %collective-permute-start.3 = (f32[6,1152]{1,0:T(8,128)}, f32[6,1152]{1,0:T(8,128)S(1)}, u32[]{:S(2)}, u32[]{:S(2)}) collective-permute-start(f32[6,1152]{1,0:T(8,128)} %p0_hbm.1), channel_id=1, source_target_pairs={{0,32},{32,64},{64,96},{96,0},{1,33},{33,65},{65,97},{97,1},{2,34}... | collective-permute-start | bytes 82952 | tf_op jit(solution)/shard_map/ppermute | solution.py:476
  2.4 2.9 %collective-permute-start.4 = (f32[6,1152]{1,0:T(8,128)}, f32[6,1152]{1,0:T(8,128)S(1)}, u32[]{:S(2)}, u32[]{:S(2)}) collective-permute-start(f32[6,1152]{1,0:T(8,128)} %p0_hbm.1), channel_id=1, source_target_pairs={{0,64},{32,96},{64,0},{96,32},{1,65},{33,97},{65,1},{97,33},{2,66}... | collective-permute-start | bytes 82952 | tf_op jit(solution)/shard_map/ppermute | solution.py:476
  9.5 1.7 %place.1 = f32[16,56,128]{2,1,0:T(8,128)} custom-call(s32[3,8]{1,0:T(4,128)} %bitcast.5, f32[6,1152]{1,0:T(8,128)} %p0_hbm.1, f32[6,1152]{1,0:T(8,128)S(1)} %collective-permute-done.3.p1, f32[6,1152]{1,0:T(8,128)S(1)} %collective-permute-done.4.p2, f32[6,1152]{1,0:T(8,128)S(1)} %collective-permute-done.5.p3), custom_call_target="tpu_custom_call" | custom-call | tf_op jit(solution)/shard_map/place/pallas_call | solution.py:419
  11.1 9.7 %all-to-all-start = ((f32[16,56,128]{2,1,0:T(8,128)}), f32[16,56,128]{2,1,0:T(8,128)S(1)}, u32[]{:S(2)}, u32[]{:S(2)}) async-start(f32[16,56,128]{2,1,0:T(8,128)} %place.1), calls=%async_computation | async-start | bytes 917504 | tf_op jit(solution)/shard_map/all_to_all | solution.py:486
  21.9 5.4 %prepare_first.1 = (f32[48,8,2304]{2,1,0:T(8,128)}, f32[48,8,2304]{2,1,0:T(8,128)}) custom-call(f32[8,48,2304]{2,1,0:T(8,128)} %bitcast.11, bf16[3,2,512,128]{3,2,1,0:T(8,128)(2,1)S(1)} %copy-done.2), custom_call_target="tpu_custom_call" | custom-call | flops 2000000000 | bytes 11000000 | tf_op jit(solution)/shard_map/prepare_first/pallas_call | solution.py:326
  27.5 1.8 %collective-permute-done.6.other_ref = f32[16,56,128]{2,1,0:T(8,128)S(1)} collective-permute-done((f32[16,56,128]{2,1,0:T(8,128)S(1)}, f32[16,56,128]{2,1,0:T(8,128)S(1)}, u32[]{:S(2)}, u32[]{:S(2)}) %collective-permute-start.6) | collective-permute-done | bytes 458784 | tf_op jit(solution)/shard_map/ppermute | solution.py:481
  29.3 11.7 %filter_first.1 = (f32[48,8,2304]{2,1,0:T(8,128)}, f32[8,128]{1,0:T(8,128)S(1)}, f32[16,56,128]{2,1,0:T(8,128)S(1)}, f32[16,56,128]{2,1,0:T(8,128)S(1)}) custom-call(f32[48,8,2304]{2,1,0:T(8,128)} %get-tuple-element.30.field_hbm, f32[48,8,2304]{2,1,0:T(8,128)} %get-tuple-element.31.plain_hbm, f32[16,56,128]{2,1,0:T(8,128)S(1)} %all-to-all-done.mine_ref, ...), custom_call_target="tpu_custom_call" | custom-call | flops 8000000000 | bytes 14000000 | tf_op jit(solution)/shard_map/filter_first/pallas_call | solution.py:340
  41.2 1.7 %collective-permute-done.7 = f32[16,56,128]{2,1,0:T(8,128)S(1)} collective-permute-done((f32[16,56,128]{2,1,0:T(8,128)S(1)}, f32[16,56,128]{2,1,0:T(8,128)S(1)}, u32[]{:S(2)}, u32[]{:S(2)}) %collective-permute-start.7) | collective-permute-done | bytes 458784 | tf_op jit(solution)/shard_map/ppermute | solution.py:481
  43.7 7.2 %all-to-all-start.1 = ((f32[16,56,128]{2,1,0:T(8,128)}), f32[16,56,128]{2,1,0:T(8,128)S(1)}, u32[]{:S(2)}, u32[]{:S(2)}) async-start(f32[16,56,128]{2,1,0:T(8,128)} %add.6), calls=%async_computation.1 | async-start | bytes 917504 | tf_op jit(solution)/shard_map/all_to_all | solution.py:486
  51.2 3.8 %collective-permute-start.1 = (f32[2,6,1152]{2,1,0:T(8,128)S(1)}, f32[2,6,1152]{2,1,0:T(8,128)S(1)}, u32[]{:S(2)}, u32[]{:S(2)}) collective-permute-start(f32[2,6,1152]{2,1,0:T(8,128)S(1)} %pad_maximum_fusion.refs_0_), channel_id=1, source_target_pairs={{0,64},{32,96},{64,0},{96,32},{1,65},{33,97},{65,1},{97,33},{2,66}... | collective-permute-start | bytes 165896 | tf_op jit(solution)/shard_map/ppermute | solution.py:476
  55.1 2.8 %all-to-all-done.1 = f32[16,56,128]{2,1,0:T(8,128)S(1)} async-done(((f32[16,56,128]{2,1,0:T(8,128)}), f32[16,56,128]{2,1,0:T(8,128)S(1)}, u32[]{:S(2)}, u32[]{:S(2)}) %all-to-all-start.1) | async-done | bytes 458784 | tf_op jit(solution)/shard_map/all_to_all | solution.py:486
  57.9 2.6 %collective-permute-start.10 = (f32[56,128]{1,0:T(8,128)S(1)}, f32[56,128]{1,0:T(8,128)S(1)}, u32[]{:S(2)}, u32[]{:S(2)}) collective-permute-start(f32[56,128]{1,0:T(8,128)S(1)} %reduce_sum.18.d0), channel_id=1, source_target_pairs={{0,96},{32,0},{64,32},{96,64},{1,97},{33,1},{65,33},{97,65},{2,98}... | collective-permute-start | bytes 86024 | tf_op jit(solution)/shard_map/ppermute | solution.py:476
  60.6 1.5 %collective-permute-start.9 = (f32[56,128]{1,0:T(8,128)S(1)}, f32[56,128]{1,0:T(8,128)S(1)}, u32[]{:S(2)}, u32[]{:S(2)}) collective-permute-start(f32[56,128]{1,0:T(8,128)S(1)} %reduce_sum.18.d0), channel_id=1, source_target_pairs={{0,64},{32,96},{64,0},{96,32},{1,65},{33,97},{65,1},{97,33},{2,66}... | collective-permute-start | bytes 86024 | tf_op jit(solution)/shard_map/ppermute | solution.py:476
  63.0 2.7 %collective-permute-done.8.d1 = f32[56,128]{1,0:T(8,128)S(1)} collective-permute-done((f32[56,128]{1,0:T(8,128)S(1)}, f32[56,128]{1,0:T(8,128)S(1)}, u32[]{:S(2)}, u32[]{:S(2)}) %collective-permute-start.8) | collective-permute-done | bytes 28704 | tf_op jit(solution)/shard_map/ppermute | solution.py:476
  66.0 1.6 %update_first.1 = f32[16,56,128]{2,1,0:T(8,128)} custom-call(s32[3,8]{1,0:T(4,128)S(1)} %bitcast.7, s32[8]{0:T(128)S(1)} %copy-done.1, f32[54,128]{1,0:T(8,128)S(1)} %get-tuple-element.25.core_ref, f32[54,128]{1,0:T(8,128)S(1)} %get-tuple-element.26.ion_ref, f32[56,128]{1,0:T(8,128)S(1)} %reduce_sum.18.d0, f32[56,128]{1,0:T(8,128)S(1)} %collective-permute-done.8.d1, ...), custom_call_target="tpu_custom_call" | custom-call | tf_op jit(solution)/shard_map/update_first/pallas_call | solution.py:464
  67.6 7.6 %all-to-all-start.2 = ((f32[16,56,128]{2,1,0:T(8,128)}), f32[16,56,128]{2,1,0:T(8,128)S(1)}, u32[]{:S(2)}, u32[]{:S(2)}) async-start(f32[16,56,128]{2,1,0:T(8,128)} %update_first.1), calls=%async_computation.2 | async-start | bytes 917504 | tf_op jit(solution)/shard_map/all_to_all | solution.py:486
  75.2 6.8 %prepare_next.1 = (f32[48,8,2304]{2,1,0:T(8,128)}, f32[48,8,2304]{2,1,0:T(8,128)}) custom-call(f32[48,8,2304]{2,1,0:T(8,128)} %get-tuple-element.37.source, f32[8,128]{1,0:T(8,128)S(1)} %get-tuple-element.38.refs_0_, bf16[3,2,512,128]{3,2,1,0:T(8,128)(2,1)S(1)} %copy-done.3), custom_call_target="tpu_custom_call" | custom-call | flops 2000000000 | bytes 11000000 | tf_op jit(solution)/shard_map/prepare_next/pallas_call | solution.py:326
  82.1 1.8 %collective-permute-done.11.other_ref = f32[16,56,128]{2,1,0:T(8,128)S(1)} collective-permute-done((f32[16,56,128]{2,1,0:T(8,128)S(1)}, f32[16,56,128]{2,1,0:T(8,128)S(1)}, u32[]{:S(2)}, u32[]{:S(2)}) %collective-permute-start.11) | collective-permute-done | bytes 458784 | tf_op jit(solution)/shard_map/ppermute | solution.py:481
  83.9 12.6 %filter_last.1 = (f32[8,48,2304]{2,1,0:T(8,128)}, f32[8,128]{1,0:T(8,128)}, f32[16,56,128]{2,1,0:T(8,128)S(1)}, f32[16,56,128]{2,1,0:T(8,128)S(1)}) custom-call(f32[48,8,2304]{2,1,0:T(8,128)} %get-tuple-element.40.field_hbm, f32[48,8,2304]{2,1,0:T(8,128)} %get-tuple-element.41.plain_hbm, f32[16,56,128]{2,1,0:T(8,128)S(1)} %all-to-all-done.2.mine_ref, ...), custom_call_target="tpu_custom_call" | custom-call | flops 8000000000 | bytes 14000000 | tf_op jit(solution)/shard_map/filter_last/pallas_call | solution.py:340
  96.7 1.7 %collective-permute-done.12 = f32[16,56,128]{2,1,0:T(8,128)S(1)} collective-permute-done((f32[16,56,128]{2,1,0:T(8,128)S(1)}, f32[16,56,128]{2,1,0:T(8,128)S(1)}, u32[]{:S(2)}, u32[]{:S(2)}) %collective-permute-start.12) | collective-permute-done | bytes 458784 | tf_op jit(solution)/shard_map/ppermute | solution.py:481
  98.5 14.0 %all_to_all.20 = f32[16,56,128]{2,1,0:T(8,128)S(1)} all-to-all(f32[16,56,128]{2,1,0:T(8,128)S(1)} %add.7), channel_id=1, replica_groups={{30,28,26,24,22,20,18,16,14,12,10,8,6,4,2,0},{31,29,27,25,23,21,19,17,1..., dimensions={0} | all-to-all | bytes 917504 | tf_op jit(solution)/shard_map/all_to_all | solution.py:486
  113.1 4.1 %collective-permute-start.14 = (f32[56,128]{1,0:T(8,128)S(1)}, f32[56,128]{1,0:T(8,128)S(1)}, u32[]{:S(2)}, u32[]{:S(2)}) collective-permute-start(f32[56,128]{1,0:T(8,128)S(1)} %reduce_sum.19.d0), channel_id=1, source_target_pairs={{0,64},{32,96},{64,0},{96,32},{1,65},{33,97},{65,1},{97,33},{2,66}... | collective-permute-start | bytes 86024 | tf_op jit(solution)/shard_map/ppermute | solution.py:476
  117.7 1.7 %collective-permute-done.14.d2 = f32[56,128]{1,0:T(8,128)S(1)} collective-permute-done((f32[56,128]{1,0:T(8,128)S(1)}, f32[56,128]{1,0:T(8,128)S(1)}, u32[]{:S(2)}, u32[]{:S(2)}) %collective-permute-start.14) | collective-permute-done | bytes 28704 | tf_op jit(solution)/shard_map/ppermute | solution.py:476
  119.4 1.7 %collective-permute-done.15.d3 = f32[56,128]{1,0:T(8,128)S(1)} collective-permute-done((f32[56,128]{1,0:T(8,128)S(1)}, f32[56,128]{1,0:T(8,128)S(1)}, u32[]{:S(2)}, u32[]{:S(2)}) %collective-permute-start.15) | collective-permute-done | bytes 28704 | tf_op jit(solution)/shard_map/ppermute | solution.py:476
  (40 shorter events, 10.9 us)
Async XLA Ops:
  0.6 6.0 %collective-permute-start.3 = (f32[6,1152]{1,0:T(8,128)}, f32[6,1152]{1,0:T(8,128)S(1)}, u32[]{:S(2)}, u32[]{:S(2)}) collective-permute-start(f32[6,1152]{1,0:T(8,128)} %p0_hbm.1), channel_id=1, source_target_pairs={{0,32},{32,64},{64,96},{96,0},{1,33},{33,65},{65,97},{97,1},{2,34}... | collective-permute-start | bytes 82952 | tf_op jit(solution)/shard_map/ppermute | solution.py:476
  2.4 5.7 %collective-permute-start.4 = (f32[6,1152]{1,0:T(8,128)}, f32[6,1152]{1,0:T(8,128)S(1)}, u32[]{:S(2)}, u32[]{:S(2)}) collective-permute-start(f32[6,1152]{1,0:T(8,128)} %p0_hbm.1), channel_id=1, source_target_pairs={{0,64},{32,96},{64,0},{96,32},{1,65},{33,97},{65,1},{97,33},{2,66}... | collective-permute-start | bytes 82952 | tf_op jit(solution)/shard_map/ppermute | solution.py:476
  5.3 4.2 %collective-permute-start.5 = (f32[6,1152]{1,0:T(8,128)}, f32[6,1152]{1,0:T(8,128)S(1)}, u32[]{:S(2)}, u32[]{:S(2)}) collective-permute-start(f32[6,1152]{1,0:T(8,128)} %p0_hbm.1), channel_id=1, source_target_pairs={{0,96},{32,0},{64,32},{96,64},{1,97},{33,1},{65,33},{97,65},{2,98}... | collective-permute-start | bytes 82952 | tf_op jit(solution)/shard_map/ppermute | solution.py:476
  11.1 16.3 %all-to-all-start = ((f32[16,56,128]{2,1,0:T(8,128)}), f32[16,56,128]{2,1,0:T(8,128)S(1)}, u32[]{:S(2)}, u32[]{:S(2)}) async-start(f32[16,56,128]{2,1,0:T(8,128)} %place.1), calls=%async_computation | async-start | bytes 917504 | tf_op jit(solution)/shard_map/all_to_all | solution.py:486
  21.9 7.4 %copy-start.3 = (bf16[3,2,512,128]{3,2,1,0:T(8,128)(2,1)S(1)}, bf16[3,2,512,128]{3,2,1,0:T(8,128)(2,1)}, u32[]{:S(2)}) copy-start(bf16[3,2,512,128]{3,2,1,0:T(8,128)(2,1)} %constant.4.clone.refs_0_.mats_ref.refs_1_) | copy-start | bytes 2359300
  27.4 1.9 %collective-permute-start.6 = (f32[16,56,128]{2,1,0:T(8,128)S(1)}, f32[16,56,128]{2,1,0:T(8,128)S(1)}, u32[]{:S(2)}, u32[]{:S(2)}) collective-permute-start(f32[16,56,128]{2,1,0:T(8,128)S(1)} %all-to-all-done.mine_ref), channel_id=1, source_target_pairs={{0,1},{1,0},{2,3},{3,2},{4,5},{5,4},{6,7},{7,6},{8,9},{9,8},{10,11... | collective-permute-start | bytes 1376264 | tf_op jit(solution)/shard_map/ppermute | solution.py:481
  29.3 21.6 %copy-start.4 = (f32[6,1152]{1,0:T(8,128)S(1)}, f32[6,1152]{1,0:T(8,128)}, u32[]{:S(2)}) copy-start(f32[6,1152]{1,0:T(8,128)} %param.9) | copy-start | bytes 82948
  29.3 21.6 %copy-start.5 = (f32[6,1152]{1,0:T(8,128)S(1)}, f32[6,1152]{1,0:T(8,128)}, u32[]{:S(2)}) copy-start(f32[6,1152]{1,0:T(8,128)} %param.10) | copy-start | bytes 82948
  29.3 32.8 %copy-start = (s32[8,3]{0,1:T(4,128)S(1)}, s32[8,3]{0,1:T(4,128)}, u32[]{:S(2)}) copy-start(s32[8,3]{0,1:T(4,128)} %param.11) | copy-start | bytes 292
  29.3 36.6 %copy-start.1 = (s32[8]{0:T(128)S(1)}, s32[8]{0:T(128)}, u32[]{:S(2)}) copy-start(s32[8]{0:T(128)} %signs_ref.3) | copy-start | bytes 100
  41.0 1.9 %collective-permute-start.7 = (f32[16,56,128]{2,1,0:T(8,128)S(1)}, f32[16,56,128]{2,1,0:T(8,128)S(1)}, u32[]{:S(2)}, u32[]{:S(2)}) collective-permute-start(f32[16,56,128]{2,1,0:T(8,128)S(1)} %get-tuple-element.34), channel_id=1, source_target_pairs={{0,1},{1,0},{2,3},{3,2},{4,5},{5,4},{6,7},{7,6},{8,9},{9,8},{10,11... | collective-permute-start | bytes 1376264 | tf_op jit(solution)/shard_map/ppermute | solution.py:481
  43.7 14.2 %all-to-all-start.1 = ((f32[16,56,128]{2,1,0:T(8,128)}), f32[16,56,128]{2,1,0:T(8,128)S(1)}, u32[]{:S(2)}, u32[]{:S(2)}) async-start(f32[16,56,128]{2,1,0:T(8,128)} %add.6), calls=%async_computation.1 | async-start | bytes 917504 | tf_op jit(solution)/shard_map/all_to_all | solution.py:486
  50.9 9.6 %collective-permute-start = (f32[2,6,1152]{2,1,0:T(8,128)S(1)}, f32[2,6,1152]{2,1,0:T(8,128)S(1)}, u32[]{:S(2)}, u32[]{:S(2)}) collective-permute-start(f32[2,6,1152]{2,1,0:T(8,128)S(1)} %pad_maximum_fusion.refs_0_), channel_id=1, source_target_pairs={{0,32},{32,64},{64,96},{96,0},{1,33},{33,65},{65,97},{97,1},{2,34}... | collective-permute-start | bytes 165896 | tf_op jit(solution)/shard_map/ppermute | solution.py:476
  51.2 10.9 %collective-permute-start.1 = (f32[2,6,1152]{2,1,0:T(8,128)S(1)}, f32[2,6,1152]{2,1,0:T(8,128)S(1)}, u32[]{:S(2)}, u32[]{:S(2)}) collective-permute-start(f32[2,6,1152]{2,1,0:T(8,128)S(1)} %pad_maximum_fusion.refs_0_), channel_id=1, source_target_pairs={{0,64},{32,96},{64,0},{96,32},{1,65},{33,97},{65,1},{97,33},{2,66}... | collective-permute-start | bytes 165896 | tf_op jit(solution)/shard_map/ppermute | solution.py:476
  55.0 7.1 %collective-permute-start.2 = (f32[2,6,1152]{2,1,0:T(8,128)S(1)}, f32[2,6,1152]{2,1,0:T(8,128)S(1)}, u32[]{:S(2)}, u32[]{:S(2)}) collective-permute-start(f32[2,6,1152]{2,1,0:T(8,128)S(1)} %pad_maximum_fusion.refs_0_), channel_id=1, source_target_pairs={{0,96},{32,0},{64,32},{96,64},{1,97},{33,1},{65,33},{97,65},{2,98}... | collective-permute-start | bytes 165896 | tf_op jit(solution)/shard_map/ppermute | solution.py:476
  57.9 5.0 %collective-permute-start.10 = (f32[56,128]{1,0:T(8,128)S(1)}, f32[56,128]{1,0:T(8,128)S(1)}, u32[]{:S(2)}, u32[]{:S(2)}) collective-permute-start(f32[56,128]{1,0:T(8,128)S(1)} %reduce_sum.18.d0), channel_id=1, source_target_pairs={{0,96},{32,0},{64,32},{96,64},{1,97},{33,1},{65,33},{97,65},{2,98}... | collective-permute-start | bytes 86024 | tf_op jit(solution)/shard_map/ppermute | solution.py:476
  60.6 5.1 %collective-permute-start.8 = (f32[56,128]{1,0:T(8,128)S(1)}, f32[56,128]{1,0:T(8,128)S(1)}, u32[]{:S(2)}, u32[]{:S(2)}) collective-permute-start(f32[56,128]{1,0:T(8,128)S(1)} %reduce_sum.18.d0), channel_id=1, source_target_pairs={{0,32},{32,64},{64,96},{96,0},{1,33},{33,65},{65,97},{97,1},{2,34}... | collective-permute-start | bytes 86024 | tf_op jit(solution)/shard_map/ppermute | solution.py:476
  60.6 5.4 %collective-permute-start.9 = (f32[56,128]{1,0:T(8,128)S(1)}, f32[56,128]{1,0:T(8,128)S(1)}, u32[]{:S(2)}, u32[]{:S(2)}) collective-permute-start(f32[56,128]{1,0:T(8,128)S(1)} %reduce_sum.18.d0), channel_id=1, source_target_pairs={{0,64},{32,96},{64,0},{96,32},{1,65},{33,97},{65,1},{97,33},{2,66}... | collective-permute-start | bytes 86024 | tf_op jit(solution)/shard_map/ppermute | solution.py:476
  67.6 14.4 %all-to-all-start.2 = ((f32[16,56,128]{2,1,0:T(8,128)}), f32[16,56,128]{2,1,0:T(8,128)S(1)}, u32[]{:S(2)}, u32[]{:S(2)}) async-start(f32[16,56,128]{2,1,0:T(8,128)} %update_first.1), calls=%async_computation.2 | async-start | bytes 917504 | tf_op jit(solution)/shard_map/all_to_all | solution.py:486
  82.0 1.9 %collective-permute-start.11 = (f32[16,56,128]{2,1,0:T(8,128)S(1)}, f32[16,56,128]{2,1,0:T(8,128)S(1)}, u32[]{:S(2)}, u32[]{:S(2)}) collective-permute-start(f32[16,56,128]{2,1,0:T(8,128)S(1)} %all-to-all-done.2.mine_ref), channel_id=1, source_target_pairs={{0,1},{1,0},{2,3},{3,2},{4,5},{5,4},{6,7},{7,6},{8,9},{9,8},{10,11... | collective-permute-start | bytes 1376264 | tf_op jit(solution)/shard_map/ppermute | solution.py:481
  96.5 1.9 %collective-permute-start.12 = (f32[16,56,128]{2,1,0:T(8,128)S(1)}, f32[16,56,128]{2,1,0:T(8,128)S(1)}, u32[]{:S(2)}, u32[]{:S(2)}) collective-permute-start(f32[16,56,128]{2,1,0:T(8,128)S(1)} %get-tuple-element.47), channel_id=1, source_target_pairs={{0,1},{1,0},{2,3},{3,2},{4,5},{5,4},{6,7},{7,6},{8,9},{9,8},{10,11... | collective-permute-start | bytes 1376264 | tf_op jit(solution)/shard_map/ppermute | solution.py:481
  112.5 5.2 %collective-permute-start.13 = (f32[56,128]{1,0:T(8,128)S(1)}, f32[56,128]{1,0:T(8,128)S(1)}, u32[]{:S(2)}, u32[]{:S(2)}) collective-permute-start(f32[56,128]{1,0:T(8,128)S(1)} %reduce_sum.19.d0), channel_id=1, source_target_pairs={{0,32},{32,64},{64,96},{96,0},{1,33},{33,65},{65,97},{97,1},{2,34}... | collective-permute-start | bytes 86024 | tf_op jit(solution)/shard_map/ppermute | solution.py:476
  113.1 6.3 %collective-permute-start.14 = (f32[56,128]{1,0:T(8,128)S(1)}, f32[56,128]{1,0:T(8,128)S(1)}, u32[]{:S(2)}, u32[]{:S(2)}) collective-permute-start(f32[56,128]{1,0:T(8,128)S(1)} %reduce_sum.19.d0), channel_id=1, source_target_pairs={{0,64},{32,96},{64,0},{96,32},{1,65},{33,97},{65,1},{97,33},{2,66}... | collective-permute-start | bytes 86024 | tf_op jit(solution)/shard_map/ppermute | solution.py:476
  117.3 3.9 %collective-permute-start.15 = (f32[56,128]{1,0:T(8,128)S(1)}, f32[56,128]{1,0:T(8,128)S(1)}, u32[]{:S(2)}, u32[]{:S(2)}) collective-permute-start(f32[56,128]{1,0:T(8,128)S(1)} %reduce_sum.19.d0), channel_id=1, source_target_pairs={{0,96},{32,0},{64,32},{96,64},{1,97},{33,1},{65,33},{97,65},{2,98}... | collective-permute-start | bytes 86024 | tf_op jit(solution)/shard_map/ppermute | solution.py:476
  (1 other events, 1.1 us)
